TPU v7x, 32 devices: a whole 2x2x4 slice. The times are simulated.
32 devices in a mesh: sec: 4 (over y, x), tile: 8 (over z, core).
Axes of the slice: x: 2, y: 2, z: 4, core: 2. Of those that a mesh axis runs over, the one named last changes fastest.
Arguments:
- atm_state: float32 [4, 32, 262144], P(None, None, ('sec', 'tile')), may hold values from -6 to 6
- diffusivity: float32 [32, 262144], P(None, ('sec', 'tile')), may hold values from 0.05 to 32
- surface_prev: float32 [4, 262144], P(None, ('sec', 'tile')), may hold values from -6 to 6
- flux_mix: float32 [10, 12], replicated, may hold values from -1.75 to 1.75
- entry_dest: int32 [2048, 1], P(('sec', 'tile')), may hold values from 0 to 31; in each aligned block of 64 rows (0 to 63, 64 to 127, ...) at most 4 rows name the same one
- entry_tile: int32 [2048], P(('sec', 'tile')), may hold values from 0 to 63
- entry_row: int32 [2048], P(('sec', 'tile')), may hold values from 0 to 63
- regrid_blocks: bfloat16 [2048, 128, 128], P(('sec', 'tile')), may hold values from -0.5 to 0.5
- ocean_state: float32 [4, 8, 256, 1024], P(None, None, 'sec', 'tile'), may hold values from -6 to 6
- land_mask: int32 [256, 1024], P('sec', 'tile'), may hold values 0 or 1
- flux_response: float32 [4, 10], replicated, may hold values from -2 to 2
Outputs:
- atm_next: float32 [4, 32, 262144], P(None, None, ('sec', 'tile'))
- ocean_next: float32 [4, 8, 256, 1024], P(None, None, 'sec', 'tile')
- surface_next: float32 [4, 262144], P(None, ('sec', 'tile'))
Inputs may be any that keep to these rules, and one draw needn't show every extreme that they name: `entry_dest`: among the 64 entries of one device no destination is named more than 4 times, and in some device's entries one destination is named exactly 4 times; every device is named by some entry.
All inputs are finite; a program needn't handle non-finite values. No bound on the sum of `land_mask` on one device may be relied on, other than what follows from the above.
Results may differ from a plain program's by a relative error of at most 0.0003.
Values sent between devices are 32-bit elements; how exact they have to be, the bound alone decides.
No kernel may reach another device: no remote copies, remote signals or barrier semaphores. Data moves between devices by JAX's collectives and lax.ppermute only.
A program may use at most 128 MiB of HBM per device.

v0:
```python
import jax
import jax.numpy as jnp
from jax import lax
from jax.sharding import PartitionSpec as P

CAP = 4


PRECISE = lax.Precision.HIGHEST
DIFFUSE = 0.2
CORIOLIS = 0.3
OCEAN_DT = 0.2


def with_halo(cells, sides, width):
    for axis, dim in sides:
        count = lax.axis_size(axis)
        ends = count - 1
        head = lax.slice_in_dim(cells, 0, width, axis=dim)
        tail = lax.slice_in_dim(cells, cells.shape[dim] - width, cells.shape[dim], axis=dim)
        cells = jnp.concatenate(
            [
                lax.ppermute(tail, axis, [(i, (i + 1) % count) for i in range(ends)]),
                cells,
                lax.ppermute(head, axis, [((i + 1) % count, i) for i in range(ends)]),
            ],
            axis=dim,
        )
    return cells


def boundary_layer(atmos_state, coupling, surface_value):
    levels = atmos_state.shape[1]
    coupling_up = jnp.concatenate([coupling[1:], jnp.zeros_like(coupling[:1])], 0)
    diagonal = 1.0 + coupling + coupling_up
    c_list = []
    d_list = []
    c_prev = -coupling_up[0] / diagonal[0]
    d_prev = (atmos_state[:, 0] + coupling[0] * surface_value) / diagonal[0]
    c_list.append(c_prev)
    d_list.append(d_prev)
    for lev_index in range(1, levels):
        coupling_low = -coupling[lev_index]
        pivot_value = diagonal[lev_index] - coupling_low * c_prev
        c_prev = -coupling_up[lev_index] / pivot_value
        d_prev = (atmos_state[:, lev_index] - coupling_low * d_prev) / pivot_value
        c_list.append(c_prev)
        d_list.append(d_prev)
    solved = d_list[levels - 1]
    solved_levels = [solved]
    for lev_index in range(levels - 2, -1, -1):
        solved = d_list[lev_index] - c_list[lev_index] * solved
        solved_levels.append(solved)
    updated_state = jnp.stack(solved_levels[::-1], axis=1)
    turbulent = coupling[0] * (surface_value - updated_state[:, 0])
    features = jnp.concatenate([turbulent, updated_state[:, 0], turbulent * updated_state[:, 1]], 0)
    return (updated_state, features)


def ocean_update(padded, forcing, ocean_depth):
    mask_grid = padded[-1]
    fields = padded[:-1].reshape(4, ocean_depth, padded.shape[1], padded.shape[2])
    centre = fields[:, :, 1:-1, 1:-1]
    east_cells = fields[:, :, 2:, 1:-1]
    west_cells = fields[:, :, :-2, 1:-1]
    north_cells = fields[:, :, 1:-1, 2:]
    south_cells = fields[:, :, 1:-1, :-2]
    laplace = mask_grid[2:, 1:-1] * (east_cells - centre) + mask_grid[:-2, 1:-1] * (
        west_cells - centre
    )
    laplace = (
        laplace
        + mask_grid[1:-1, 2:] * (north_cells - centre)
        + mask_grid[1:-1, :-2] * (south_cells - centre)
    )
    zonal_flow = centre[2]
    merid_flow = centre[3]
    advect = 0.5 * (
        zonal_flow * (east_cells - west_cells) + merid_flow * (north_cells - south_cells)
    )
    nothing = jnp.zeros_like(zonal_flow)
    rotation = jnp.stack([nothing, nothing, CORIOLIS * merid_flow, -CORIOLIS * zonal_flow])
    tendency = DIFFUSE * laplace - advect + rotation
    surface_on = (lax.broadcasted_iota(jnp.int32, (1, ocean_depth, 1, 1), 1) == 0).astype(
        jnp.float32
    )
    updated = centre + OCEAN_DT * tendency + forcing[:, None] * surface_on
    return mask_grid[1:-1, 1:-1] * updated


def per_device(
    atm_state,
    diffusivity,
    surface_prev,
    flux_mix,
    entry_dest,
    entry_tile,
    entry_row,
    regrid_blocks,
    ocean_state,
    land_mask,
    flux_response,
):
    sec_count = lax.axis_size("sec")
    tile_count = lax.axis_size("tile")
    devices = sec_count * tile_count
    entries, tile_cols, ocean_cols = regrid_blocks.shape
    columns = atm_state.shape[2]
    atm_tiles = columns // tile_cols
    ocean_depth = ocean_state.shape[1]
    ocean_rows = ocean_state.shape[2]
    slot_count = devices * CAP
    atm_next, features = boundary_layer(atm_state, diffusivity, surface_prev)
    fluxes = jnp.dot(flux_mix, features, precision=PRECISE)
    flux_tiles = (
        fluxes.reshape(10, atm_tiles, tile_cols)
        .transpose(1, 0, 2)
        .reshape(atm_tiles, 10 * tile_cols)
    )
    pick_tile = (entry_tile[:, None] == jnp.arange(atm_tiles, dtype=jnp.int32)[None, :]).astype(
        jnp.float32
    )
    picked = jnp.dot(pick_tile, flux_tiles, precision=PRECISE).reshape(entries, 10, tile_cols)
    weights = regrid_blocks.astype(jnp.float32)
    contrib = jnp.einsum("efa,eat->eft", picked, weights, precision=PRECISE).reshape(
        entries, 10 * ocean_cols
    )
    dest_ids = entry_dest[:, 0]
    order_ids = jnp.arange(entries, dtype=jnp.int32)
    earlier = (dest_ids[:, None] == dest_ids[None, :]) & (order_ids[None, :] < order_ids[:, None])
    rank_ids = jnp.sum(earlier.astype(jnp.int32), axis=1)
    slot_ids = dest_ids * CAP + rank_ids
    placed = slot_ids[None, :] == jnp.arange(slot_count, dtype=jnp.int32)[:, None]
    place_f = placed.astype(jnp.float32)
    outgoing = jnp.dot(place_f, contrib, precision=PRECISE)
    row_slots = jnp.sum(jnp.where(placed, entry_row[None, :] + 1, 0), axis=1) - 1
    row_recv = lax.all_to_all(
        row_slots.reshape(devices, CAP), ("sec", "tile"), split_axis=0, concat_axis=0, tiled=True
    ).reshape(slot_count)
    incoming = lax.all_to_all(
        outgoing.reshape(devices, CAP, 10 * ocean_cols),
        ("sec", "tile"),
        split_axis=0,
        concat_axis=0,
        tiled=True,
    )
    incoming = incoming.reshape(slot_count, 10 * ocean_cols)
    gather_rows = (row_recv[None, :] == jnp.arange(ocean_rows, dtype=jnp.int32)[:, None]).astype(
        jnp.float32
    )
    cell_flux = jnp.dot(gather_rows, incoming, precision=PRECISE).reshape(
        ocean_rows, 10, ocean_cols
    )
    bulk_arg = jnp.einsum("kf,kxt->xft", flux_response, ocean_state[:, 0], precision=PRECISE)
    bulk = 1.0 + 0.5 * jnp.tanh(bulk_arg)
    forcing = jnp.einsum("gf,xft->gxt", flux_response, cell_flux * bulk, precision=PRECISE)
    stacked = jnp.concatenate(
        [
            ocean_state.reshape(4 * ocean_depth, ocean_rows, ocean_cols),
            land_mask.astype(jnp.float32)[None],
        ],
        0,
    )
    padded = with_halo(stacked, (("sec", 1), ("tile", 2)), 1)
    ocean_next = ocean_update(padded, forcing, ocean_depth)
    surface_rows = ocean_next[:, 0].transpose(1, 0, 2).reshape(ocean_rows, 4 * ocean_cols)
    returning = jnp.dot(gather_rows.T, surface_rows, precision=PRECISE)
    arrived = lax.all_to_all(
        returning.reshape(devices, CAP, 4 * ocean_cols),
        ("sec", "tile"),
        split_axis=0,
        concat_axis=0,
        tiled=True,
    )
    fetched = jnp.dot(place_f.T, arrived.reshape(slot_count, 4 * ocean_cols), precision=PRECISE)
    back_flux = jnp.einsum(
        "eft,eat->efa", fetched.reshape(entries, 4, ocean_cols), weights, precision=PRECISE
    ).reshape(entries, 4 * tile_cols)
    summed = jnp.dot(pick_tile.T, back_flux, precision=PRECISE)
    surface_next = summed.reshape(atm_tiles, 4, tile_cols).transpose(1, 0, 2).reshape(4, columns)
    return (atm_next, ocean_next, surface_next)


def solution(mesh):
    return jax.shard_map(
        per_device,
        mesh=mesh,
        in_specs=(
            P(None, None, ("sec", "tile")),
            P(None, ("sec", "tile")),
            P(None, ("sec", "tile")),
            P(),
            P(("sec", "tile"), None),
            P(("sec", "tile")),
            P(("sec", "tile")),
            P(("sec", "tile"), None, None),
            P(None, None, "sec", "tile"),
            P("sec", "tile"),
            P(),
        ),
        out_specs=(
            P(None, None, ("sec", "tile")),
            P(None, None, "sec", "tile"),
            P(None, ("sec", "tile")),
        ),
        check_vma=False,
    )
```

profile of v0, /device:TPU:0, one launch (start us, length us, event | category | flops | bytes accessed | tf_op | source)
XLA Modules:
  0.0 142.2 jit_solution(15345516979304194026)
XLA Ops:
  1.6 1.6 %pad_maximum_fusion.7 = (f32[33,1,128]{2,1,0:T(1,128)}, f32[33,1,128]{2,1,0:T(1,128)}) fusion(f32[1,64,128]{2,1,0:T(8,128)S(1)} %convert_bitcast_fusion, f32[32,64,128]{2,1,0:T(8,128)} %bitcast.556), kind=kLoop, calls=%fused_computation.288 | loop fusion | flops 8448 | bytes 1115136 | tf_op jit(solution)/shard_map/slice | solution.py:20
  4.5 6.1 %collective-permute-start = (f32[33,1,128]{2,1,0:T(1,128)}, f32[33,1,128]{2,1,0:T(1,128)}, u32[]{:S(2)}, u32[]{:S(2)}) collective-permute-start(f32[33,1,128]{2,1,0:T(1,128)} %get-tuple-element.148), channel_id=1, source_target_pairs={{0,8},{8,16},{16,24},{1,9},{9,17},{17,25},{2,10},{10,18},{18,26},{... | collective-permute-start | bytes 50696 | tf_op jit(solution)/shard_map/ppermute | solution.py:23
  13.5 5.7 %all-to-all-start = ((s32[32,1,4]{2,1,0:T(1,128)}), s32[32,1,4]{2,1,0:T(1,128)S(1)}, u32[]{:S(2)}, u32[]{:S(2)}) async-start(s32[32,1,4]{2,1,0:T(1,128)} %bitcast.166), calls=%async_computation | async-start | bytes 32768 | tf_op jit(solution)/shard_map/all_to_all | solution.py:137
  19.3 3.0 %slice_negate_fusion.27 = (f32[1,8192]{1,0:T(1,128)S(1)}, f32[1,8192]{1,0:T(1,128)S(1)}, f32[1,8192]{1,0:T(1,128)S(1)}, f32[1,8192]{1,0:T(1,128)S(1)}, f32[1,819...) fusion(f32[32,8192]{1,0:T(8,128)} %param.12), kind=kLoop, calls=%fused_computation.279 | loop fusion | flops 98304 | bytes 851968 | tf_op jit(solution)/shard_map/neg | solution.py:45
  23.7 2.8 %slice_subtract_fusion = (f32[1,8192]{1,0:T(1,128)S(1)}, f32[1,8192]{1,0:T(1,128)S(1)}, f32[1,8192]{1,0:T(1,128)S(1)}, f32[1,8192]{1,0:T(1,128)S(1)}, f32[1,8192...) fusion(f32[32,8192]{1,0:T(8,128)S(1)} %pad_add_fusion, ...), kind=kLoop, calls=%fused_computation.210 | loop fusion | flops 1015808 | bytes 4096000 | tf_op jit(solution)/shard_map/sub | solution.py:44
  28.9 2.6 %fusion.187 = (f32[4,1,8192]{2,1,0:T(1,128)S(1)}, f32[4,1,8192]{2,1,0:T(1,128)S(1)}, f32[4,1,8192]{2,1,0:T(1,128)S(1)}, f32[4,1,8192]{2,1,0:T(1,128)S(1)}, f32[4...) fusion(f32[4,32,8192]{2,1,0:T(8,128)S(1)} %copy-done.6), kind=kLoop, calls=%fused_computation.333 | loop fusion | bytes 4980736 | tf_op jit(solution)/shard_map/slice | solution.py:46
  32.7 5.8 %fusion.141 = (f32[4,8192]{1,0:T(4,128)S(1)}, f32[4,8192]{1,0:T(4,128)S(1)}, f32[4,8192]{1,0:T(4,128)S(1)}, f32[4,8192]{1,0:T(4,128)S(1)}, f32[4,8192]{1,0:T(4,1...) fusion(f32[4,8192]{1,0:T(4,128)S(1)} %copy-done.8, ...), kind=kLoop, calls=%fused_computation.332 | loop fusion | flops 5275648 | bytes 11763712 | tf_op jit(solution)/shard_map/mul | solution.py:56
  60.2 2.5 %fusion.11 = f32[64,10,128]{2,1,0:T(8,128)} fusion(bf16[64,128,128]{2,1,0:T(8,128)(2,1)S(1)} %copy-done, f32[64,10,128]{2,0,1:T(8,128)S(1)} %fusion.13), kind=kOutput, calls=%fused_computation.22 | convolution fusion | flops 125829120 | bytes 2752512 | tf_op jit(solution)/shard_map/efa,eat->eft/dot_general | solution.py:125
  62.7 1.8 %reshape.136 = f32[64,1280,1]{1,0,2:T(8,128)} reshape(f32[64,10,128]{2,1,0:T(8,128)} %fusion.11) | data formatting | bytes 655360 | tf_op jit(solution)/shard_map/reshape | solution.py:125
  66.8 2.3 %fusion.20 = f32[64,128,10]{1,2,0:T(8,128)} fusion(f32[4,1,64,128]{3,2,1,0:T(8,128)} %slice.532, f32[4,10]{1,0:T(4,128)} %param.21), kind=kOutput, calls=%fused_computation.41 | convolution fusion | flops 3932160 | bytes 458912 | tf_op jit(solution)/shard_map/kf,kxt->xft/dot_general | solution.py:154
  70.4 5.9 %all-to-all-start.1 = ((f32[32,4,1280]{2,1,0:T(4,128)}), f32[32,4,1280]{2,1,0:T(4,128)}, u32[]{:S(2)}, u32[]{:S(2)}) async-start(f32[32,4,1280]{2,1,0:T(4,128)} %copy.280), calls=%async_computation.1 | async-start | bytes 1310720 | tf_op jit(solution)/shard_map/all_to_all | solution.py:140
  77.2 1.8 %fusion.189 = (f32[33,66,1]{2,1,0:T(8,128)}, f32[33,66,1]{2,1,0:T(8,128)}) fusion(f32[33,66,128]{2,1,0:T(8,128)S(1)} %pad_maximum_fusion.5), kind=kLoop, calls=%fused_computation.335 | loop fusion | bytes 34848 | tf_op jit(solution)/shard_map/slice | solution.py:20
  79.0 2.3 %copy.272 = f32[33,66,1]{1,2,0:T(1,128)} copy(f32[33,66,1]{2,1,0:T(8,128)} %get-tuple-element.147) | data formatting | bytes 17424 | tf_op jit(solution)/shard_map/slice | solution.py:19
  82.7 2.3 %copy.271 = f32[33,66,1]{1,2,0:T(1,128)} copy(f32[33,66,1]{2,1,0:T(8,128)} %get-tuple-element.146) | data formatting | bytes 17424 | tf_op jit(solution)/shard_map/slice | solution.py:20
  85.0 3.6 %collective-permute-start.2 = (f32[33,66,1]{1,2,0:T(1,128)}, f32[33,66,1]{1,2,0:T(1,128)}, u32[]{:S(2)}, u32[]{:S(2)}) collective-permute-start(f32[33,66,1]{1,2,0:T(1,128)} %copy.271), channel_id=1, source_target_pairs={{0,1},{1,2},{2,3},{3,4},{4,5},{5,6},{6,7},{8,9},{9,10},{10,11},{11... | collective-permute-start | bytes 26144 | tf_op jit(solution)/shard_map/ppermute | solution.py:23
  92.3 2.2 %copy.274 = f32[33,66,1]{2,1,0:T(8,128)} copy(f32[33,66,1]{1,2,0:T(1,128)} %collective-permute-done.3) | data formatting | bytes 17424 | tf_op jit(solution)/shard_map/ppermute | solution.py:25
  94.5 2.3 %copy.273 = f32[33,66,1]{2,1,0:T(8,128)} copy(f32[33,66,1]{1,2,0:T(1,128)} %collective-permute-done.2) | data formatting | bytes 17424 | tf_op jit(solution)/shard_map/ppermute | solution.py:23
  98.5 1.9 %pad_maximum_fusion = f32[32,66,130]{2,1,0:T(8,128)S(1)} fusion(f32[33,66,1]{2,1,0:T(8,128)S(1)} %copy-done.4, f32[33,66,1]{2,1,0:T(8,128)S(1)} %copy-done.5, f32[33,1,128]{2,1,0:T(1,128)} %collective-permute-done.1, f32[33,1,128]{2,1,0:T(1,128)} %collective-permute-done, f32[1,64,128]{2,1,0:T(8,128)S(1)} %convert_bitcast_fusion, f32[32,64,128]{2,1,0:T(8,128)S(1)} %bitcast.559), kind=kLoop, calls=%fused_computation | loop fusion | flops 1372800 | bytes 2230800 | tf_op jit(solution)/shard_map/concatenate | solution.py:21
  103.1 2.1 %reshape.130 = f32[128,1280]{1,0:T(8,128)} reshape(f32[32,4,1280]{2,1,0:T(4,128)} %all-to-all-done.1) | data formatting | bytes 1310720 | tf_op jit(solution)/shard_map/reshape | solution.py:147
  108.8 6.5 %fusion.3 = f32[4,8,64,128]{3,2,1,0:T(8,128)S(1)} fusion(f32[1,8,64,128]{3,2,1,0:T(8,128)} %get-tuple-element.143, f32[1,8,64,128]{3,2,1,0:T(8,128)} %get-tuple-element.144, f32[4,8,66,130]{3,2,1,0:T(8,128)} %bitcast.555, f32[4]{0:T(128)S(1)} %copy-done.18, f32[8]{0:T(128)S(1)} %copy-done.17, f32[4,64,128]{2,1,0:T(8,128)S(1)} %copy.285, ...), kind=kLoop, calls=%fused_computation.13 | loop fusion | flops 7077888 | bytes 7634992 | tf_op jit(solution)/shard_map/mul | solution.py:88
  120.0 6.1 %all-to-all-start.2 = ((f32[32,4,512]{2,1,0:T(4,128)}), f32[32,4,512]{2,1,0:T(4,128)}, u32[]{:S(2)}, u32[]{:S(2)}) async-start(f32[32,4,512]{2,1,0:T(4,128)} %copy.288), calls=%async_computation.2 | async-start | bytes 524288 | tf_op jit(solution)/shard_map/all_to_all | solution.py:168
  126.9 6.6 %copy.292 = f32[4,32,8192]{2,1,0:T(8,128)} copy(f32[4,32,8192]{2,0,1:T(4,128)} %bitcast_dynamic-update-slice_fusion) | data formatting | bytes 8388608
  133.5 2.9 %all-to-all-done.2 = f32[32,4,512]{2,1,0:T(4,128)} async-done(((f32[32,4,512]{2,1,0:T(4,128)}), f32[32,4,512]{2,1,0:T(4,128)}, u32[]{:S(2)}, u32[]{:S(2)}) %all-to-all-start.2) | async-done | bytes 262176 | tf_op jit(solution)/shard_map/all_to_all | solution.py:168
  137.9 3.3 %fusion.85 = f32[64,4,128]{2,1,0:T(4,128)S(1)} fusion(bf16[64,128,128]{2,1,0:T(8,128)(2,1)S(1)} %copy-done, f32[64,4,128]{2,0,1:T(8,128)S(1)} %fusion.97), kind=kOutput, calls=%fused_computation.170 | convolution fusion | flops 50331648 | bytes 2359296 | tf_op jit(solution)/shard_map/eft,eat->efa/dot_general | solution.py:176
  (123 shorter events, 56.8 us)
Async XLA Ops:
  0.6 59.6 %copy-start = (bf16[64,128,128]{2,1,0:T(8,128)(2,1)S(1)}, bf16[64,128,128]{2,1,0:T(8,128)(2,1)}, u32[]{:S(2)}) copy-start(bf16[64,128,128]{2,1,0:T(8,128)(2,1)} %param.18) | copy-start | bytes 6291460
  0.6 22.9 %copy-start.3 = (f32[32,8192]{1,0:T(8,128)S(1)}, f32[32,8192]{1,0:T(8,128)}, u32[]{:S(2)}) copy-start(f32[32,8192]{1,0:T(8,128)} %param.12) | copy-start | bytes 3145732
  3.2 73.1 %collective-permute-start.1 = (f32[33,1,128]{2,1,0:T(1,128)}, f32[33,1,128]{2,1,0:T(1,128)}, u32[]{:S(2)}, u32[]{:S(2)}) collective-permute-start(f32[33,1,128]{2,1,0:T(1,128)} %get-tuple-element.149), channel_id=1, source_target_pairs={{8,0},{16,8},{24,16},{9,1},{17,9},{25,17},{10,2},{18,10},{26,18},{... | collective-permute-start | bytes 50696 | tf_op jit(solution)/shard_map/ppermute | solution.py:25
  4.5 71.9 %collective-permute-start = (f32[33,1,128]{2,1,0:T(1,128)}, f32[33,1,128]{2,1,0:T(1,128)}, u32[]{:S(2)}, u32[]{:S(2)}) collective-permute-start(f32[33,1,128]{2,1,0:T(1,128)} %get-tuple-element.148), channel_id=1, source_target_pairs={{0,8},{8,16},{16,24},{1,9},{9,17},{17,25},{2,10},{10,18},{18,26},{... | collective-permute-start | bytes 50696 | tf_op jit(solution)/shard_map/ppermute | solution.py:23
  13.5 56.9 %all-to-all-start = ((s32[32,1,4]{2,1,0:T(1,128)}), s32[32,1,4]{2,1,0:T(1,128)S(1)}, u32[]{:S(2)}, u32[]{:S(2)}) async-start(s32[32,1,4]{2,1,0:T(1,128)} %bitcast.166), calls=%async_computation | async-start | bytes 32768 | tf_op jit(solution)/shard_map/all_to_all | solution.py:137
  23.6 3.7 %copy-start.6 = (f32[4,32,8192]{2,1,0:T(8,128)S(1)}, f32[4,32,8192]{2,1,0:T(8,128)}, u32[]{:S(2)}) copy-start(f32[4,32,8192]{2,1,0:T(8,128)} %param.11) | copy-start | bytes 12582916
  27.3 4.8 %copy-start.2 = (f32[4,8,64,128]{3,2,1,0:T(8,128)S(1)}, f32[4,8,64,128]{3,2,1,0:T(8,128)}, u32[]{:S(2)}) copy-start(f32[4,8,64,128]{3,2,1,0:T(8,128)} %param.19) | copy-start | bytes 3145732
  27.3 5.4 %copy-start.8 = (f32[4,8192]{1,0:T(4,128)S(1)}, f32[4,8192]{1,0:T(4,128)}, u32[]{:S(2)}) copy-start(f32[4,8192]{1,0:T(4,128)} %param.13) | copy-start | bytes 393220
  42.6 16.2 %copy-start.9 = (f32[10,12]{1,0:T(8,128)S(1)}, f32[10,12]{1,0:T(8,128)}, u32[]{:S(2)}) copy-start(f32[10,12]{1,0:T(8,128)} %param.14) | copy-start | bytes 1444
  49.3 10.5 %copy-start.15 = (s32[64]{0:T(128)S(1)}, s32[64]{0:T(128)}, u32[]{:S(2)}) copy-start(s32[64]{0:T(128)} %param.16) | copy-start | bytes 772
  70.4 32.7 %all-to-all-start.1 = ((f32[32,4,1280]{2,1,0:T(4,128)}), f32[32,4,1280]{2,1,0:T(4,128)}, u32[]{:S(2)}, u32[]{:S(2)}) async-start(f32[32,4,1280]{2,1,0:T(4,128)} %copy.280), calls=%async_computation.1 | async-start | bytes 1310720 | tf_op jit(solution)/shard_map/all_to_all | solution.py:140
  81.4 10.9 %collective-permute-start.3 = (f32[33,66,1]{1,2,0:T(1,128)}, f32[33,66,1]{1,2,0:T(1,128)}, u32[]{:S(2)}, u32[]{:S(2)}) collective-permute-start(f32[33,66,1]{1,2,0:T(1,128)} %copy.272), channel_id=1, source_target_pairs={{1,0},{2,1},{3,2},{4,3},{5,4},{6,5},{7,6},{9,8},{10,9},{11,10},{12... | collective-permute-start | bytes 26144 | tf_op jit(solution)/shard_map/ppermute | solution.py:25
  85.0 9.5 %collective-permute-start.2 = (f32[33,66,1]{1,2,0:T(1,128)}, f32[33,66,1]{1,2,0:T(1,128)}, u32[]{:S(2)}, u32[]{:S(2)}) collective-permute-start(f32[33,66,1]{1,2,0:T(1,128)} %copy.271), channel_id=1, source_target_pairs={{0,1},{1,2},{2,3},{3,4},{4,5},{5,6},{6,7},{8,9},{9,10},{10,11},{11... | collective-permute-start | bytes 26144 | tf_op jit(solution)/shard_map/ppermute | solution.py:23
  96.8 1.7 %copy-start.5 = (f32[33,66,1]{2,1,0:T(8,128)S(1)}, f32[33,66,1]{2,1,0:T(8,128)}, u32[]{:S(2)}) copy-start(f32[33,66,1]{2,1,0:T(8,128)} %copy.273) | copy-start | bytes 26140
  98.5 8.0 %copy-start.14 = (s32[128]{0:T(128)S(1)}, s32[128]{0:T(128)}, u32[]{:S(2)}) copy-start(s32[128]{0:T(128)} %eq.104) | copy-start | bytes 1540
  100.4 1.4 %copy-start.1 = (f32[32,66,130]{2,1,0:T(8,128)}, f32[32,66,130]{2,1,0:T(8,128)S(1)}, u32[]{:S(2)}) copy-start(f32[32,66,130]{2,1,0:T(8,128)S(1)} %pad_maximum_fusion) | copy-start | bytes 3294724
  100.4 7.7 %copy-start.10 = (f32[4,10]{1,0:T(4,128)S(1)}, f32[4,10]{1,0:T(4,128)}, u32[]{:S(2)}) copy-start(f32[4,10]{1,0:T(4,128)} %param.21) | copy-start | bytes 484
  100.4 8.4 %copy-start.17 = (f32[8]{0:T(128)S(1)}, f32[8]{0:T(128)}, u32[]{:S(2)}) copy-start(f32[8]{0:T(128)} %compare_convert_fusion) | copy-start | bytes 100
  100.5 8.4 %copy-start.18 = (f32[4]{0:T(128)S(1)}, f32[4]{0:T(128)}, u32[]{:S(2)}) copy-start(f32[4]{0:T(128)} %pad.4.clone) | copy-start | bytes 52
  108.8 9.0 %copy-start.11 = (s32[32,1,4]{0,2,1:T(4,128)S(1)}, s32[32,1,4]{0,2,1:T(4,128)}, u32[]{:S(2)}) copy-start(s32[32,1,4]{0,2,1:T(4,128)} %copy.286) | copy-start | bytes 1540
  115.3 18.2 %copy-start.7 = (f32[4,8,64,128]{3,2,1,0:T(8,128)}, f32[4,8,64,128]{3,2,1,0:T(8,128)S(1)}, u32[]{:S(2)}) copy-start(f32[4,8,64,128]{3,2,1,0:T(8,128)S(1)} %fusion.3) | copy-start | bytes 3145732
  120.0 16.5 %all-to-all-start.2 = ((f32[32,4,512]{2,1,0:T(4,128)}), f32[32,4,512]{2,1,0:T(4,128)}, u32[]{:S(2)}, u32[]{:S(2)}) async-start(f32[32,4,512]{2,1,0:T(4,128)} %copy.288), calls=%async_computation.2 | async-start | bytes 524288 | tf_op jit(solution)/shard_map/all_to_all | solution.py:168
  126.9 10.7 %copy-start.13 = (s32[64]{0:T(128)S(1)}, s32[64]{0:T(128)}, u32[]{:S(2)}) copy-start(s32[64]{0:T(128)} %copy-done.12) | copy-start | bytes 772
  126.9 14.4 %copy-start.16 = (s32[64]{0:T(128)S(1)}, s32[64]{0:T(128)}, u32[]{:S(2)}) copy-start(s32[64]{0:T(128)} %param.16) | copy-start | bytes 772
  (2 other events, 1.9 us)
where the time goes:
time: 143 us; the launch traced here: 142 us
  local copies, waits for them, and re-layouts  52.2 us (37%)
  other arithmetic  41.3 us (29%)
  starting transfers between devices  30 us (21%)
  matrix products  14.6 us (10%)
  waiting for transfers between devices  2.93 us (2%)
    unnamed x57, local copies, waits for them, and re-layouts  19.8 us
    unnamed x15, other arithmetic  10.5 us
    ppermute x2, starting transfers between devices, with_halo(): lax.ppermute(tail, axis, [(i, (i + 1) % count) for i in range(ends)])  9.7 us
    mul x1, other arithmetic, ocean_update(): return mask_grid[1:-1, 1:-1] * updated  6.49 us
    all_to_all x1, starting transfers between devices, per_device(): lax.all_to_all(returning.reshape(devices, CAP, 4 * ocean_cols), ('sec', '...  6.11 us
    all_to_all x1, starting transfers between devices, per_device(): lax.all_to_all(outgoing.reshape(devices, CAP, 10 * ocean_cols), ('sec', '...  5.95 us
    mul x1, other arithmetic, boundary_layer(): turbulent * updated_state[:, 1]  5.78 us
    all_to_all x1, starting transfers between devices, per_device(): lax.all_to_all(row_slots.reshape(devices, CAP), ('sec', 'tile'), split_ax...  5.73 us
  transfers between devices with their start and end apart: 7, of which 1 were waited for; matrix products, arithmetic and copies ran while one was open for 57% of the time, Pallas kernels for 0%

commit v1 on v0

v1 whole, which is shorter than its diff:
```python
import functools

import jax
import jax.numpy as jnp
from jax import lax
from jax.experimental import pallas as pl
from jax.experimental.pallas import tpu as pltpu
from jax.sharding import PartitionSpec as P

CAP = 4
LANES = 128
SUB = 8
FLUXES = 10
FEATURES = 12
FIELDS = 4
DIFFUSE = 0.2
CORIOLIS = 0.3
OCEAN_DT = 0.2
F32 = jnp.float32
BF16 = jnp.bfloat16
BOTH = ("sec", "tile")


def halves(x):
    high = x.astype(BF16)
    return high, (x - high.astype(F32)).astype(BF16)


def dot32(a, b):
    return jnp.dot(a, b, preferred_element_type=F32)


def spec_any():
    return pl.BlockSpec(memory_space=pltpu.HBM)


def spec_vmem():
    return pl.BlockSpec(memory_space=pltpu.VMEM)


def spec_smem():
    return pl.BlockSpec(memory_space=pltpu.SMEM)


def params(mib):
    return pltpu.CompilerParams(vmem_limit_bytes=mib * 2**20)


def atm_kernel(
    chunks,
    a_ref,
    d_ref,
    s_ref,
    mix_ref,
    dest_ref,
    tile_ref,
    w_ref,
    y_ref,
    e_ref,
    out_ref,
    a_buf,
    d_buf,
    s_buf,
    w_buf,
    y_buf,
    e_buf,
    flux,
    count,
    in_sems,
    out_sems,
    s_sem,
    w_sem,
):
    blocks, tiles = a_buf.shape[1], a_buf.shape[2]
    levels = blocks * SUB
    entries = w_buf.shape[0]
    per = tiles // chunks
    groups = per // SUB
    devices = count.shape[0]

    def loads(ci):
        at = pl.ds(ci * per, per)
        return (
            pltpu.make_async_copy(a_ref.at[:, :, at], a_buf.at[:, :, at], in_sems.at[ci, 0]),
            pltpu.make_async_copy(d_ref.at[:, at], d_buf.at[:, at], in_sems.at[ci, 1]),
        )

    def saves(ci):
        at = pl.ds(ci * per, per)
        return (
            pltpu.make_async_copy(y_buf.at[:, :, at], y_ref.at[:, :, at], out_sems.at[ci, 0]),
            pltpu.make_async_copy(e_buf.at[:, at], e_ref.at[:, at], out_sems.at[ci, 1]),
        )

    s_copy = pltpu.make_async_copy(s_ref, s_buf, s_sem)
    w_copy = pltpu.make_async_copy(w_ref, w_buf, w_sem)
    for copy in loads(0):
        copy.start()
    s_copy.start()
    for ci in range(1, chunks):
        for copy in loads(ci):
            copy.start()
    w_copy.start()

    a_rows = a_buf.reshape(FIELDS * blocks * tiles * SUB, LANES)
    d_rows = d_buf.reshape(blocks * tiles * SUB, LANES)
    s_copy.wait()
    for d in range(devices):
        count[d] = 0
    out_ref[...] = jnp.zeros_like(out_ref)

    def chunk(ci, _):
        for copy in loads(ci):
            copy.wait()
        first = ci * per

        def block(step, carry):
            lb = blocks - 1 - step
            bottom = jnp.where(lb == 0, 1.0, 0.0).astype(F32)
            carry = list(carry)
            for r in range(SUB - 1, -1, -1):
                for g in range(groups):
                    tile = first + g * SUB
                    grow, above, ys = carry[g]
                    coup = d_rows[pl.ds((lb * tiles + tile) * SUB + r, SUB, stride=SUB), :]
                    weight = 1.0 + above * grow
                    inverse = 1.0 / (weight + coup)
                    solved = []
                    for v in range(FIELDS):
                        row = ((v * blocks + lb) * tiles + tile) * SUB + r
                        rhs = a_rows[pl.ds(row, SUB, stride=SUB), :]
                        if r == 0:
                            rhs = rhs + coup * (s_buf[v, pl.ds(tile, SUB), :] * bottom)
                        value = (rhs + above * ys[v]) * inverse
                        y_buf[v, lb * SUB + r, pl.ds(tile, SUB), :] = value
                        solved.append(value)
                    e_buf[lb * SUB + r, pl.ds(tile, SUB), :] = coup * inverse
                    carry[g] = (weight * inverse, coup, tuple(solved))
            return tuple(carry)

        zero = jnp.zeros((SUB, LANES), F32)
        start = tuple((zero, zero, (zero,) * FIELDS) for _ in range(groups))
        final = lax.fori_loop(0, blocks, block, start)
        for copy in saves(ci):
            copy.start()
        for g in range(groups):
            tile = first + g * SUB
            _, coup, x0 = final[g]
            e1 = e_buf[1, pl.ds(tile, SUB), :]
            turb = [coup * (s_buf[v, pl.ds(tile, SUB), :] - x0[v]) for v in range(FIELDS)]
            x1 = [y_buf[v, 1, pl.ds(tile, SUB), :] + e1 * x0[v] for v in range(FIELDS)]
            feats = turb + list(x0) + [turb[v] * x1[v] for v in range(FIELDS)]
            for f in range(FLUXES):
                total = mix_ref[f, 0] * feats[0]
                for k in range(1, FEATURES):
                    total = total + mix_ref[f, k] * feats[k]
                flux[pl.ds(tile * 16 + f, SUB, stride=16), :] = total
        return 0

    lax.fori_loop(0, chunks, chunk, 0)
    w_copy.wait()

    def entry(e, _):
        d = dest_ref[e, 0]
        k = count[d]
        count[d] = k + 1
        picked = flux[pl.ds(pl.multiple_of(tile_ref[e] * 16, 16), 16), :]
        high, low = halves(picked)
        both = dot32(jnp.concatenate([high, low], axis=0), w_buf[e])
        both = both[:16] + both[16:]
        row = d * (FLUXES * CAP) + k
        out_ref[pl.ds(row, SUB, stride=CAP), :] = both[:SUB]
        out_ref[pl.ds(row + SUB * CAP, FLUXES - SUB, stride=CAP), :] = both[SUB:FLUXES]
        return 0

    lax.fori_loop(0, entries, entry, 0, unroll=8)
    for ci in range(chunks):
        for copy in saves(ci):
            copy.wait()


def atm_forward(a_tiles, d_tiles, s_tiles, mix, dest, tile_ids, weights, devices):
    _, blocks, tiles, _, _ = a_tiles.shape
    levels = blocks * SUB
    entries = weights.shape[0]
    chunks = 2
    return pl.pallas_call(
        functools.partial(atm_kernel, chunks),
        out_shape=(
            jax.ShapeDtypeStruct((FIELDS, levels, tiles, LANES), F32),
            jax.ShapeDtypeStruct((levels, tiles, LANES), F32),
            jax.ShapeDtypeStruct((devices * FLUXES * CAP, LANES), F32),
        ),
        in_specs=[
            spec_any(),
            spec_any(),
            spec_any(),
            spec_smem(),
            spec_smem(),
            spec_smem(),
            spec_any(),
        ],
        out_specs=(spec_any(), spec_any(), spec_vmem()),
        scratch_shapes=[
            pltpu.VMEM(a_tiles.shape, F32),
            pltpu.VMEM(d_tiles.shape, F32),
            pltpu.VMEM(s_tiles.shape, F32),
            pltpu.VMEM(weights.shape, BF16),
            pltpu.VMEM((FIELDS, levels, tiles, LANES), F32),
            pltpu.VMEM((levels, tiles, LANES), F32),
            pltpu.VMEM((tiles * 16, LANES), F32),
            pltpu.SMEM((devices,), jnp.int32),
            pltpu.SemaphoreType.DMA((chunks, 2)),
            pltpu.SemaphoreType.DMA((chunks, 2)),
            pltpu.SemaphoreType.DMA,
            pltpu.SemaphoreType.DMA,
        ],
        compiler_params=params(48),
        name="atm_forward",
    )(a_tiles, d_tiles, s_tiles, mix, dest, tile_ids, weights)


def back_kernel(y_ref, e_ref, out_ref):
    blocks, tiles = out_ref.shape[1], out_ref.shape[2]
    rows = out_ref.reshape(FIELDS * blocks * tiles * SUB, LANES)
    groups = tiles // SUB

    def block(lb, carry):
        carry = list(carry)
        for r in range(SUB):
            for g in range(groups):
                coef = e_ref[lb * SUB + r, pl.ds(g * SUB, SUB), :]
                if r == 0:
                    coef = coef * jnp.where(lb == 0, 0.0, 1.0).astype(F32)
                for v in range(FIELDS):
                    x = y_ref[v, lb * SUB + r, pl.ds(g * SUB, SUB), :]
                    x = x + coef * carry[g * FIELDS + v]
                    row = ((v * blocks + lb) * tiles + g * SUB) * SUB + r
                    rows[pl.ds(row, SUB, stride=SUB), :] = x
                    carry[g * FIELDS + v] = x
        return tuple(carry)

    zero = jnp.zeros((SUB, LANES), F32)
    lax.fori_loop(0, blocks, block, (zero,) * (groups * FIELDS))


def atm_back(y, e):
    _, levels, tiles, _ = y.shape
    blocks = levels // SUB
    per = 16
    return pl.pallas_call(
        back_kernel,
        grid=(tiles // per,),
        out_shape=jax.ShapeDtypeStruct((FIELDS, blocks, tiles, SUB, LANES), F32),
        in_specs=[
            pl.BlockSpec((FIELDS, levels, per, LANES), lambda i: (0, 0, i, 0)),
            pl.BlockSpec((levels, per, LANES), lambda i: (0, i, 0)),
        ],
        out_specs=pl.BlockSpec((FIELDS, blocks, per, SUB, LANES), lambda i: (0, 0, i, 0, 0)),
        compiler_params=params(32),
        cost_estimate=pl.CostEstimate(
            flops=2 * y.size, bytes_accessed=9 * y.size, transcendentals=0
        ),
        name="atm_back",
    )(y, e)


def edge_kernel(
    q_ref, m_ref, dest_ref, row_ref, low_row, high_row, low_col, high_col, table, slots, count
):
    sec, tile = lax.axis_index("sec"), lax.axis_index("tile")
    me = sec * lax.axis_size("tile") + tile
    fields, rows, _ = q_ref.shape
    devices = count.shape[0]
    entries = row_ref.shape[0]
    pad = low_row.shape[0]
    lane_rows = table.shape[1]
    mask = m_ref[...].astype(F32)

    for dst, at in ((low_row, 0), (high_row, rows - 1)):
        dst[...] = jnp.zeros_like(dst)
        for i in range(fields):
            dst[i : i + 1, :] = q_ref[i, at : at + 1, :]
        dst[fields : fields + 1, :] = mask[at : at + 1, :]

    lane = lax.broadcasted_iota(jnp.int32, (SUB, LANES), 1)
    sub = lax.broadcasted_iota(jnp.int32, (SUB, LANES), 0)
    pick = ((sub == 0) & (lane == 0)) | ((sub == 1) & (lane == LANES - 1))
    pick = pick.astype(F32)
    low_col[...] = jnp.zeros_like(low_col)
    high_col[...] = jnp.zeros_like(high_col)
    for i in range(fields + 1):
        cells = q_ref[i] if i < fields else mask
        ends = lax.dot_general(
            pick,
            cells,
            (((1,), (1,)), ((), ())),
            precision=lax.Precision.HIGHEST,
            preferred_element_type=F32,
        )
        low_col[i : i + 1, 0:rows] = ends[0:1]
        high_col[i : i + 1, 0:rows] = ends[1:2]

    table[...] = jnp.zeros_like(table)
    for d in range(devices):
        count[d] = 0
    spot = lax.broadcasted_iota(jnp.int32, (lane_rows, LANES), 0) * LANES
    spot = spot + lax.broadcasted_iota(jnp.int32, (lane_rows, LANES), 1)

    def entry(e, _):
        d = dest_ref[e, 0]
        k = count[d]
        count[d] = k + 1
        slots[e] = d * CAP + k
        here = me * (2 * CAP) + k
        hit = (spot == here) | (spot == here + CAP)
        table[d] = table[d] + jnp.where(hit, row_ref[e] + 1, 0)
        return 0

    lax.fori_loop(0, entries, entry, 0)


def ocean_edges(q, mask, dest, row_ids, devices):
    pad = -(-(q.shape[0] + 1) // SUB) * SUB
    edge = jax.ShapeDtypeStruct((pad, LANES), F32)
    lane_rows = devices * 2 * CAP // LANES
    return pl.pallas_call(
        edge_kernel,
        out_shape=(edge,) * 4
        + (
            jax.ShapeDtypeStruct((devices, lane_rows, LANES), jnp.int32),
            jax.ShapeDtypeStruct((row_ids.shape[0],), jnp.int32),
        ),
        in_specs=[spec_vmem(), spec_vmem(), spec_smem(), spec_smem()],
        out_specs=(spec_vmem(),) * 5 + (spec_smem(),),
        scratch_shapes=[pltpu.SMEM((devices,), jnp.int32)],
        compiler_params=params(32),
        name="ocean_edges",
    )(q, mask, dest, row_ids)


def shift(axis, step):
    count = lax.axis_size(axis)
    if step > 0:
        return [(i, i + 1) for i in range(count - 1)]
    return [(i + 1, i) for i in range(count - 1)]


def ocean_kernel(
    depth,
    q_ref,
    m_ref,
    east_ref,
    west_ref,
    north_ref,
    south_ref,
    table_ref,
    resp_ref,
    out_ref,
    surf_ref,
    bulk_ref,
    hot_ref,
    hot_t_ref,
    col_buf,
):
    fields, rows, _ = q_ref.shape
    pad = north_ref.shape[0]
    lane_rows = table_ref.shape[1]
    col_buf[...] = jnp.zeros_like(col_buf)
    col_buf[0, 0:pad, :] = north_ref[...]
    col_buf[1, 0:pad, :] = south_ref[...]
    north_t = jnp.transpose(col_buf[0])[0:rows]
    south_t = jnp.transpose(col_buf[1])[0:rows]
    lane = lax.broadcasted_iota(jnp.int32, (rows, LANES), 1)
    last, first = lane == LANES - 1, lane == 0

    def around(cells, i):
        east = jnp.concatenate([cells[1:], east_ref[i : i + 1, :]], axis=0)
        west = jnp.concatenate([west_ref[i : i + 1, :], cells[:-1]], axis=0)
        north = jnp.where(last, north_t[:, i : i + 1], pltpu.roll(cells, LANES - 1, 1))
        south = jnp.where(first, south_t[:, i : i + 1], pltpu.roll(cells, 1, 1))
        return east, west, north, south

    mask = m_ref[...].astype(F32)
    m_east, m_west, m_north, m_south = around(mask, fields)
    m_all = m_east + m_west + m_north + m_south
    for level in range(depth):
        zonal = q_ref[2 * depth + level]
        merid = q_ref[3 * depth + level]
        for v in range(FIELDS):
            i = v * depth + level
            cells = q_ref[i]
            east, west, north, south = around(cells, i)
            lap = m_east * east + m_west * west + m_north * north + m_south * south
            lap = lap - m_all * cells
            adv = 0.5 * (zonal * (east - west) + merid * (north - south))
            tend = DIFFUSE * lap - adv
            if v == 2:
                tend = tend + CORIOLIS * merid
            if v == 3:
                tend = tend - CORIOLIS * zonal
            value = mask * (cells + OCEAN_DT * tend)
            out_ref[i] = value
            if level == 0:
                surf_ref[v] = value

    tops = [q_ref[v * depth] for v in range(FIELDS)]
    for f in range(FLUXES):
        total = resp_ref[0, f] * tops[0]
        for v in range(1, FIELDS):
            total = total + resp_ref[v, f] * tops[v]
        bulk_ref[f] = 1.0 + 0.5 * jnp.tanh(total)

    seen = jnp.sum(table_ref[...], axis=0)
    x = lax.broadcasted_iota(jnp.int32, (2 * rows, LANES), 0)
    spot = lax.broadcasted_iota(jnp.int32, (2 * rows, LANES), 1)
    pair = (spot // CAP) % 2 == x // rows
    for j in range(lane_rows):
        hot = (seen[j : j + 1, :] - 1 == x % rows) & pair
        hot = hot.astype(F32)
        hot_ref[:, j * LANES : (j + 1) * LANES] = hot.astype(BF16)
        hot_t_ref[j * LANES : (j + 1) * LANES, :] = jnp.transpose(hot).astype(BF16)


def ocean_step(q, mask, edges, table, response, depth):
    fields, rows, _ = q.shape
    slots = table.shape[0] * 2 * CAP
    return pl.pallas_call(
        functools.partial(ocean_kernel, depth),
        out_shape=(
            jax.ShapeDtypeStruct(q.shape, F32),
            jax.ShapeDtypeStruct((FIELDS, rows, LANES), F32),
            jax.ShapeDtypeStruct((FLUXES, rows, LANES), F32),
            jax.ShapeDtypeStruct((2 * rows, slots), BF16),
            jax.ShapeDtypeStruct((slots, 2 * rows), BF16),
        ),
        in_specs=[spec_vmem()] * 7 + [spec_smem()],
        out_specs=(spec_vmem(),) * 5,
        scratch_shapes=[pltpu.VMEM((2, LANES, LANES), F32)],
        compiler_params=params(32),
        name="ocean_step",
    )(q, mask, *edges, table, response)


def combine_kernel(
    depth, got_ref, hot_ref, hot_t_ref, bulk_ref, surf_ref, m_ref, resp_ref, q_ref,
    out_ref, back_ref, top, sems,
):
    rows = m_ref.shape[0]
    sources = got_ref.shape[0]
    force = [None] * FIELDS
    hot = hot_ref[...]
    for j in range(FLUXES // 2):
        data = got_ref[:, j * SUB : (j + 1) * SUB, :].reshape(sources * SUB, LANES)
        high, low = halves(data)
        both = dot32(hot, high) + dot32(hot, low)
        for p in range(2):
            f = 2 * j + p
            drive = both[p * rows : (p + 1) * rows] * bulk_ref[f]
            for g in range(FIELDS):
                term = resp_ref[g, f] * drive
                force[g] = term if f == 0 else force[g] + term
    mask = m_ref[...].astype(F32)
    for g in range(FIELDS):
        top[g] = surf_ref[g] + mask * force[g]
    copies = [
        pltpu.make_async_copy(top.at[g], out_ref.at[g * depth], sems.at[g]) for g in range(FIELDS)
    ]
    for copy in copies:
        copy.start()
    hot_t = hot_t_ref[...]
    for j in range(FIELDS // 2):
        pair = jnp.concatenate([top[2 * j], top[2 * j + 1]], axis=0)
        high, low = halves(pair)
        both = dot32(hot_t, high) + dot32(hot_t, low)
        back_ref[:, j * SUB : (j + 1) * SUB, :] = both.reshape(sources, SUB, LANES)
    for copy in copies:
        copy.wait()


def ocean_combine(got, hot, hot_t, bulk, surf, mask, response, q_next, depth):
    sources = got.shape[0]
    return pl.pallas_call(
        functools.partial(combine_kernel, depth),
        out_shape=(
            jax.ShapeDtypeStruct(q_next.shape, F32),
            jax.ShapeDtypeStruct((sources, FIELDS * CAP, LANES), F32),
        ),
        in_specs=[spec_vmem()] * 6 + [spec_smem(), spec_any()],
        out_specs=(spec_any(), spec_vmem()),
        scratch_shapes=[
            pltpu.VMEM(surf.shape, F32),
            pltpu.SemaphoreType.DMA((FIELDS,)),
        ],
        input_output_aliases={7: 0},
        compiler_params=params(32),
        name="ocean_combine",
    )(got, hot, hot_t, bulk, surf, mask, response, q_next)


def regrid_kernel(got_ref, w_ref, slot_ref, tile_ref, out_ref):
    entries = w_ref.shape[0]
    out_ref[...] = jnp.zeros_like(out_ref)

    def group(i, _):
        results = []
        for u in range(SUB):
            e = i * SUB + u
            slot = slot_ref[e]
            row = (slot // CAP) * (FIELDS * CAP) + slot % CAP
            rows = got_ref[pl.ds(row, FIELDS, stride=CAP), :]
            high, low = halves(rows)
            both = lax.dot_general(
                jnp.concatenate([high, low], axis=0),
                w_ref[e],
                (((1,), (1,)), ((), ())),
                preferred_element_type=F32,
            )
            results.append((tile_ref[e], both[:FIELDS] + both[FIELDS:]))
        for tile, value in results:
            out_ref[tile] = out_ref[tile] + value
        return 0

    lax.fori_loop(0, entries // SUB, group, 0)


def regrid_back(got, weights, slots, tile_ids, tiles):
    return pl.pallas_call(
        regrid_kernel,
        out_shape=jax.ShapeDtypeStruct((tiles, FIELDS, LANES), F32),
        in_specs=[spec_vmem(), spec_vmem(), spec_smem(), spec_smem()],
        out_specs=spec_vmem(),
        compiler_params=params(32),
        name="regrid_back",
    )(got, weights, slots, tile_ids)


def exchange(x):
    return lax.all_to_all(x, BOTH, split_axis=0, concat_axis=0, tiled=True)


def per_device(
    atm_state,
    diffusivity,
    surface_prev,
    flux_mix,
    entry_dest,
    entry_tile,
    entry_row,
    regrid_blocks,
    ocean_state,
    land_mask,
    flux_response,
):
    devices = lax.axis_size("sec") * lax.axis_size("tile")
    _, levels, columns = atm_state.shape
    blocks, tiles = levels // SUB, columns // LANES
    _, depth, rows, _ = ocean_state.shape

    a_tiles = atm_state.reshape(FIELDS, blocks, SUB, tiles, LANES).transpose(0, 1, 3, 2, 4)
    d_tiles = diffusivity.reshape(blocks, SUB, tiles, LANES).transpose(0, 2, 1, 3)
    s_tiles = surface_prev.reshape(FIELDS, tiles, LANES)
    y, e, outgoing = atm_forward(
        a_tiles, d_tiles, s_tiles, flux_mix, entry_dest, entry_tile, regrid_blocks, devices
    )

    q = ocean_state.reshape(FIELDS * depth, rows, LANES)
    outgoing, q = lax.optimization_barrier((outgoing, q))
    incoming = exchange(outgoing.reshape(devices, FLUXES * CAP, LANES))

    low_row, high_row, low_col, high_col, table, slots = ocean_edges(
        q, land_mask, entry_dest, entry_row, devices
    )
    edges = (
        lax.ppermute(low_row, "sec", shift("sec", -1)),
        lax.ppermute(high_row, "sec", shift("sec", 1)),
        lax.ppermute(low_col, "tile", shift("tile", -1)),
        lax.ppermute(high_col, "tile", shift("tile", 1)),
    )
    table = exchange(table)
    q_base, surf, bulk, hot, hot_t = ocean_step(q, land_mask, edges, table, flux_response, depth)

    q_next, returning = ocean_combine(
        incoming, hot, hot_t, bulk, surf, land_mask, flux_response, q_base, depth
    )
    returning, y, e = lax.optimization_barrier((returning, y, e))
    arrived = exchange(returning)
    atm_next = atm_back(y, e).transpose(0, 1, 3, 2, 4).reshape(FIELDS, levels, columns)
    back = regrid_back(
        arrived.reshape(devices * FIELDS * CAP, LANES), regrid_blocks, slots, entry_tile, tiles
    )
    surface_next = back.transpose(1, 0, 2).reshape(FIELDS, columns)
    return atm_next, q_next.reshape(ocean_state.shape), surface_next


def solution(mesh):
    return jax.shard_map(
        per_device,
        mesh=mesh,
        in_specs=(
            P(None, None, BOTH),
            P(None, BOTH),
            P(None, BOTH),
            P(),
            P(BOTH, None),
            P(BOTH),
            P(BOTH),
            P(BOTH, None, None),
            P(None, None, "sec", "tile"),
            P("sec", "tile"),
            P(),
        ),
        out_specs=(
            P(None, None, BOTH),
            P(None, None, "sec", "tile"),
            P(None, BOTH),
        ),
        check_vma=False,
    )
```

time: 143 us -> 73.9 us (0.52)
  local copies, waits for them, and re-layouts: 52.2 us -> 8.04 us
  other arithmetic: 41.3 us -> 0 us
  Pallas kernels: 0 us -> 21.8 us
  matrix products: 14.6 us -> 0 us
  blocking collectives: 0 us -> 14.3 us
  starting transfers between devices: 30 us -> 17.2 us
  waiting for transfers between devices: 2.93 us -> 11.1 us
    pallas_call x0 -> x6, Pallas kernels: none -> 21.8 us  [the longest x1 5.97 us: atm_forward(): pl.pallas_call(functools.partial(atm_kernel, chunks), out_shape=(jax.Shap...]
    dot_general x11 -> x0, matrix products: 14.6 us -> none  [the longest x1 3.33 us: per_device(): jnp.einsum('eft,eat->efa', fetched.reshape(entries, 4, ocean_cols), weigh...]
    all_to_all x0 -> x1, blocking collectives: none -> 14.3 us  [exchange(): return lax.all_to_all(x, BOTH, split_axis=0, concat_axis=0, tiled=True)]
    slice x9 -> x0, local copies, waits for them, and re-layouts: 13.5 us -> none  [the longest x2 4.15 us: boundary_layer(): d_prev = (atmos_state[:, lev_index] - coupling_low * d_prev) / pivot_value]
    mul x3 -> x0, other arithmetic: 13.5 us -> none  [the longest x1 6.49 us: ocean_update(): return mask_grid[1:-1, 1:-1] * updated]
    unnamed x57 -> x26, local copies, waits for them, and re-layouts: 19.8 us -> 8.04 us
    all_to_all x3 -> x2, starting transfers between devices: 17.8 us -> 7.07 us  [exchange(): return lax.all_to_all(x, BOTH, split_axis=0, concat_axis=0, tiled=True)]
    unnamed x15 -> x0, other arithmetic: 10.5 us -> none
  transfers between devices with their start and end apart: 7 -> 6, of which waited for: 1 -> 3; matrix products, arithmetic and copies ran while one was open for 57% -> 0% of each run, Pallas kernels for 0% -> 8%
where the time goes in v1:
time: 73.9 us; the launch traced here: 73.3 us
  Pallas kernels  21.8 us (29%)
  starting transfers between devices  17.2 us (23%)
  blocking collectives  14.3 us (19%)
  waiting for transfers between devices  11.1 us (15%)
  local copies, waits for them, and re-layouts  8.04 us (11%)
  between operations  0.8 us (1%)
    all_to_all x1, blocking collectives, exchange(): return lax.all_to_all(x, BOTH, split_axis=0, concat_axis=0, tiled=True)  14.3 us
    all_to_all x2, waiting for transfers between devices, exchange(): return lax.all_to_all(x, BOTH, split_axis=0, concat_axis=0, tiled=True)  10.3 us
    unnamed x26, local copies, waits for them, and re-layouts  8.04 us
    all_to_all x2, starting transfers between devices, exchange(): return lax.all_to_all(x, BOTH, split_axis=0, concat_axis=0, tiled=True)  7.07 us
    pallas_call x1, Pallas kernels, atm_forward(): pl.pallas_call(functools.partial(atm_kernel, chunks), out_shape=(jax.Shap...  5.97 us
    ppermute x1, starting transfers between devices, per_device(): lax.ppermute(high_row, 'sec', shift('sec', 1))  4.55 us
    pallas_call x1, Pallas kernels, ocean_edges(): pl.pallas_call(edge_kernel, out_shape=(edge,) * 4 + (jax.ShapeDtypeStruct...  4.24 us
    pallas_call x1, Pallas kernels, regrid_back(): pl.pallas_call(regrid_kernel, out_shape=jax.ShapeDtypeStruct((tiles, FIEL...  3.25 us
  transfers between devices with their start and end apart: 6, of which 3 were waited for; matrix products, arithmetic and copies ran while one was open for 0% of the time, Pallas kernels for 8%

profile of v1, /device:TPU:0, one launch (start us, length us, event | category | flops | bytes accessed | tf_op | source)
XLA Modules:
  0.0 73.3 jit_solution(14905246318998678997)
XLA Ops:
  0.7 0.8 %copy.15.dest_ref = s32[64,1]{1,0:T(8,128)S(1)} copy(s32[64,1]{0,1:T(1,128)} %param.15) | data formatting | bytes 512 | tf_op args[4]
  1.4 0.9 %copy.19 = f32[1,4,64,128]{3,2,1,0:T(8,128)S(1)} copy(f32[1,4,64,128]{3,1,2,0:T(4,128)} %bitcast.30) | data formatting | bytes 262144
  2.3 0.0 copy-start
  2.3 1.6 %copy-done = bf16[64,128,128]{2,1,0:T(8,128)(2,1)S(1)} copy-done((bf16[64,128,128]{2,1,0:T(8,128)(2,1)S(1)}, bf16[64,128,128]{2,1,0:T(8,128)(2,1)}, u32[]{:S(2)}) %copy-start) | copy-done | bytes 2097176
  3.9 1.2 %copy-done.4 = f32[32,8192]{1,0:T(8,128)S(1)} copy-done((f32[32,8192]{1,0:T(8,128)S(1)}, f32[32,8192]{1,0:T(8,128)}, u32[]{:S(2)}) %copy-start.4) | copy-done | bytes 1048600
  5.1 0.7 copy-done.7
  5.8 0.7 copy-done.9
  6.5 6.0 %atm_forward.1 = (f32[4,32,64,128]{3,2,1,0:T(8,128)}, f32[32,64,128]{2,1,0:T(8,128)S(1)}, f32[1280,128]{1,0:T(8,128)S(1)}) custom-call(f32[4,4,64,8,128]{4,3,2,1,0:T(8,128)} %bitcast.26, f32[4,64,8,128]{3,2,1,0:T(8,128)S(1)} %bitcast.23, f32[4,64,128]{2,1,0:T(8,128)S(1)} %bitcast.25, f32[10,12]{1,0:T(8,128)S(1)} %copy-done.7, s32[64,1]{1,0:T(8,128)S(1)} %copy.15.dest_ref, ...), custom_call_target="tpu_custom_call" | custom-call | tf_op jit(solution)/shard_map/atm_forward/pallas_call | solution.py:187
  12.5 4.2 %ocean_edges.1 = (f32[40,128]{1,0:T(8,128)S(1)}, f32[40,128]{1,0:T(8,128)S(1)}, f32[40,128]{1,0:T(8,128)S(1)}, f32[40,128]{1,0:T(8,128)S(1)}, s32[32,2,128]{2,1,0:T(2,128)S(1)}, /*index=5*/s32[64]{0:T(128)S(1)}) custom-call(f32[32,64,128]{2,1,0:T(8,128)S(1)} %bitcast.20, s32[64,128]{1,0:T(8,128)S(1)} %copy-done.6, s32[64,1]{1,0:T(8,128)S(1)} %copy.15.dest_ref, ...), custom_call_target="tpu_custom_call" | custom-call | tf_op jit(solution)/shard_map/ocean_edges/pallas_call | solution.py:327
  16.8 14.3 %all_to_all.15.table_ref = s32[32,2,128]{2,1,0:T(2,128)S(1)} all-to-all(s32[32,2,128]{2,1,0:T(2,128)S(1)} %get-tuple-element.31), channel_id=1, replica_groups=mesh['sec'=4,'tile'=8] {'sec','tile'}, dimensions={0} | all-to-all | bytes 65536 | tf_op jit(solution)/shard_map/all_to_all | solution.py:539
  31.1 2.6 %all-to-all-start = ((f32[32,40,128]{2,1,0:T(8,128)}), f32[32,40,128]{2,1,0:T(8,128)S(1)}, u32[]{:S(2)}, u32[]{:S(2)}) async-start(f32[32,40,128]{2,1,0:T(8,128)} %bitcast.24), calls=%async_computation | async-start | bytes 1310720 | tf_op jit(solution)/shard_map/all_to_all | solution.py:539
  33.7 1.3 %collective-permute-start = (f32[40,128]{1,0:T(8,128)S(1)}, f32[40,128]{1,0:T(8,128)S(1)}, u32[]{:S(2)}, u32[]{:S(2)}) collective-permute-start(f32[40,128]{1,0:T(8,128)S(1)} %get-tuple-element.27), channel_id=1, source_target_pairs={{8,0},{16,8},{24,16},{9,1},{17,9},{25,17},{10,2},{18,10},{26,18},{... | collective-permute-start | bytes 61448 | tf_op jit(solution)/shard_map/ppermute | solution.py:575
  35.0 4.5 %collective-permute-start.1 = (f32[40,128]{1,0:T(8,128)S(1)}, f32[40,128]{1,0:T(8,128)S(1)}, u32[]{:S(2)}, u32[]{:S(2)}) collective-permute-start(f32[40,128]{1,0:T(8,128)S(1)} %get-tuple-element.28), channel_id=1, source_target_pairs={{0,8},{8,16},{16,24},{1,9},{9,17},{17,25},{2,10},{10,18},{18,26},{... | collective-permute-start | bytes 61448 | tf_op jit(solution)/shard_map/ppermute | solution.py:576
  39.6 1.3 %collective-permute-start.2 = (f32[40,128]{1,0:T(8,128)S(1)}, f32[40,128]{1,0:T(8,128)S(1)}, u32[]{:S(2)}, u32[]{:S(2)}) collective-permute-start(f32[40,128]{1,0:T(8,128)S(1)} %get-tuple-element.29), channel_id=1, source_target_pairs={{1,0},{2,1},{3,2},{4,3},{5,4},{6,5},{7,6},{9,8},{10,9},{11,10},{12... | collective-permute-start | bytes 61448 | tf_op jit(solution)/shard_map/ppermute | solution.py:577
  40.9 3.0 %collective-permute-start.3 = (f32[40,128]{1,0:T(8,128)S(1)}, f32[40,128]{1,0:T(8,128)S(1)}, u32[]{:S(2)}, u32[]{:S(2)}) collective-permute-start(f32[40,128]{1,0:T(8,128)S(1)} %get-tuple-element.30), channel_id=1, source_target_pairs={{0,1},{1,2},{2,3},{3,4},{4,5},{5,6},{6,7},{8,9},{9,10},{10,11},{11... | collective-permute-start | bytes 61448 | tf_op jit(solution)/shard_map/ppermute | solution.py:578
  44.0 0.8 %collective-permute-done.3.south_ref = f32[40,128]{1,0:T(8,128)S(1)} collective-permute-done((f32[40,128]{1,0:T(8,128)S(1)}, f32[40,128]{1,0:T(8,128)S(1)}, u32[]{:S(2)}, u32[]{:S(2)}) %collective-permute-start.3) | collective-permute-done | bytes 20512 | tf_op jit(solution)/shard_map/ppermute | solution.py:578
  44.8 3.0 %ocean_step.1 = (f32[32,64,128]{2,1,0:T(8,128)}, f32[4,64,128]{2,1,0:T(8,128)S(1)}, f32[10,64,128]{2,1,0:T(8,128)S(1)}, bf16[128,256]{1,0:T(8,128)(2,1)S(1)}, bf16[256,128]{1,0:T(8,128)(2,1)S(1)}) custom-call(f32[32,64,128]{2,1,0:T(8,128)S(1)} %bitcast.21, s32[64,128]{1,0:T(8,128)S(1)} %copy-done.6, f32[40,128]{1,0:T(8,128)S(1)} %collective-permute-done.east_ref, ...), custom_call_target="tpu_custom_call" | custom-call | tf_op jit(solution)/shard_map/ocean_step/pallas_call | solution.py:428
  47.7 5.2 %all-to-all-done.got_ref = f32[32,40,128]{2,1,0:T(8,128)S(1)} async-done(((f32[32,40,128]{2,1,0:T(8,128)}), f32[32,40,128]{2,1,0:T(8,128)S(1)}, u32[]{:S(2)}, u32[]{:S(2)}) %all-to-all-start) | async-done | bytes 655392 | tf_op jit(solution)/shard_map/all_to_all | solution.py:539
  52.9 2.3 %ocean_combine.1 = (f32[32,64,128]{2,1,0:T(8,128)}, f32[32,16,128]{2,1,0:T(8,128)}) custom-call(f32[32,40,128]{2,1,0:T(8,128)S(1)} %all-to-all-done.got_ref, bf16[128,256]{1,0:T(8,128)(2,1)S(1)} %get-tuple-element.32.hot_ref, bf16[256,128]{1,0:T(8,128)(2,1)S(1)} %get-tuple-element.33.hot_t_ref, ...), custom_call_target="tpu_custom_call", output_to_operand_aliasing={{0}: (7, {})} | custom-call | tf_op jit(solution)/shard_map/ocean_combine/pallas_call | solution.py:483
  55.2 4.5 %all-to-all-start.2 = ((f32[32,16,128]{2,1,0:T(8,128)}), f32[32,16,128]{2,1,0:T(8,128)S(1)}, u32[]{:S(2)}, u32[]{:S(2)}) async-start(f32[32,16,128]{2,1,0:T(8,128)} %get-tuple-element.43), calls=%async_computation.2 | async-start | bytes 524288 | tf_op jit(solution)/shard_map/all_to_all | solution.py:539
  59.7 2.2 %copy-done.2 = f32[4,32,64,128]{3,2,1,0:T(8,128)S(1)} copy-done((f32[4,32,64,128]{3,2,1,0:T(8,128)S(1)}, f32[4,32,64,128]{3,2,1,0:T(8,128)}, u32[]{:S(2)}) %copy-start.2) | copy-done | bytes 4194328
  61.8 3.1 %atm_back.1 = f32[4,4,64,8,128]{4,3,2,1,0:T(8,128)} custom-call(f32[4,32,64,128]{3,2,1,0:T(8,128)S(1)} %copy-done.2, f32[32,64,128]{2,1,0:T(8,128)S(1)} %get-tuple-element.41.e_ref), custom_call_target="tpu_custom_call" | custom-call | flops 2097152 | bytes 9437184 | tf_op jit(solution)/shard_map/atm_back/pallas_call | solution.py:251
  65.0 5.1 %all-to-all-done.2 = f32[32,16,128]{2,1,0:T(8,128)S(1)} async-done(((f32[32,16,128]{2,1,0:T(8,128)}), f32[32,16,128]{2,1,0:T(8,128)S(1)}, u32[]{:S(2)}, u32[]{:S(2)}) %all-to-all-start.2) | async-done | bytes 262176 | tf_op jit(solution)/shard_map/all_to_all | solution.py:539
  70.0 3.3 %regrid_back.1 = f32[64,4,128]{2,1,0:T(4,128)} custom-call(f32[512,128]{1,0:T(8,128)S(1)} %bitcast.22, bf16[64,128,128]{2,1,0:T(8,128)(2,1)S(1)} %copy-done.1, s32[64]{0:T(128)S(1)} %get-tuple-element.44.slot_ref, s32[64]{0:T(128)S(1)} %copy-done.10), custom_call_target="tpu_custom_call" | custom-call | tf_op jit(solution)/shard_map/regrid_back/pallas_call | solution.py:528
  (21 shorter events, 0.0 us)
Async XLA Ops:
  0.6 11.9 %copy-start.11 = (s32[64]{0:T(128)S(1)}, s32[64]{0:T(128)}, u32[]{:S(2)}) copy-start(s32[64]{0:T(128)} %row_ref.1) | copy-start | bytes 772
  0.6 11.9 %copy-start.6 = (s32[64,128]{1,0:T(8,128)S(1)}, s32[64,128]{1,0:T(8,128)}, u32[]{:S(2)}) copy-start(s32[64,128]{1,0:T(8,128)} %m_ref.5) | copy-start | bytes 98308
  2.3 1.6 %copy-start = (bf16[64,128,128]{2,1,0:T(8,128)(2,1)S(1)}, bf16[64,128,128]{2,1,0:T(8,128)(2,1)}, u32[]{:S(2)}) copy-start(bf16[64,128,128]{2,1,0:T(8,128)(2,1)} %w_ref.3) | copy-start | bytes 6291460
  3.9 1.2 %copy-start.4 = (f32[32,8192]{1,0:T(8,128)S(1)}, f32[32,8192]{1,0:T(8,128)}, u32[]{:S(2)}) copy-start(f32[32,8192]{1,0:T(8,128)} %param.12) | copy-start | bytes 3145732
  5.1 0.7 copy-start.7
  5.8 0.7 copy-start.9
  6.5 6.0 %copy-start.3 = (f32[4,8,64,128]{3,2,1,0:T(8,128)S(1)}, f32[4,8,64,128]{3,2,1,0:T(8,128)}, u32[]{:S(2)}) copy-start(f32[4,8,64,128]{3,2,1,0:T(8,128)} %param.19) | copy-start | bytes 3145732
  6.5 38.3 %copy-start.8 = (f32[4,10]{1,0:T(4,128)S(1)}, f32[4,10]{1,0:T(4,128)}, u32[]{:S(2)}) copy-start(f32[4,10]{1,0:T(4,128)} %resp_ref.3) | copy-start | bytes 484
  12.5 18.6 %copy-start.5 = (f32[1280,128]{1,0:T(8,128)}, f32[1280,128]{1,0:T(8,128)S(1)}, u32[]{:S(2)}) copy-start(f32[1280,128]{1,0:T(8,128)S(1)} %get-tuple-element.25) | copy-start | bytes 1966084
  31.1 21.8 %all-to-all-start = ((f32[32,40,128]{2,1,0:T(8,128)}), f32[32,40,128]{2,1,0:T(8,128)S(1)}, u32[]{:S(2)}, u32[]{:S(2)}) async-start(f32[32,40,128]{2,1,0:T(8,128)} %bitcast.24), calls=%async_computation | async-start | bytes 1310720 | tf_op jit(solution)/shard_map/all_to_all | solution.py:539
  33.7 10.2 %collective-permute-start = (f32[40,128]{1,0:T(8,128)S(1)}, f32[40,128]{1,0:T(8,128)S(1)}, u32[]{:S(2)}, u32[]{:S(2)}) collective-permute-start(f32[40,128]{1,0:T(8,128)S(1)} %get-tuple-element.27), channel_id=1, source_target_pairs={{8,0},{16,8},{24,16},{9,1},{17,9},{25,17},{10,2},{18,10},{26,18},{... | collective-permute-start | bytes 61448 | tf_op jit(solution)/shard_map/ppermute | solution.py:575
  35.0 8.9 %collective-permute-start.1 = (f32[40,128]{1,0:T(8,128)S(1)}, f32[40,128]{1,0:T(8,128)S(1)}, u32[]{:S(2)}, u32[]{:S(2)}) collective-permute-start(f32[40,128]{1,0:T(8,128)S(1)} %get-tuple-element.28), channel_id=1, source_target_pairs={{0,8},{8,16},{16,24},{1,9},{9,17},{17,25},{2,10},{10,18},{18,26},{... | collective-permute-start | bytes 61448 | tf_op jit(solution)/shard_map/ppermute | solution.py:576
  39.6 4.4 %collective-permute-start.2 = (f32[40,128]{1,0:T(8,128)S(1)}, f32[40,128]{1,0:T(8,128)S(1)}, u32[]{:S(2)}, u32[]{:S(2)}) collective-permute-start(f32[40,128]{1,0:T(8,128)S(1)} %get-tuple-element.29), channel_id=1, source_target_pairs={{1,0},{2,1},{3,2},{4,3},{5,4},{6,5},{7,6},{9,8},{10,9},{11,10},{12... | collective-permute-start | bytes 61448 | tf_op jit(solution)/shard_map/ppermute | solution.py:577
  40.9 3.9 %collective-permute-start.3 = (f32[40,128]{1,0:T(8,128)S(1)}, f32[40,128]{1,0:T(8,128)S(1)}, u32[]{:S(2)}, u32[]{:S(2)}) collective-permute-start(f32[40,128]{1,0:T(8,128)S(1)} %get-tuple-element.30), channel_id=1, source_target_pairs={{0,1},{1,2},{2,3},{3,4},{4,5},{5,6},{6,7},{8,9},{9,10},{10,11},{11... | collective-permute-start | bytes 61448 | tf_op jit(solution)/shard_map/ppermute | solution.py:578
  55.2 14.8 %all-to-all-start.2 = ((f32[32,16,128]{2,1,0:T(8,128)}), f32[32,16,128]{2,1,0:T(8,128)S(1)}, u32[]{:S(2)}, u32[]{:S(2)}) async-start(f32[32,16,128]{2,1,0:T(8,128)} %get-tuple-element.43), calls=%async_computation.2 | async-start | bytes 524288 | tf_op jit(solution)/shard_map/all_to_all | solution.py:539
  59.6 2.2 %copy-start.2 = (f32[4,32,64,128]{3,2,1,0:T(8,128)S(1)}, f32[4,32,64,128]{3,2,1,0:T(8,128)}, u32[]{:S(2)}) copy-start(f32[4,32,64,128]{3,2,1,0:T(8,128)} %get-tuple-element.40.y_ref) | copy-start | bytes 12582916
  61.8 8.2 %copy-start.1 = (bf16[64,128,128]{2,1,0:T(8,128)(2,1)S(1)}, bf16[64,128,128]{2,1,0:T(8,128)(2,1)}, u32[]{:S(2)}) copy-start(bf16[64,128,128]{2,1,0:T(8,128)(2,1)} %w_ref.3) | copy-start | bytes 6291460
  61.8 8.2 %copy-start.10 = (s32[64]{0:T(128)S(1)}, s32[64]{0:T(128)}, u32[]{:S(2)}) copy-start(s32[64]{0:T(128)} %tile_ref.3) | copy-start | bytes 772

commit v2 on v1

--- a/solution.py
+++ b/solution.py
@@ -54,10 +54,12 @@
     mix_ref,
     dest_ref,
     tile_ref,
+    row_ref,
     w_ref,
     y_ref,
     e_ref,
     out_ref,
+    slot_ref,
     a_buf,
     d_buf,
     s_buf,
@@ -77,6 +79,12 @@
     per = tiles // chunks
     groups = per // SUB
     devices = count.shape[0]
+    chunk_rows = out_ref.shape[0] // devices
+    table_rows = chunk_rows - FLUXES * CAP
+    me = lax.axis_index("sec") * lax.axis_size("tile") + lax.axis_index("tile")
+
+    def surface(v, tile):
+        return s_buf[pl.ds(tile * FIELDS + v, SUB, stride=FIELDS), :]
 
     def loads(ci):
         at = pl.ds(ci * per, per)
@@ -130,7 +138,7 @@
                         row = ((v * blocks + lb) * tiles + tile) * SUB + r
                         rhs = a_rows[pl.ds(row, SUB, stride=SUB), :]
                         if r == 0:
-                            rhs = rhs + coup * (s_buf[v, pl.ds(tile, SUB), :] * bottom)
+                            rhs = rhs + coup * (surface(v, tile) * bottom)
                         value = (rhs + above * ys[v]) * inverse
                         y_buf[v, lb * SUB + r, pl.ds(tile, SUB), :] = value
                         solved.append(value)
@@ -147,7 +155,7 @@
             tile = first + g * SUB
             _, coup, x0 = final[g]
             e1 = e_buf[1, pl.ds(tile, SUB), :]
-            turb = [coup * (s_buf[v, pl.ds(tile, SUB), :] - x0[v]) for v in range(FIELDS)]
+            turb = [coup * (surface(v, tile) - x0[v]) for v in range(FIELDS)]
             x1 = [y_buf[v, 1, pl.ds(tile, SUB), :] + e1 * x0[v] for v in range(FIELDS)]
             feats = turb + list(x0) + [turb[v] * x1[v] for v in range(FIELDS)]
             for f in range(FLUXES):
@@ -160,15 +168,23 @@
     lax.fori_loop(0, chunks, chunk, 0)
     w_copy.wait()
 
+    spot = lax.broadcasted_iota(jnp.int32, (table_rows, LANES), 0) * LANES
+    spot = spot + lax.broadcasted_iota(jnp.int32, (table_rows, LANES), 1)
+
     def entry(e, _):
-        d = dest_ref[e, 0]
+        d = dest_ref[e]
         k = count[d]
         count[d] = k + 1
+        slot_ref[e] = d * (FIELDS * CAP) + k
+        here = me * (2 * CAP) + k
+        hit = (spot == here) | (spot == here + CAP)
+        table = pl.ds(d * chunk_rows + FLUXES * CAP, table_rows)
+        out_ref[table, :] += jnp.where(hit, row_ref[e] + 1, 0).astype(F32)
         picked = flux[pl.ds(pl.multiple_of(tile_ref[e] * 16, 16), 16), :]
         high, low = halves(picked)
         both = dot32(jnp.concatenate([high, low], axis=0), w_buf[e])
         both = both[:16] + both[16:]
-        row = d * (FLUXES * CAP) + k
+        row = d * chunk_rows + k
         out_ref[pl.ds(row, SUB, stride=CAP), :] = both[:SUB]
         out_ref[pl.ds(row + SUB * CAP, FLUXES - SUB, stride=CAP), :] = both[SUB:FLUXES]
         return 0
@@ -179,17 +195,19 @@
             copy.wait()
 
 
-def atm_forward(a_tiles, d_tiles, s_tiles, mix, dest, tile_ids, weights, devices):
+def atm_forward(a_tiles, d_tiles, s_rows, mix, dest, tile_ids, row_ids, weights, devices):
     _, blocks, tiles, _, _ = a_tiles.shape
     levels = blocks * SUB
     entries = weights.shape[0]
     chunks = 2
+    chunk_rows = FLUXES * CAP + devices * 2 * CAP // LANES
     return pl.pallas_call(
         functools.partial(atm_kernel, chunks),
         out_shape=(
             jax.ShapeDtypeStruct((FIELDS, levels, tiles, LANES), F32),
             jax.ShapeDtypeStruct((levels, tiles, LANES), F32),
-            jax.ShapeDtypeStruct((devices * FLUXES * CAP, LANES), F32),
+            jax.ShapeDtypeStruct((devices * chunk_rows, LANES), F32),
+            jax.ShapeDtypeStruct((entries,), jnp.int32),
         ),
         in_specs=[
             spec_any(),
@@ -198,13 +216,14 @@
             spec_smem(),
             spec_smem(),
             spec_smem(),
+            spec_smem(),
             spec_any(),
         ],
-        out_specs=(spec_any(), spec_any(), spec_vmem()),
+        out_specs=(spec_any(), spec_any(), spec_vmem(), spec_smem()),
         scratch_shapes=[
             pltpu.VMEM(a_tiles.shape, F32),
             pltpu.VMEM(d_tiles.shape, F32),
-            pltpu.VMEM(s_tiles.shape, F32),
+            pltpu.VMEM(s_rows.shape, F32),
             pltpu.VMEM(weights.shape, BF16),
             pltpu.VMEM((FIELDS, levels, tiles, LANES), F32),
             pltpu.VMEM((levels, tiles, LANES), F32),
@@ -215,9 +234,9 @@
             pltpu.SemaphoreType.DMA,
             pltpu.SemaphoreType.DMA,
         ],
-        compiler_params=params(48),
+        compiler_params=params(60),
         name="atm_forward",
-    )(a_tiles, d_tiles, s_tiles, mix, dest, tile_ids, weights)
+    )(a_tiles, d_tiles, s_rows, mix, dest, tile_ids, row_ids, weights)
 
 
 def back_kernel(y_ref, e_ref, out_ref):
@@ -257,7 +276,7 @@
             pl.BlockSpec((levels, per, LANES), lambda i: (0, i, 0)),
         ],
         out_specs=pl.BlockSpec((FIELDS, blocks, per, SUB, LANES), lambda i: (0, 0, i, 0, 0)),
-        compiler_params=params(32),
+        compiler_params=params(56),
         cost_estimate=pl.CostEstimate(
             flops=2 * y.size, bytes_accessed=9 * y.size, transcendentals=0
         ),
@@ -265,78 +284,40 @@
     )(y, e)
 
 
-def edge_kernel(
-    q_ref, m_ref, dest_ref, row_ref, low_row, high_row, low_col, high_col, table, slots, count
-):
-    sec, tile = lax.axis_index("sec"), lax.axis_index("tile")
-    me = sec * lax.axis_size("tile") + tile
+def edge_kernel(q_ref, m_ref, low_row, high_row, low_col, high_col):
     fields, rows, _ = q_ref.shape
-    devices = count.shape[0]
-    entries = row_ref.shape[0]
-    pad = low_row.shape[0]
-    lane_rows = table.shape[1]
     mask = m_ref[...].astype(F32)
-
     for dst, at in ((low_row, 0), (high_row, rows - 1)):
         dst[...] = jnp.zeros_like(dst)
         for i in range(fields):
             dst[i : i + 1, :] = q_ref[i, at : at + 1, :]
         dst[fields : fields + 1, :] = mask[at : at + 1, :]
 
-    lane = lax.broadcasted_iota(jnp.int32, (SUB, LANES), 1)
-    sub = lax.broadcasted_iota(jnp.int32, (SUB, LANES), 0)
-    pick = ((sub == 0) & (lane == 0)) | ((sub == 1) & (lane == LANES - 1))
-    pick = pick.astype(F32)
-    low_col[...] = jnp.zeros_like(low_col)
-    high_col[...] = jnp.zeros_like(high_col)
+    lane = lax.broadcasted_iota(jnp.int32, (rows, LANES), 1)
+    low = jnp.zeros((rows, LANES), F32)
+    high = jnp.zeros((rows, LANES), F32)
     for i in range(fields + 1):
         cells = q_ref[i] if i < fields else mask
-        ends = lax.dot_general(
-            pick,
-            cells,
-            (((1,), (1,)), ((), ())),
-            precision=lax.Precision.HIGHEST,
-            preferred_element_type=F32,
-        )
-        low_col[i : i + 1, 0:rows] = ends[0:1]
-        high_col[i : i + 1, 0:rows] = ends[1:2]
-
-    table[...] = jnp.zeros_like(table)
-    for d in range(devices):
-        count[d] = 0
-    spot = lax.broadcasted_iota(jnp.int32, (lane_rows, LANES), 0) * LANES
-    spot = spot + lax.broadcasted_iota(jnp.int32, (lane_rows, LANES), 1)
-
-    def entry(e, _):
-        d = dest_ref[e, 0]
-        k = count[d]
-        count[d] = k + 1
-        slots[e] = d * CAP + k
-        here = me * (2 * CAP) + k
-        hit = (spot == here) | (spot == here + CAP)
-        table[d] = table[d] + jnp.where(hit, row_ref[e] + 1, 0)
-        return 0
-
-    lax.fori_loop(0, entries, entry, 0)
-
-
-def ocean_edges(q, mask, dest, row_ids, devices):
+        turned = pltpu.roll(cells, i, 1) if i else cells
+        low = jnp.where(lane == i, turned, low)
+        high = jnp.where(lane == (i + LANES - 1) % LANES, turned, high)
+    low_col[...] = low
+    high_col[...] = high
+
+
+def ocean_edges(q, mask):
     pad = -(-(q.shape[0] + 1) // SUB) * SUB
-    edge = jax.ShapeDtypeStruct((pad, LANES), F32)
-    lane_rows = devices * 2 * CAP // LANES
+    row = jax.ShapeDtypeStruct((pad, LANES), F32)
+    col = jax.ShapeDtypeStruct(mask.shape, F32)
     return pl.pallas_call(
         edge_kernel,
-        out_shape=(edge,) * 4
-        + (
-            jax.ShapeDtypeStruct((devices, lane_rows, LANES), jnp.int32),
-            jax.ShapeDtypeStruct((row_ids.shape[0],), jnp.int32),
-        ),
-        in_specs=[spec_vmem(), spec_vmem(), spec_smem(), spec_smem()],
-        out_specs=(spec_vmem(),) * 5 + (spec_smem(),),
-        scratch_shapes=[pltpu.SMEM((devices,), jnp.int32)],
+        out_shape=(row, row, col, col),
+        in_specs=[spec_vmem(), spec_vmem()],
+        out_specs=(spec_vmem(),) * 4,
         compiler_params=params(32),
+        cost_estimate=pl.CostEstimate(flops=q.size, bytes_accessed=4 * q.size, transcendentals=0),
         name="ocean_edges",
-    )(q, mask, dest, row_ids)
+    )(q, mask)
 
 
 def shift(axis, step):
@@ -354,31 +335,23 @@
     west_ref,
     north_ref,
     south_ref,
-    table_ref,
     resp_ref,
     out_ref,
     surf_ref,
     bulk_ref,
-    hot_ref,
-    hot_t_ref,
-    col_buf,
 ):
     fields, rows, _ = q_ref.shape
-    pad = north_ref.shape[0]
-    lane_rows = table_ref.shape[1]
-    col_buf[...] = jnp.zeros_like(col_buf)
-    col_buf[0, 0:pad, :] = north_ref[...]
-    col_buf[1, 0:pad, :] = south_ref[...]
-    north_t = jnp.transpose(col_buf[0])[0:rows]
-    south_t = jnp.transpose(col_buf[1])[0:rows]
     lane = lax.broadcasted_iota(jnp.int32, (rows, LANES), 1)
     last, first = lane == LANES - 1, lane == 0
+
+    def south_at(i):
+        return (i + LANES - 1) % LANES
 
     def around(cells, i):
         east = jnp.concatenate([cells[1:], east_ref[i : i + 1, :]], axis=0)
         west = jnp.concatenate([west_ref[i : i + 1, :], cells[:-1]], axis=0)
-        north = jnp.where(last, north_t[:, i : i + 1], pltpu.roll(cells, LANES - 1, 1))
-        south = jnp.where(first, south_t[:, i : i + 1], pltpu.roll(cells, 1, 1))
+        north = jnp.where(last, north_ref[:, i : i + 1], pltpu.roll(cells, LANES - 1, 1))
+        south = jnp.where(first, south_ref[:, south_at(i) : south_at(i) + 1], pltpu.roll(cells, 1, 1))
         return east, west, north, south
 
     mask = m_ref[...].astype(F32)
@@ -411,47 +384,50 @@
             total = total + resp_ref[v, f] * tops[v]
         bulk_ref[f] = 1.0 + 0.5 * jnp.tanh(total)
 
-    seen = jnp.sum(table_ref[...], axis=0)
-    x = lax.broadcasted_iota(jnp.int32, (2 * rows, LANES), 0)
-    spot = lax.broadcasted_iota(jnp.int32, (2 * rows, LANES), 1)
-    pair = (spot // CAP) % 2 == x // rows
-    for j in range(lane_rows):
-        hot = (seen[j : j + 1, :] - 1 == x % rows) & pair
-        hot = hot.astype(F32)
-        hot_ref[:, j * LANES : (j + 1) * LANES] = hot.astype(BF16)
-        hot_t_ref[j * LANES : (j + 1) * LANES, :] = jnp.transpose(hot).astype(BF16)
-
-
-def ocean_step(q, mask, edges, table, response, depth):
-    fields, rows, _ = q.shape
-    slots = table.shape[0] * 2 * CAP
+
+def ocean_step(q, mask, edges, response, depth):
+    rows = q.shape[1]
     return pl.pallas_call(
         functools.partial(ocean_kernel, depth),
         out_shape=(
             jax.ShapeDtypeStruct(q.shape, F32),
             jax.ShapeDtypeStruct((FIELDS, rows, LANES), F32),
             jax.ShapeDtypeStruct((FLUXES, rows, LANES), F32),
-            jax.ShapeDtypeStruct((2 * rows, slots), BF16),
-            jax.ShapeDtypeStruct((slots, 2 * rows), BF16),
         ),
-        in_specs=[spec_vmem()] * 7 + [spec_smem()],
-        out_specs=(spec_vmem(),) * 5,
-        scratch_shapes=[pltpu.VMEM((2, LANES, LANES), F32)],
+        in_specs=[spec_vmem()] * 6 + [spec_smem()],
+        out_specs=(spec_vmem(),) * 3,
         compiler_params=params(32),
+        cost_estimate=pl.CostEstimate(
+            flops=30 * q.size, bytes_accessed=8 * q.size, transcendentals=0
+        ),
         name="ocean_step",
-    )(q, mask, *edges, table, response)
+    )(q, mask, *edges, response)
 
 
 def combine_kernel(
-    depth, got_ref, hot_ref, hot_t_ref, bulk_ref, surf_ref, m_ref, resp_ref, q_ref,
-    out_ref, back_ref, top, sems,
+    depth, got_ref, bulk_ref, surf_ref, m_ref, resp_ref, q_ref, out_ref, back_ref, top, sems
 ):
     rows = m_ref.shape[0]
-    sources = got_ref.shape[0]
+    sources = back_ref.shape[0]
+    chunk_rows = got_ref.shape[0] // sources
+    table_rows = chunk_rows - FLUXES * CAP
+
+    x = lax.broadcasted_iota(jnp.int32, (2 * rows, LANES), 0)
+    spot = lax.broadcasted_iota(jnp.int32, (2 * rows, LANES), 1)
+    pair = (spot // CAP) % 2 == x // rows
+    wanted = jnp.where(pair, (x % rows + 1).astype(F32), -1.0)
+    hots = []
+    for j in range(table_rows):
+        seen = got_ref[pl.ds(FLUXES * CAP + j, sources, stride=chunk_rows), :]
+        seen = jnp.sum(seen, axis=0, keepdims=True)
+        hots.append((seen == wanted).astype(F32))
+    hot = jnp.concatenate([h.astype(BF16) for h in hots], axis=1)
+
     force = [None] * FIELDS
-    hot = hot_ref[...]
     for j in range(FLUXES // 2):
-        data = got_ref[:, j * SUB : (j + 1) * SUB, :].reshape(sources * SUB, LANES)
+        data = jnp.concatenate(
+            [got_ref[pl.ds(s * chunk_rows + j * SUB, SUB), :] for s in range(sources)], axis=0
+        )
         high, low = halves(data)
         both = dot32(hot, high) + dot32(hot, low)
         for p in range(2):
@@ -468,7 +444,7 @@
     ]
     for copy in copies:
         copy.start()
-    hot_t = hot_t_ref[...]
+    hot_t = jnp.concatenate([jnp.transpose(h).astype(BF16) for h in hots], axis=0)
     for j in range(FIELDS // 2):
         pair = jnp.concatenate([top[2 * j], top[2 * j + 1]], axis=0)
         high, low = halves(pair)
@@ -478,24 +454,23 @@
         copy.wait()
 
 
-def ocean_combine(got, hot, hot_t, bulk, surf, mask, response, q_next, depth):
-    sources = got.shape[0]
+def ocean_combine(got, bulk, surf, mask, response, q_next, depth, sources):
     return pl.pallas_call(
         functools.partial(combine_kernel, depth),
         out_shape=(
             jax.ShapeDtypeStruct(q_next.shape, F32),
             jax.ShapeDtypeStruct((sources, FIELDS * CAP, LANES), F32),
         ),
-        in_specs=[spec_vmem()] * 6 + [spec_smem(), spec_any()],
+        in_specs=[spec_vmem()] * 4 + [spec_smem(), spec_any()],
         out_specs=(spec_any(), spec_vmem()),
         scratch_shapes=[
             pltpu.VMEM(surf.shape, F32),
             pltpu.SemaphoreType.DMA((FIELDS,)),
         ],
-        input_output_aliases={7: 0},
+        input_output_aliases={5: 0},
         compiler_params=params(32),
         name="ocean_combine",
-    )(got, hot, hot_t, bulk, surf, mask, response, q_next)
+    )(got, bulk, surf, mask, response, q_next)
 
 
 def regrid_kernel(got_ref, w_ref, slot_ref, tile_ref, out_ref):
@@ -507,8 +482,7 @@
         for u in range(SUB):
             e = i * SUB + u
             slot = slot_ref[e]
-            row = (slot // CAP) * (FIELDS * CAP) + slot % CAP
-            rows = got_ref[pl.ds(row, FIELDS, stride=CAP), :]
+            rows = got_ref[pl.ds(slot, FIELDS, stride=CAP), :]
             high, low = halves(rows)
             both = lax.dot_general(
                 jnp.concatenate([high, low], axis=0),
@@ -559,29 +533,37 @@
 
     a_tiles = atm_state.reshape(FIELDS, blocks, SUB, tiles, LANES).transpose(0, 1, 3, 2, 4)
     d_tiles = diffusivity.reshape(blocks, SUB, tiles, LANES).transpose(0, 2, 1, 3)
-    s_tiles = surface_prev.reshape(FIELDS, tiles, LANES)
-    y, e, outgoing = atm_forward(
-        a_tiles, d_tiles, s_tiles, flux_mix, entry_dest, entry_tile, regrid_blocks, devices
+    s_rows = surface_prev.reshape(FIELDS, tiles, LANES).transpose(1, 0, 2)
+    s_rows = s_rows.reshape(tiles * FIELDS, LANES)
+    y, e, outgoing, slots = atm_forward(
+        a_tiles,
+        d_tiles,
+        s_rows,
+        flux_mix,
+        entry_dest[:, 0],
+        entry_tile,
+        entry_row,
+        regrid_blocks,
+        devices,
     )
 
     q = ocean_state.reshape(FIELDS * depth, rows, LANES)
     outgoing, q = lax.optimization_barrier((outgoing, q))
-    incoming = exchange(outgoing.reshape(devices, FLUXES * CAP, LANES))
-
-    low_row, high_row, low_col, high_col, table, slots = ocean_edges(
-        q, land_mask, entry_dest, entry_row, devices
-    )
+    chunk_rows = outgoing.shape[0] // devices
+    incoming = exchange(outgoing.reshape(devices, chunk_rows // 2, 2, LANES))
+    incoming = incoming.reshape(outgoing.shape)
+
+    low_row, high_row, low_col, high_col = ocean_edges(q, land_mask)
     edges = (
         lax.ppermute(low_row, "sec", shift("sec", -1)),
         lax.ppermute(high_row, "sec", shift("sec", 1)),
         lax.ppermute(low_col, "tile", shift("tile", -1)),
         lax.ppermute(high_col, "tile", shift("tile", 1)),
     )
-    table = exchange(table)
-    q_base, surf, bulk, hot, hot_t = ocean_step(q, land_mask, edges, table, flux_response, depth)
+    q_base, surf, bulk = ocean_step(q, land_mask, edges, flux_response, depth)
 
     q_next, returning = ocean_combine(
-        incoming, hot, hot_t, bulk, surf, land_mask, flux_response, q_base, depth
+        incoming, bulk, surf, land_mask, flux_response, q_base, depth, devices
     )
     returning, y, e = lax.optimization_barrier((returning, y, e))
     arrived = exchange(returning)

time: 73.9 us -> 56.5 us (0.76)
  blocking collectives: 14.3 us -> 0 us
  local copies, waits for them, and re-layouts: 8.04 us -> 0.03 us
  starting transfers between devices: 17.2 us -> 22.5 us
    all_to_all x1 -> x0, blocking collectives: 14.3 us -> none  [exchange(): return lax.all_to_all(x, BOTH, split_axis=0, concat_axis=0, tiled=True)]
    unnamed x26 -> x12, local copies, waits for them, and re-layouts: 8.04 us -> 0.03 us
    all_to_all x2, starting transfers between devices: 7.07 us -> 12.3 us  [exchange(): return lax.all_to_all(x, BOTH, split_axis=0, concat_axis=0, tiled=True)]
    pallas_call x1, Pallas kernels: 4.24 us -> 0.36 us  [ocean_edges(): pl.pallas_call(edge_kernel, out_shape=(row, row, col, col), in_specs=[spe...]
    pallas_call x1, Pallas kernels: 3.12 us -> 5.39 us  [atm_back(): pl.pallas_call(back_kernel, grid=(tiles // per,), out_shape=jax.ShapeDtyp...]
    ppermute x1, waiting for transfers between devices: 0.01 us -> 1.45 us  [per_device(): lax.ppermute(high_row, 'sec', shift('sec', 1))]
    pallas_call x1, Pallas kernels: 5.97 us -> 7.29 us  [atm_forward(): pl.pallas_call(functools.partial(atm_kernel, chunks), out_shape=(jax.Shap...]
    ppermute x1, waiting for transfers between devices: 0.79 us -> 0.01 us  [per_device(): lax.ppermute(high_col, 'tile', shift('tile', 1))]
  transfers between devices with their start and end apart: 6 -> 6, of which waited for: 3 -> 3; matrix products, arithmetic and copies ran while one was open for 0% -> 0% of each run, Pallas kernels for 8% -> 16%
where the time goes in v2:
time: 56.5 us; the launch traced here: 56.2 us
  starting transfers between devices  22.5 us (40%)
  Pallas kernels  21.9 us (39%)
  waiting for transfers between devices  10.9 us (19%)
  between operations  0.79 us (1%)
    all_to_all x2, starting transfers between devices, exchange(): return lax.all_to_all(x, BOTH, split_axis=0, concat_axis=0, tiled=True)  12.3 us
    all_to_all x2, waiting for transfers between devices, exchange(): return lax.all_to_all(x, BOTH, split_axis=0, concat_axis=0, tiled=True)  9.47 us
    pallas_call x1, Pallas kernels, atm_forward(): pl.pallas_call(functools.partial(atm_kernel, chunks), out_shape=(jax.Shap...  7.29 us
    pallas_call x1, Pallas kernels, atm_back(): pl.pallas_call(back_kernel, grid=(tiles // per,), out_shape=jax.ShapeDtyp...  5.39 us
    ppermute x1, starting transfers between devices, per_device(): lax.ppermute(high_row, 'sec', shift('sec', 1))  4.55 us
    pallas_call x1, Pallas kernels, ocean_step(): pl.pallas_call(functools.partial(ocean_kernel, depth), out_shape=(jax.Sha...  3.29 us
    pallas_call x1, Pallas kernels, regrid_back(): pl.pallas_call(regrid_kernel, out_shape=jax.ShapeDtypeStruct((tiles, FIEL...  3.27 us
    ppermute x1, starting transfers between devices, per_device(): lax.ppermute(high_col, 'tile', shift('tile', 1))  3.03 us
  transfers between devices with their start and end apart: 6, of which 3 were waited for; matrix products, arithmetic and copies ran while one was open for 0% of the time, Pallas kernels for 16%

profile of v2, /device:TPU:0, one launch (start us, length us, event | category | flops | bytes accessed | tf_op | source)
XLA Modules:
  0.0 56.2 jit_solution(13084587429908456705)
XLA Ops:
  0.7 7.3 %atm_forward.1 = (f32[4,32,64,128]{3,2,1,0:T(8,128)}, f32[32,64,128]{2,1,0:T(8,128)}, f32[1344,128]{1,0:T(8,128)}, s32[64]{0:T(128)}) custom-call(f32[4,4,64,8,128]{4,3,2,1,0:T(8,128)} %bitcast.27, f32[4,64,8,128]{3,2,1,0:T(8,128)} %bitcast.29, f32[256,128]{1,0:T(8,128)} %bitcast.32, f32[10,12]{1,0:T(8,128)} %mix_ref.1, s32[64]{0:T(128)} %bitcast.34, ...), custom_call_target="tpu_custom_call" | custom-call | tf_op jit(solution)/shard_map/atm_forward/pallas_call | solution.py:204
  8.0 7.3 %all-to-all-start = ((f32[32,21,2,128]{3,2,1,0:T(2,128)}), f32[32,21,2,128]{3,2,1,0:T(2,128)S(1)}, u32[]{:S(2)}, u32[]{:S(2)}) async-start(f32[32,21,2,128]{3,2,1,0:T(2,128)} %bitcast.31), calls=%async_computation | async-start | bytes 1376256 | tf_op jit(solution)/shard_map/all_to_all | solution.py:513
  15.3 0.4 ocean_edges.1
  15.7 1.3 %collective-permute-start.2 = (f32[64,128]{1,0:T(8,128)S(1)}, f32[64,128]{1,0:T(8,128)S(1)}, u32[]{:S(2)}, u32[]{:S(2)}) collective-permute-start(f32[64,128]{1,0:T(8,128)S(1)} %get-tuple-element.26), channel_id=1, source_target_pairs={{1,0},{2,1},{3,2},{4,3},{5,4},{6,5},{7,6},{9,8},{10,9},{11,10},{12... | collective-permute-start | bytes 98312 | tf_op jit(solution)/shard_map/ppermute | solution.py:560
  17.0 3.0 %collective-permute-start.3 = (f32[64,128]{1,0:T(8,128)S(1)}, f32[64,128]{1,0:T(8,128)S(1)}, u32[]{:S(2)}, u32[]{:S(2)}) collective-permute-start(f32[64,128]{1,0:T(8,128)S(1)} %get-tuple-element.27), channel_id=1, source_target_pairs={{0,1},{1,2},{2,3},{3,4},{4,5},{5,6},{6,7},{8,9},{9,10},{10,11},{11... | collective-permute-start | bytes 98312 | tf_op jit(solution)/shard_map/ppermute | solution.py:561
  20.0 1.3 %collective-permute-start = (f32[40,128]{1,0:T(8,128)S(1)}, f32[40,128]{1,0:T(8,128)S(1)}, u32[]{:S(2)}, u32[]{:S(2)}) collective-permute-start(f32[40,128]{1,0:T(8,128)S(1)} %get-tuple-element.24), channel_id=1, source_target_pairs={{8,0},{16,8},{24,16},{9,1},{17,9},{25,17},{10,2},{18,10},{26,18},{... | collective-permute-start | bytes 61448 | tf_op jit(solution)/shard_map/ppermute | solution.py:558
  21.3 4.5 %collective-permute-start.1 = (f32[40,128]{1,0:T(8,128)S(1)}, f32[40,128]{1,0:T(8,128)S(1)}, u32[]{:S(2)}, u32[]{:S(2)}) collective-permute-start(f32[40,128]{1,0:T(8,128)S(1)} %get-tuple-element.25), channel_id=1, source_target_pairs={{0,8},{8,16},{16,24},{1,9},{9,17},{17,25},{2,10},{10,18},{18,26},{... | collective-permute-start | bytes 61448 | tf_op jit(solution)/shard_map/ppermute | solution.py:559
  25.9 0.0 collective-permute-done.east_ref
  25.9 1.5 %collective-permute-done.1.west_ref = f32[40,128]{1,0:T(8,128)S(1)} collective-permute-done((f32[40,128]{1,0:T(8,128)S(1)}, f32[40,128]{1,0:T(8,128)S(1)}, u32[]{:S(2)}, u32[]{:S(2)}) %collective-permute-start.1) | collective-permute-done | bytes 20512 | tf_op jit(solution)/shard_map/ppermute | solution.py:559
  27.3 0.0 collective-permute-done.2.north_ref
  27.3 0.0 collective-permute-done.3.south_ref
  27.3 0.0 copy-done.3
  27.3 3.3 %ocean_step.1 = (f32[32,64,128]{2,1,0:T(8,128)}, f32[4,64,128]{2,1,0:T(8,128)S(1)}, f32[10,64,128]{2,1,0:T(8,128)S(1)}) custom-call(f32[32,64,128]{2,1,0:T(8,128)S(1)} %bitcast.24, s32[64,128]{1,0:T(8,128)S(1)} %copy-done.2, f32[40,128]{1,0:T(8,128)S(1)} %collective-permute-done.east_ref, f32[40,128]{1,0:T(8,128)S(1)} %collective-permute-done.1.west_ref, ...), custom_call_target="tpu_custom_call" | custom-call | flops 7864320 | bytes 2097152 | tf_op jit(solution)/shard_map/ocean_step/pallas_call | solution.py:390
  30.6 4.5 %all-to-all-done = f32[32,21,2,128]{3,2,1,0:T(2,128)S(1)} async-done(((f32[32,21,2,128]{3,2,1,0:T(2,128)}), f32[32,21,2,128]{3,2,1,0:T(2,128)S(1)}, u32[]{:S(2)}, u32[]{:S(2)}) %all-to-all-start) | async-done | bytes 688160 | tf_op jit(solution)/shard_map/all_to_all | solution.py:513
  35.1 2.3 %ocean_combine.1 = (f32[32,64,128]{2,1,0:T(8,128)}, f32[32,16,128]{2,1,0:T(8,128)}) custom-call(f32[1344,128]{1,0:T(8,128)S(1)} %bitcast.25, f32[10,64,128]{2,1,0:T(8,128)S(1)} %get-tuple-element.28.bulk_ref, f32[4,64,128]{2,1,0:T(8,128)S(1)} %get-tuple-element.29.surf_ref, s32[64,128]{1,0:T(8,128)S(1)} %copy-done.2, ...), custom_call_target="tpu_custom_call", output_to_operand_aliasing={{0}: (5, {})} | custom-call | tf_op jit(solution)/shard_map/ocean_combine/pallas_call | solution.py:458
  37.5 5.0 %all-to-all-start.1 = ((f32[32,16,128]{2,1,0:T(8,128)}), f32[32,16,128]{2,1,0:T(8,128)S(1)}, u32[]{:S(2)}, u32[]{:S(2)}) async-start(f32[32,16,128]{2,1,0:T(8,128)} %get-tuple-element.37), calls=%async_computation.1 | async-start | bytes 524288 | tf_op jit(solution)/shard_map/all_to_all | solution.py:513
  42.5 0.0 copy-start
  42.5 0.0 copy-start.4
  42.5 0.0 copy-start.5
  42.5 5.4 %atm_back.1 = f32[4,4,64,8,128]{4,3,2,1,0:T(8,128)} custom-call(f32[4,32,64,128]{3,2,1,0:T(8,128)} %get-tuple-element.34.y_ref, f32[32,64,128]{2,1,0:T(8,128)} %get-tuple-element.35.e_ref), custom_call_target="tpu_custom_call" | custom-call | flops 2097152 | bytes 9437184 | tf_op jit(solution)/shard_map/atm_back/pallas_call | solution.py:270
  47.9 5.0 %all-to-all-done.1 = f32[32,16,128]{2,1,0:T(8,128)S(1)} async-done(((f32[32,16,128]{2,1,0:T(8,128)}), f32[32,16,128]{2,1,0:T(8,128)S(1)}, u32[]{:S(2)}, u32[]{:S(2)}) %all-to-all-start.1) | async-done | bytes 262176 | tf_op jit(solution)/shard_map/all_to_all | solution.py:513
  52.9 0.0 copy-done
  52.9 0.0 copy-done.5
  52.9 3.3 %regrid_back.1 = f32[64,4,128]{2,1,0:T(4,128)} custom-call(f32[512,128]{1,0:T(8,128)S(1)} %bitcast.26, bf16[64,128,128]{2,1,0:T(8,128)(2,1)S(1)} %copy-done, s32[64]{0:T(128)S(1)} %copy-done.5, s32[64]{0:T(128)S(1)} %copy-done.4), custom_call_target="tpu_custom_call" | custom-call | tf_op jit(solution)/shard_map/regrid_back/pallas_call | solution.py:502
  (6 shorter events, 0.0 us)
Async XLA Ops:
  0.6 14.6 %copy-start.1 = (f32[4,8,64,128]{3,2,1,0:T(8,128)S(1)}, f32[4,8,64,128]{3,2,1,0:T(8,128)}, u32[]{:S(2)}) copy-start(f32[4,8,64,128]{3,2,1,0:T(8,128)} %param.19) | copy-start | bytes 3145732
  0.6 14.6 %copy-start.2 = (s32[64,128]{1,0:T(8,128)S(1)}, s32[64,128]{1,0:T(8,128)}, u32[]{:S(2)}) copy-start(s32[64,128]{1,0:T(8,128)} %m_ref.5) | copy-start | bytes 98308
  0.7 26.7 %copy-start.3 = (f32[4,10]{1,0:T(4,128)S(1)}, f32[4,10]{1,0:T(4,128)}, u32[]{:S(2)}) copy-start(f32[4,10]{1,0:T(4,128)} %resp_ref.3) | copy-start | bytes 484
  8.0 27.2 %all-to-all-start = ((f32[32,21,2,128]{3,2,1,0:T(2,128)}), f32[32,21,2,128]{3,2,1,0:T(2,128)S(1)}, u32[]{:S(2)}, u32[]{:S(2)}) async-start(f32[32,21,2,128]{3,2,1,0:T(2,128)} %bitcast.31), calls=%async_computation | async-start | bytes 1376256 | tf_op jit(solution)/shard_map/all_to_all | solution.py:513
  15.7 11.7 %collective-permute-start.2 = (f32[64,128]{1,0:T(8,128)S(1)}, f32[64,128]{1,0:T(8,128)S(1)}, u32[]{:S(2)}, u32[]{:S(2)}) collective-permute-start(f32[64,128]{1,0:T(8,128)S(1)} %get-tuple-element.26), channel_id=1, source_target_pairs={{1,0},{2,1},{3,2},{4,3},{5,4},{6,5},{7,6},{9,8},{10,9},{11,10},{12... | collective-permute-start | bytes 98312 | tf_op jit(solution)/shard_map/ppermute | solution.py:560
  17.0 10.4 %collective-permute-start.3 = (f32[64,128]{1,0:T(8,128)S(1)}, f32[64,128]{1,0:T(8,128)S(1)}, u32[]{:S(2)}, u32[]{:S(2)}) collective-permute-start(f32[64,128]{1,0:T(8,128)S(1)} %get-tuple-element.27), channel_id=1, source_target_pairs={{0,1},{1,2},{2,3},{3,4},{4,5},{5,6},{6,7},{8,9},{9,10},{10,11},{11... | collective-permute-start | bytes 98312 | tf_op jit(solution)/shard_map/ppermute | solution.py:561
  20.0 5.9 %collective-permute-start = (f32[40,128]{1,0:T(8,128)S(1)}, f32[40,128]{1,0:T(8,128)S(1)}, u32[]{:S(2)}, u32[]{:S(2)}) collective-permute-start(f32[40,128]{1,0:T(8,128)S(1)} %get-tuple-element.24), channel_id=1, source_target_pairs={{8,0},{16,8},{24,16},{9,1},{17,9},{25,17},{10,2},{18,10},{26,18},{... | collective-permute-start | bytes 61448 | tf_op jit(solution)/shard_map/ppermute | solution.py:558
  21.3 6.0 %collective-permute-start.1 = (f32[40,128]{1,0:T(8,128)S(1)}, f32[40,128]{1,0:T(8,128)S(1)}, u32[]{:S(2)}, u32[]{:S(2)}) collective-permute-start(f32[40,128]{1,0:T(8,128)S(1)} %get-tuple-element.25), channel_id=1, source_target_pairs={{0,8},{8,16},{16,24},{1,9},{9,17},{17,25},{2,10},{10,18},{18,26},{... | collective-permute-start | bytes 61448 | tf_op jit(solution)/shard_map/ppermute | solution.py:559
  37.5 15.4 %all-to-all-start.1 = ((f32[32,16,128]{2,1,0:T(8,128)}), f32[32,16,128]{2,1,0:T(8,128)S(1)}, u32[]{:S(2)}, u32[]{:S(2)}) async-start(f32[32,16,128]{2,1,0:T(8,128)} %get-tuple-element.37), calls=%async_computation.1 | async-start | bytes 524288 | tf_op jit(solution)/shard_map/all_to_all | solution.py:513
  42.5 10.4 %copy-start = (bf16[64,128,128]{2,1,0:T(8,128)(2,1)S(1)}, bf16[64,128,128]{2,1,0:T(8,128)(2,1)}, u32[]{:S(2)}) copy-start(bf16[64,128,128]{2,1,0:T(8,128)(2,1)} %w_ref.3) | copy-start | bytes 6291460
  42.5 10.4 %copy-start.4 = (s32[64]{0:T(128)S(1)}, s32[64]{0:T(128)}, u32[]{:S(2)}) copy-start(s32[64]{0:T(128)} %tile_ref.3) | copy-start | bytes 772
  42.5 10.4 %copy-start.5 = (s32[64]{0:T(128)S(1)}, s32[64]{0:T(128)}, u32[]{:S(2)}) copy-start(s32[64]{0:T(128)} %get-tuple-element.38.slot_ref) | copy-start | bytes 772

commit v3 on v2

--- a/solution.py
+++ b/solution.py
@@ -276,7 +276,7 @@
             pl.BlockSpec((levels, per, LANES), lambda i: (0, i, 0)),
         ],
         out_specs=pl.BlockSpec((FIELDS, blocks, per, SUB, LANES), lambda i: (0, 0, i, 0, 0)),
-        compiler_params=params(56),
+        compiler_params=params(16),
         cost_estimate=pl.CostEstimate(
             flops=2 * y.size, bytes_accessed=9 * y.size, transcendentals=0
         ),
@@ -314,7 +314,7 @@
         out_shape=(row, row, col, col),
         in_specs=[spec_vmem(), spec_vmem()],
         out_specs=(spec_vmem(),) * 4,
-        compiler_params=params(32),
+        compiler_params=params(8),
         cost_estimate=pl.CostEstimate(flops=q.size, bytes_accessed=4 * q.size, transcendentals=0),
         name="ocean_edges",
     )(q, mask)
@@ -327,37 +327,48 @@
     return [(i + 1, i) for i in range(count - 1)]
 
 
-def ocean_kernel(
-    depth,
-    q_ref,
-    m_ref,
-    east_ref,
-    west_ref,
-    north_ref,
-    south_ref,
-    resp_ref,
-    out_ref,
-    surf_ref,
-    bulk_ref,
-):
+def bulk_kernel(q_ref, resp_ref, bulk_ref):
+    depth = q_ref.shape[0] // FIELDS
+    tops = [q_ref[v * depth] for v in range(FIELDS)]
+    for f in range(FLUXES):
+        total = resp_ref[0, f] * tops[0]
+        for v in range(1, FIELDS):
+            total = total + resp_ref[v, f] * tops[v]
+        bulk_ref[f] = 1.0 + 0.5 * jnp.tanh(total)
+
+
+def ocean_bulk(q, response):
+    return pl.pallas_call(
+        bulk_kernel,
+        out_shape=jax.ShapeDtypeStruct((FLUXES,) + q.shape[1:], F32),
+        in_specs=[spec_vmem(), spec_smem()],
+        out_specs=spec_vmem(),
+        compiler_params=params(8),
+        cost_estimate=pl.CostEstimate(
+            flops=3 * q.size, bytes_accessed=2 * q.size, transcendentals=q.size // 3
+        ),
+        name="ocean_bulk",
+    )(q, response)
+
+
+def stencil(levels, q_ref, m_ref, east_ref, west_ref, north_ref, south_ref, save):
     fields, rows, _ = q_ref.shape
+    depth = fields // FIELDS
     lane = lax.broadcasted_iota(jnp.int32, (rows, LANES), 1)
     last, first = lane == LANES - 1, lane == 0
 
-    def south_at(i):
-        return (i + LANES - 1) % LANES
-
     def around(cells, i):
+        high = (i + LANES - 1) % LANES
         east = jnp.concatenate([cells[1:], east_ref[i : i + 1, :]], axis=0)
         west = jnp.concatenate([west_ref[i : i + 1, :], cells[:-1]], axis=0)
         north = jnp.where(last, north_ref[:, i : i + 1], pltpu.roll(cells, LANES - 1, 1))
-        south = jnp.where(first, south_ref[:, south_at(i) : south_at(i) + 1], pltpu.roll(cells, 1, 1))
+        south = jnp.where(first, south_ref[:, high : high + 1], pltpu.roll(cells, 1, 1))
         return east, west, north, south
 
     mask = m_ref[...].astype(F32)
     m_east, m_west, m_north, m_south = around(mask, fields)
     m_all = m_east + m_west + m_north + m_south
-    for level in range(depth):
+    for level in levels:
         zonal = q_ref[2 * depth + level]
         merid = q_ref[3 * depth + level]
         for v in range(FIELDS):
@@ -372,40 +383,56 @@
                 tend = tend + CORIOLIS * merid
             if v == 3:
                 tend = tend - CORIOLIS * zonal
-            value = mask * (cells + OCEAN_DT * tend)
-            out_ref[i] = value
-            if level == 0:
-                surf_ref[v] = value
-
-    tops = [q_ref[v * depth] for v in range(FIELDS)]
-    for f in range(FLUXES):
-        total = resp_ref[0, f] * tops[0]
-        for v in range(1, FIELDS):
-            total = total + resp_ref[v, f] * tops[v]
-        bulk_ref[f] = 1.0 + 0.5 * jnp.tanh(total)
-
-
-def ocean_step(q, mask, edges, response, depth):
-    rows = q.shape[1]
-    return pl.pallas_call(
-        functools.partial(ocean_kernel, depth),
-        out_shape=(
-            jax.ShapeDtypeStruct(q.shape, F32),
-            jax.ShapeDtypeStruct((FIELDS, rows, LANES), F32),
-            jax.ShapeDtypeStruct((FLUXES, rows, LANES), F32),
-        ),
-        in_specs=[spec_vmem()] * 6 + [spec_smem()],
-        out_specs=(spec_vmem(),) * 3,
-        compiler_params=params(32),
+            save(v, level, mask * (cells + OCEAN_DT * tend))
+
+
+def top_kernel(q_ref, m_ref, east_ref, west_ref, north_ref, south_ref, surf_ref):
+    def save(v, level, value):
+        surf_ref[v] = value
+
+    stencil((0,), q_ref, m_ref, east_ref, west_ref, north_ref, south_ref, save)
+
+
+def ocean_top(q, mask, edges):
+    return pl.pallas_call(
+        top_kernel,
+        out_shape=jax.ShapeDtypeStruct((FIELDS,) + q.shape[1:], F32),
+        in_specs=[spec_vmem()] * 6,
+        out_specs=spec_vmem(),
+        compiler_params=params(8),
+        cost_estimate=pl.CostEstimate(flops=4 * q.size, bytes_accessed=q.size, transcendentals=0),
+        name="ocean_top",
+    )(q, mask, *edges)
+
+
+def deep_kernel(q_ref, m_ref, east_ref, west_ref, north_ref, south_ref, top_ref, out_ref):
+    depth = q_ref.shape[0] // FIELDS
+
+    def save(v, level, value):
+        out_ref[v * depth + level] = value
+
+    for v in range(FIELDS):
+        out_ref[v * depth] = top_ref[v]
+    levels = range(1, depth)
+    stencil(levels, q_ref, m_ref, east_ref, west_ref, north_ref, south_ref, save)
+
+
+def ocean_deep(q, mask, edges, top):
+    return pl.pallas_call(
+        deep_kernel,
+        out_shape=jax.ShapeDtypeStruct(q.shape, F32),
+        in_specs=[spec_vmem()] * 7,
+        out_specs=spec_vmem(),
+        compiler_params=params(8),
         cost_estimate=pl.CostEstimate(
             flops=30 * q.size, bytes_accessed=8 * q.size, transcendentals=0
         ),
-        name="ocean_step",
-    )(q, mask, *edges, response)
+        name="ocean_deep",
+    )(q, mask, *edges, top)
 
 
 def combine_kernel(
-    depth, got_ref, bulk_ref, surf_ref, m_ref, resp_ref, q_ref, out_ref, back_ref, top, sems
+    got_ref, bulk_ref, surf_ref, m_ref, resp_ref, top, back_ref
 ):
     rows = m_ref.shape[0]
     sources = back_ref.shape[0]
@@ -439,38 +466,29 @@
     mask = m_ref[...].astype(F32)
     for g in range(FIELDS):
         top[g] = surf_ref[g] + mask * force[g]
-    copies = [
-        pltpu.make_async_copy(top.at[g], out_ref.at[g * depth], sems.at[g]) for g in range(FIELDS)
-    ]
-    for copy in copies:
-        copy.start()
     hot_t = jnp.concatenate([jnp.transpose(h).astype(BF16) for h in hots], axis=0)
     for j in range(FIELDS // 2):
         pair = jnp.concatenate([top[2 * j], top[2 * j + 1]], axis=0)
         high, low = halves(pair)
         both = dot32(hot_t, high) + dot32(hot_t, low)
         back_ref[:, j * SUB : (j + 1) * SUB, :] = both.reshape(sources, SUB, LANES)
-    for copy in copies:
-        copy.wait()
-
-
-def ocean_combine(got, bulk, surf, mask, response, q_next, depth, sources):
-    return pl.pallas_call(
-        functools.partial(combine_kernel, depth),
+
+
+def ocean_combine(got, bulk, surf, mask, response, sources):
+    return pl.pallas_call(
+        combine_kernel,
         out_shape=(
-            jax.ShapeDtypeStruct(q_next.shape, F32),
+            jax.ShapeDtypeStruct(surf.shape, F32),
             jax.ShapeDtypeStruct((sources, FIELDS * CAP, LANES), F32),
         ),
-        in_specs=[spec_vmem()] * 4 + [spec_smem(), spec_any()],
-        out_specs=(spec_any(), spec_vmem()),
-        scratch_shapes=[
-            pltpu.VMEM(surf.shape, F32),
-            pltpu.SemaphoreType.DMA((FIELDS,)),
-        ],
-        input_output_aliases={5: 0},
-        compiler_params=params(32),
+        in_specs=[spec_vmem()] * 4 + [spec_smem()],
+        out_specs=(spec_vmem(), spec_vmem()),
+        compiler_params=params(16),
+        cost_estimate=pl.CostEstimate(
+            flops=4 * got.size, bytes_accessed=4 * got.size, transcendentals=0
+        ),
         name="ocean_combine",
-    )(got, bulk, surf, mask, response, q_next)
+    )(got, bulk, surf, mask, response)
 
 
 def regrid_kernel(got_ref, w_ref, slot_ref, tile_ref, out_ref):
@@ -504,7 +522,7 @@
         out_shape=jax.ShapeDtypeStruct((tiles, FIELDS, LANES), F32),
         in_specs=[spec_vmem(), spec_vmem(), spec_smem(), spec_smem()],
         out_specs=spec_vmem(),
-        compiler_params=params(32),
+        compiler_params=params(16),
         name="regrid_back",
     )(got, weights, slots, tile_ids)
 
@@ -560,14 +578,13 @@
         lax.ppermute(low_col, "tile", shift("tile", -1)),
         lax.ppermute(high_col, "tile", shift("tile", 1)),
     )
-    q_base, surf, bulk = ocean_step(q, land_mask, edges, flux_response, depth)
-
-    q_next, returning = ocean_combine(
-        incoming, bulk, surf, land_mask, flux_response, q_base, depth, devices
-    )
-    returning, y, e = lax.optimization_barrier((returning, y, e))
+    bulk = ocean_bulk(q, flux_response)
+    surf = ocean_top(q, land_mask, edges)
+    atm_next = atm_back(y, e).transpose(0, 1, 3, 2, 4).reshape(FIELDS, levels, columns)
+
+    top, returning = ocean_combine(incoming, bulk, surf, land_mask, flux_response, devices)
     arrived = exchange(returning)
-    atm_next = atm_back(y, e).transpose(0, 1, 3, 2, 4).reshape(FIELDS, levels, columns)
+    q_next = ocean_deep(q, land_mask, edges, top)
     back = regrid_back(
         arrived.reshape(devices * FIELDS * CAP, LANES), regrid_blocks, slots, entry_tile, tiles
     )

time: 56.5 us -> 53.7 us (0.950)
  local copies, waits for them, and re-layouts: 0.03 us -> 3.44 us
  Pallas kernels: 21.9 us -> 19.2 us
  starting transfers between devices: 22.5 us -> 20 us
  waiting for transfers between devices: 10.9 us -> 9.77 us
    unnamed x12 -> x20, local copies, waits for them, and re-layouts: 0.03 us -> 3.44 us
    all_to_all x2, starting transfers between devices: 12.3 us -> 9.88 us  [exchange(): return lax.all_to_all(x, BOTH, split_axis=0, concat_axis=0, tiled=True)]
    pallas_call x1, Pallas kernels: 5.39 us -> 3.13 us  [atm_back(): pl.pallas_call(back_kernel, grid=(tiles // per,), out_shape=jax.ShapeDtyp...]
    ppermute x1, waiting for transfers between devices: 1.45 us -> 0.75 us  [per_device(): lax.ppermute(high_row, 'sec', shift('sec', 1))]
    pallas_call x2 -> x4, Pallas kernels: 5.6 us -> 5.13 us  [the longest x1 2.34 us: ocean_deep(): pl.pallas_call(deep_kernel, out_shape=jax.ShapeDtypeStruct(q.shape, F32),...]
  transfers between devices with their start and end apart: 6 -> 6, of which waited for: 3 -> 3; matrix products, arithmetic and copies ran while one was open for 0% -> 0% of each run, Pallas kernels for 16% -> 13%
where the time goes in v3:
time: 53.7 us; the launch traced here: 53.2 us
  starting transfers between devices  20 us (37%)
  Pallas kernels  19.2 us (36%)
  waiting for transfers between devices  9.77 us (18%)
  local copies, waits for them, and re-layouts  3.44 us (6%)
  between operations  0.8 us (1%)
    all_to_all x2, starting transfers between devices, exchange(): return lax.all_to_all(x, BOTH, split_axis=0, concat_axis=0, tiled=True)  9.88 us
    all_to_all x2, waiting for transfers between devices, exchange(): return lax.all_to_all(x, BOTH, split_axis=0, concat_axis=0, tiled=True)  9.01 us
    pallas_call x1, Pallas kernels, atm_forward(): pl.pallas_call(functools.partial(atm_kernel, chunks), out_shape=(jax.Shap...  7.33 us
    ppermute x1, starting transfers between devices, per_device(): lax.ppermute(high_row, 'sec', shift('sec', 1))  4.55 us
    unnamed x20, local copies, waits for them, and re-layouts  3.44 us
    pallas_call x1, Pallas kernels, regrid_back(): pl.pallas_call(regrid_kernel, out_shape=jax.ShapeDtypeStruct((tiles, FIEL...  3.26 us
    pallas_call x1, Pallas kernels, atm_back(): pl.pallas_call(back_kernel, grid=(tiles // per,), out_shape=jax.ShapeDtyp...  3.13 us
    ppermute x1, starting transfers between devices, per_device(): lax.ppermute(high_col, 'tile', shift('tile', 1))  3.03 us
  transfers between devices with their start and end apart: 6, of which 3 were waited for; matrix products, arithmetic and copies ran while one was open for 0% of the time, Pallas kernels for 13%

profile of v3, /device:TPU:0, one launch (start us, length us, event | category | flops | bytes accessed | tf_op | source)
XLA Modules:
  0.0 53.2 jit_solution(18011433252252237645)
XLA Ops:
  0.6 0.0 copy-start
  0.7 7.3 %atm_forward.1 = (f32[4,32,64,128]{3,2,1,0:T(8,128)}, f32[32,64,128]{2,1,0:T(8,128)}, f32[1344,128]{1,0:T(8,128)}, s32[64]{0:T(128)}) custom-call(f32[4,4,64,8,128]{4,3,2,1,0:T(8,128)} %bitcast.29, f32[4,64,8,128]{3,2,1,0:T(8,128)} %bitcast.31, f32[256,128]{1,0:T(8,128)} %bitcast.34, f32[10,12]{1,0:T(8,128)} %mix_ref.1, s32[64]{0:T(128)} %bitcast.36, ...), custom_call_target="tpu_custom_call" | custom-call | tf_op jit(solution)/shard_map/atm_forward/pallas_call | solution.py:204
  8.0 7.3 %all-to-all-start = ((f32[32,21,2,128]{3,2,1,0:T(2,128)}), f32[32,21,2,128]{3,2,1,0:T(2,128)S(1)}, u32[]{:S(2)}, u32[]{:S(2)}) async-start(f32[32,21,2,128]{3,2,1,0:T(2,128)} %bitcast.33), calls=%async_computation | async-start | bytes 1376256 | tf_op jit(solution)/shard_map/all_to_all | solution.py:531
  15.3 0.4 ocean_edges.1
  15.7 1.3 %collective-permute-start.2 = (f32[64,128]{1,0:T(8,128)S(1)}, f32[64,128]{1,0:T(8,128)S(1)}, u32[]{:S(2)}, u32[]{:S(2)}) collective-permute-start(f32[64,128]{1,0:T(8,128)S(1)} %get-tuple-element.21), channel_id=1, source_target_pairs={{1,0},{2,1},{3,2},{4,3},{5,4},{6,5},{7,6},{9,8},{10,9},{11,10},{12... | collective-permute-start | bytes 98312 | tf_op jit(solution)/shard_map/ppermute | solution.py:578
  17.0 3.0 %collective-permute-start.3 = (f32[64,128]{1,0:T(8,128)S(1)}, f32[64,128]{1,0:T(8,128)S(1)}, u32[]{:S(2)}, u32[]{:S(2)}) collective-permute-start(f32[64,128]{1,0:T(8,128)S(1)} %get-tuple-element.22), channel_id=1, source_target_pairs={{0,1},{1,2},{2,3},{3,4},{4,5},{5,6},{6,7},{8,9},{9,10},{10,11},{11... | collective-permute-start | bytes 98312 | tf_op jit(solution)/shard_map/ppermute | solution.py:579
  20.0 1.3 %collective-permute-start = (f32[40,128]{1,0:T(8,128)S(1)}, f32[40,128]{1,0:T(8,128)S(1)}, u32[]{:S(2)}, u32[]{:S(2)}) collective-permute-start(f32[40,128]{1,0:T(8,128)S(1)} %get-tuple-element.19), channel_id=1, source_target_pairs={{8,0},{16,8},{24,16},{9,1},{17,9},{25,17},{10,2},{18,10},{26,18},{... | collective-permute-start | bytes 61448 | tf_op jit(solution)/shard_map/ppermute | solution.py:576
  21.3 4.5 %collective-permute-start.1 = (f32[40,128]{1,0:T(8,128)S(1)}, f32[40,128]{1,0:T(8,128)S(1)}, u32[]{:S(2)}, u32[]{:S(2)}) collective-permute-start(f32[40,128]{1,0:T(8,128)S(1)} %get-tuple-element.20), channel_id=1, source_target_pairs={{0,8},{8,16},{16,24},{1,9},{9,17},{17,25},{2,10},{10,18},{18,26},{... | collective-permute-start | bytes 61448 | tf_op jit(solution)/shard_map/ppermute | solution.py:577
  25.9 0.7 %ocean_bulk.1.bulk_ref = f32[10,64,128]{2,1,0:T(8,128)S(1)} custom-call(f32[32,64,128]{2,1,0:T(8,128)S(1)} %bitcast.24, f32[4,10]{1,0:T(4,128)S(1)} %copy-done.7), custom_call_target="tpu_custom_call" | custom-call | flops 786432 | bytes 524288 | tf_op jit(solution)/shard_map/ocean_bulk/pallas_call | solution.py:341
  26.6 0.0 collective-permute-done.east_ref
  26.6 0.7 %collective-permute-done.1.west_ref = f32[40,128]{1,0:T(8,128)S(1)} collective-permute-done((f32[40,128]{1,0:T(8,128)S(1)}, f32[40,128]{1,0:T(8,128)S(1)}, u32[]{:S(2)}, u32[]{:S(2)}) %collective-permute-start.1) | collective-permute-done | bytes 20512 | tf_op jit(solution)/shard_map/ppermute | solution.py:577
  27.4 0.0 collective-permute-done.2.north_ref
  27.4 0.0 collective-permute-done.3.south_ref
  27.4 0.3 ocean_top.1.surf_ref
  27.6 7.5 %all-to-all-done = f32[32,21,2,128]{3,2,1,0:T(2,128)S(1)} async-done(((f32[32,21,2,128]{3,2,1,0:T(2,128)}), f32[32,21,2,128]{3,2,1,0:T(2,128)S(1)}, u32[]{:S(2)}, u32[]{:S(2)}) %all-to-all-start) | async-done | bytes 688160 | tf_op jit(solution)/shard_map/all_to_all | solution.py:531
  35.2 1.8 %ocean_combine.1 = (f32[4,64,128]{2,1,0:T(8,128)S(1)}, f32[32,16,128]{2,1,0:T(8,128)}) custom-call(f32[1344,128]{1,0:T(8,128)S(1)} %bitcast.27, f32[10,64,128]{2,1,0:T(8,128)S(1)} %ocean_bulk.1.bulk_ref, f32[4,64,128]{2,1,0:T(8,128)S(1)} %ocean_top.1.surf_ref, s32[64,128]{1,0:T(8,128)S(1)} %copy-done.4, f32[4,10]{1,0:T(4,128)S(1)} %copy-done.7), custom_call_target="tpu_custom_call" | custom-call | flops 688128 | bytes 688128 | tf_op jit(solution)/shard_map/ocean_combine/pallas_call | solution.py:478
  37.0 2.6 %all-to-all-start.1 = ((f32[32,16,128]{2,1,0:T(8,128)}), f32[32,16,128]{2,1,0:T(8,128)S(1)}, u32[]{:S(2)}, u32[]{:S(2)}) async-start(f32[32,16,128]{2,1,0:T(8,128)} %get-tuple-element.25), calls=%async_computation.1 | async-start | bytes 524288 | tf_op jit(solution)/shard_map/all_to_all | solution.py:531
  39.6 0.0 copy-start.2
  39.6 2.2 %copy-done.2 = f32[4,32,64,128]{3,2,1,0:T(8,128)S(1)} copy-done((f32[4,32,64,128]{3,2,1,0:T(8,128)S(1)}, f32[4,32,64,128]{3,2,1,0:T(8,128)}, u32[]{:S(2)}) %copy-start.2) | copy-done | bytes 4194328
  41.8 1.2 %copy-done.3 = f32[32,64,128]{2,1,0:T(8,128)S(1)} copy-done((f32[32,64,128]{2,1,0:T(8,128)S(1)}, f32[32,64,128]{2,1,0:T(8,128)}, u32[]{:S(2)}) %copy-start.3) | copy-done | bytes 1048600
  43.0 3.1 %atm_back.1 = f32[4,4,64,8,128]{4,3,2,1,0:T(8,128)} custom-call(f32[4,32,64,128]{3,2,1,0:T(8,128)S(1)} %copy-done.2, f32[32,64,128]{2,1,0:T(8,128)S(1)} %copy-done.3), custom_call_target="tpu_custom_call" | custom-call | flops 2097152 | bytes 9437184 | tf_op jit(solution)/shard_map/atm_back/pallas_call | solution.py:270
  46.2 2.3 %ocean_deep.1 = f32[32,64,128]{2,1,0:T(8,128)} custom-call(f32[32,64,128]{2,1,0:T(8,128)S(1)} %bitcast.26, s32[64,128]{1,0:T(8,128)S(1)} %copy-done.4, f32[40,128]{1,0:T(8,128)S(1)} %collective-permute-done.east_ref, f32[40,128]{1,0:T(8,128)S(1)} %collective-permute-done.1.west_ref, f32[64,128]{1,0:T(8,128)S(1)} %collective-permute-done.2.north_ref, ...), custom_call_target="tpu_custom_call" | custom-call | flops 7864320 | bytes 2097152 | tf_op jit(solution)/shard_map/ocean_deep/pallas_call | solution.py:421
  48.5 1.5 %all-to-all-done.1 = f32[32,16,128]{2,1,0:T(8,128)S(1)} async-done(((f32[32,16,128]{2,1,0:T(8,128)}), f32[32,16,128]{2,1,0:T(8,128)S(1)}, u32[]{:S(2)}, u32[]{:S(2)}) %all-to-all-start.1) | async-done | bytes 262176 | tf_op jit(solution)/shard_map/all_to_all | solution.py:531
  50.0 3.3 %regrid_back.1 = f32[64,4,128]{2,1,0:T(4,128)} custom-call(f32[512,128]{1,0:T(8,128)S(1)} %bitcast.28, bf16[64,128,128]{2,1,0:T(8,128)(2,1)S(1)} %copy-done.1, s32[64]{0:T(128)S(1)} %copy-done.9, s32[64]{0:T(128)S(1)} %copy-done.8), custom_call_target="tpu_custom_call" | custom-call | tf_op jit(solution)/shard_map/regrid_back/pallas_call | solution.py:520
  (16 shorter events, 0.0 us)
Async XLA Ops:
  0.6 14.7 %copy-start = (f32[4,8,64,128]{3,2,1,0:T(8,128)S(1)}, f32[4,8,64,128]{3,2,1,0:T(8,128)}, u32[]{:S(2)}) copy-start(f32[4,8,64,128]{3,2,1,0:T(8,128)} %param.19) | copy-start | bytes 3145732
  0.6 14.7 %copy-start.4 = (s32[64,128]{1,0:T(8,128)S(1)}, s32[64,128]{1,0:T(8,128)}, u32[]{:S(2)}) copy-start(s32[64,128]{1,0:T(8,128)} %m_ref.7) | copy-start | bytes 98308
  0.7 25.2 %copy-start.7 = (f32[4,10]{1,0:T(4,128)S(1)}, f32[4,10]{1,0:T(4,128)}, u32[]{:S(2)}) copy-start(f32[4,10]{1,0:T(4,128)} %resp_ref.3) | copy-start | bytes 484
  8.0 27.2 %all-to-all-start = ((f32[32,21,2,128]{3,2,1,0:T(2,128)}), f32[32,21,2,128]{3,2,1,0:T(2,128)S(1)}, u32[]{:S(2)}, u32[]{:S(2)}) async-start(f32[32,21,2,128]{3,2,1,0:T(2,128)} %bitcast.33), calls=%async_computation | async-start | bytes 1376256 | tf_op jit(solution)/shard_map/all_to_all | solution.py:531
  15.7 11.7 %collective-permute-start.2 = (f32[64,128]{1,0:T(8,128)S(1)}, f32[64,128]{1,0:T(8,128)S(1)}, u32[]{:S(2)}, u32[]{:S(2)}) collective-permute-start(f32[64,128]{1,0:T(8,128)S(1)} %get-tuple-element.21), channel_id=1, source_target_pairs={{1,0},{2,1},{3,2},{4,3},{5,4},{6,5},{7,6},{9,8},{10,9},{11,10},{12... | collective-permute-start | bytes 98312 | tf_op jit(solution)/shard_map/ppermute | solution.py:578
  17.0 10.4 %collective-permute-start.3 = (f32[64,128]{1,0:T(8,128)S(1)}, f32[64,128]{1,0:T(8,128)S(1)}, u32[]{:S(2)}, u32[]{:S(2)}) collective-permute-start(f32[64,128]{1,0:T(8,128)S(1)} %get-tuple-element.22), channel_id=1, source_target_pairs={{0,1},{1,2},{2,3},{3,4},{4,5},{5,6},{6,7},{8,9},{9,10},{10,11},{11... | collective-permute-start | bytes 98312 | tf_op jit(solution)/shard_map/ppermute | solution.py:579
  20.0 6.6 %collective-permute-start = (f32[40,128]{1,0:T(8,128)S(1)}, f32[40,128]{1,0:T(8,128)S(1)}, u32[]{:S(2)}, u32[]{:S(2)}) collective-permute-start(f32[40,128]{1,0:T(8,128)S(1)} %get-tuple-element.19), channel_id=1, source_target_pairs={{8,0},{16,8},{24,16},{9,1},{17,9},{25,17},{10,2},{18,10},{26,18},{... | collective-permute-start | bytes 61448 | tf_op jit(solution)/shard_map/ppermute | solution.py:576
  21.3 6.0 %collective-permute-start.1 = (f32[40,128]{1,0:T(8,128)S(1)}, f32[40,128]{1,0:T(8,128)S(1)}, u32[]{:S(2)}, u32[]{:S(2)}) collective-permute-start(f32[40,128]{1,0:T(8,128)S(1)} %get-tuple-element.20), channel_id=1, source_target_pairs={{0,8},{8,16},{16,24},{1,9},{9,17},{17,25},{2,10},{10,18},{18,26},{... | collective-permute-start | bytes 61448 | tf_op jit(solution)/shard_map/ppermute | solution.py:577
  37.0 2.6 %copy-start.5 = (f32[4,64,128]{2,1,0:T(8,128)}, f32[4,64,128]{2,1,0:T(8,128)S(1)}, u32[]{:S(2)}) copy-start(f32[4,64,128]{2,1,0:T(8,128)S(1)} %get-tuple-element.24.top_ref) | copy-start | bytes 393220
  37.0 13.0 %all-to-all-start.1 = ((f32[32,16,128]{2,1,0:T(8,128)}), f32[32,16,128]{2,1,0:T(8,128)S(1)}, u32[]{:S(2)}, u32[]{:S(2)}) async-start(f32[32,16,128]{2,1,0:T(8,128)} %get-tuple-element.25), calls=%async_computation.1 | async-start | bytes 524288 | tf_op jit(solution)/shard_map/all_to_all | solution.py:531
  39.6 2.2 %copy-start.2 = (f32[4,32,64,128]{3,2,1,0:T(8,128)S(1)}, f32[4,32,64,128]{3,2,1,0:T(8,128)}, u32[]{:S(2)}) copy-start(f32[4,32,64,128]{3,2,1,0:T(8,128)} %get-tuple-element.15.y_ref) | copy-start | bytes 12582916
  41.8 1.2 %copy-start.3 = (f32[32,64,128]{2,1,0:T(8,128)S(1)}, f32[32,64,128]{2,1,0:T(8,128)}, u32[]{:S(2)}) copy-start(f32[32,64,128]{2,1,0:T(8,128)} %get-tuple-element.16.e_ref) | copy-start | bytes 3145732
  43.0 3.1 %copy-start.6 = (f32[4,64,128]{2,1,0:T(8,128)S(1)}, f32[4,64,128]{2,1,0:T(8,128)}, u32[]{:S(2)}) copy-start(f32[4,64,128]{2,1,0:T(8,128)} %copy-done.5) | copy-start | bytes 393220
  43.0 7.0 %copy-start.1 = (bf16[64,128,128]{2,1,0:T(8,128)(2,1)S(1)}, bf16[64,128,128]{2,1,0:T(8,128)(2,1)}, u32[]{:S(2)}) copy-start(bf16[64,128,128]{2,1,0:T(8,128)(2,1)} %w_ref.3) | copy-start | bytes 6291460
  43.0 7.0 %copy-start.8 = (s32[64]{0:T(128)S(1)}, s32[64]{0:T(128)}, u32[]{:S(2)}) copy-start(s32[64]{0:T(128)} %tile_ref.3) | copy-start | bytes 772
  43.0 7.0 %copy-start.9 = (s32[64]{0:T(128)S(1)}, s32[64]{0:T(128)}, u32[]{:S(2)}) copy-start(s32[64]{0:T(128)} %get-tuple-element.26.slot_ref) | copy-start | bytes 772

commit v4 on v3

--- a/solution.py
+++ b/solution.py
@@ -46,20 +46,47 @@
     return pltpu.CompilerParams(vmem_limit_bytes=mib * 2**20)
 
 
+def eliminate(a_rows, d_rows, surface, tiles, blocks, first, groups, keep):
+    def block(step, carry):
+        lb = blocks - 1 - step
+        bottom = jnp.where(lb == 0, 1.0, 0.0).astype(F32)
+        carry = list(carry)
+        for r in range(SUB - 1, -1, -1):
+            for g in range(groups):
+                tile = first + g * SUB
+                grow, above, ys = carry[g]
+                coup = d_rows[pl.ds((lb * tiles + tile) * SUB + r, SUB, stride=SUB), :]
+                weight = 1.0 + above * grow
+                inverse = 1.0 / (weight + coup)
+                solved = []
+                for v in range(FIELDS):
+                    row = ((v * blocks + lb) * tiles + tile) * SUB + r
+                    rhs = a_rows[pl.ds(row, SUB, stride=SUB), :]
+                    if r == 0:
+                        rhs = rhs + coup * (surface(v, tile) * bottom)
+                    solved.append((rhs + above * ys[v]) * inverse)
+                keep(lb, r, tile, coup * inverse, solved)
+                carry[g] = (weight * inverse, coup, tuple(solved))
+        return tuple(carry)
+
+    zero = jnp.zeros((SUB, LANES), F32)
+    start = tuple((zero, zero, (zero,) * FIELDS) for _ in range(groups))
+    final = lax.fori_loop(0, blocks, block, start)
+    return [(coup, x0) for _, coup, x0 in final]
+
+
 def atm_kernel(
     chunks,
+    chunk_rows,
     a_ref,
     d_ref,
     s_ref,
-    mix_ref,
-    dest_ref,
-    tile_ref,
-    row_ref,
+    mix_hbm,
+    dest_hbm,
+    tile_hbm,
+    row_hbm,
     w_ref,
-    y_ref,
-    e_ref,
-    out_ref,
-    slot_ref,
+    out_hbm,
     a_buf,
     d_buf,
     s_buf,
@@ -67,19 +94,20 @@
     y_buf,
     e_buf,
     flux,
+    out_ref,
+    mix_ref,
+    dest_ref,
+    tile_ref,
+    row_ref,
     count,
     in_sems,
-    out_sems,
-    s_sem,
-    w_sem,
+    sems,
 ):
     blocks, tiles = a_buf.shape[1], a_buf.shape[2]
-    levels = blocks * SUB
     entries = w_buf.shape[0]
     per = tiles // chunks
     groups = per // SUB
     devices = count.shape[0]
-    chunk_rows = out_ref.shape[0] // devices
     table_rows = chunk_rows - FLUXES * CAP
     me = lax.axis_index("sec") * lax.axis_size("tile") + lax.axis_index("tile")
 
@@ -89,22 +117,27 @@
     def loads(ci):
         at = pl.ds(ci * per, per)
         return (
-            pltpu.make_async_copy(a_ref.at[:, :, at], a_buf.at[:, :, at], in_sems.at[ci, 0]),
-            pltpu.make_async_copy(d_ref.at[:, at], d_buf.at[:, at], in_sems.at[ci, 1]),
+            pltpu.make_async_copy(d_ref.at[:, at], d_buf.at[:, at], in_sems.at[ci, 0]),
+            pltpu.make_async_copy(a_ref.at[:, :, at], a_buf.at[:, :, at], in_sems.at[ci, 1]),
         )
 
-    def saves(ci):
-        at = pl.ds(ci * per, per)
-        return (
-            pltpu.make_async_copy(y_buf.at[:, :, at], y_ref.at[:, :, at], out_sems.at[ci, 0]),
-            pltpu.make_async_copy(e_buf.at[:, at], e_ref.at[:, at], out_sems.at[ci, 1]),
+    small = [
+        pltpu.make_async_copy(src, dst, sems.at[i])
+        for i, (src, dst) in enumerate(
+            (
+                (s_ref, s_buf),
+                (mix_hbm, mix_ref),
+                (dest_hbm, dest_ref),
+                (tile_hbm, tile_ref),
+                (row_hbm, row_ref),
+            )
         )
-
-    s_copy = pltpu.make_async_copy(s_ref, s_buf, s_sem)
-    w_copy = pltpu.make_async_copy(w_ref, w_buf, w_sem)
+    ]
+    w_copy = pltpu.make_async_copy(w_ref, w_buf, sems.at[5])
     for copy in loads(0):
         copy.start()
-    s_copy.start()
+    for copy in small:
+        copy.start()
     for ci in range(1, chunks):
         for copy in loads(ci):
             copy.start()
@@ -112,51 +145,29 @@
 
     a_rows = a_buf.reshape(FIELDS * blocks * tiles * SUB, LANES)
     d_rows = d_buf.reshape(blocks * tiles * SUB, LANES)
-    s_copy.wait()
     for d in range(devices):
         count[d] = 0
     out_ref[...] = jnp.zeros_like(out_ref)
+    for copy in small:
+        copy.wait()
+
+    def keep(lb, r, tile, coef, solved):
+        if r == 1:
+            e_buf[pl.ds(tile, SUB), :] = coef
+            for v in range(FIELDS):
+                y_buf[v, pl.ds(tile, SUB), :] = solved[v]
 
     def chunk(ci, _):
         for copy in loads(ci):
             copy.wait()
         first = ci * per
-
-        def block(step, carry):
-            lb = blocks - 1 - step
-            bottom = jnp.where(lb == 0, 1.0, 0.0).astype(F32)
-            carry = list(carry)
-            for r in range(SUB - 1, -1, -1):
-                for g in range(groups):
-                    tile = first + g * SUB
-                    grow, above, ys = carry[g]
-                    coup = d_rows[pl.ds((lb * tiles + tile) * SUB + r, SUB, stride=SUB), :]
-                    weight = 1.0 + above * grow
-                    inverse = 1.0 / (weight + coup)
-                    solved = []
-                    for v in range(FIELDS):
-                        row = ((v * blocks + lb) * tiles + tile) * SUB + r
-                        rhs = a_rows[pl.ds(row, SUB, stride=SUB), :]
-                        if r == 0:
-                            rhs = rhs + coup * (surface(v, tile) * bottom)
-                        value = (rhs + above * ys[v]) * inverse
-                        y_buf[v, lb * SUB + r, pl.ds(tile, SUB), :] = value
-                        solved.append(value)
-                    e_buf[lb * SUB + r, pl.ds(tile, SUB), :] = coup * inverse
-                    carry[g] = (weight * inverse, coup, tuple(solved))
-            return tuple(carry)
-
-        zero = jnp.zeros((SUB, LANES), F32)
-        start = tuple((zero, zero, (zero,) * FIELDS) for _ in range(groups))
-        final = lax.fori_loop(0, blocks, block, start)
-        for copy in saves(ci):
-            copy.start()
+        final = eliminate(a_rows, d_rows, surface, tiles, blocks, first, groups, keep)
         for g in range(groups):
             tile = first + g * SUB
-            _, coup, x0 = final[g]
-            e1 = e_buf[1, pl.ds(tile, SUB), :]
+            coup, x0 = final[g]
+            e1 = e_buf[pl.ds(tile, SUB), :]
             turb = [coup * (surface(v, tile) - x0[v]) for v in range(FIELDS)]
-            x1 = [y_buf[v, 1, pl.ds(tile, SUB), :] + e1 * x0[v] for v in range(FIELDS)]
+            x1 = [y_buf[v, pl.ds(tile, SUB), :] + e1 * x0[v] for v in range(FIELDS)]
             feats = turb + list(x0) + [turb[v] * x1[v] for v in range(FIELDS)]
             for f in range(FLUXES):
                 total = mix_ref[f, 0] * feats[0]
@@ -175,7 +186,6 @@
         d = dest_ref[e]
         k = count[d]
         count[d] = k + 1
-        slot_ref[e] = d * (FIELDS * CAP) + k
         here = me * (2 * CAP) + k
         hit = (spot == here) | (spot == here + CAP)
         table = pl.ds(d * chunk_rows + FLUXES * CAP, table_rows)
@@ -189,70 +199,72 @@
         out_ref[pl.ds(row + SUB * CAP, FLUXES - SUB, stride=CAP), :] = both[SUB:FLUXES]
         return 0
 
-    lax.fori_loop(0, entries, entry, 0, unroll=8)
-    for ci in range(chunks):
-        for copy in saves(ci):
-            copy.wait()
+    lax.fori_loop(0, entries, entry, 0, unroll=min(entries, 64))
+    out_copy = pltpu.make_async_copy(out_ref, out_hbm, sems.at[6])
+    out_copy.start()
+    out_copy.wait()
 
 
 def atm_forward(a_tiles, d_tiles, s_rows, mix, dest, tile_ids, row_ids, weights, devices):
-    _, blocks, tiles, _, _ = a_tiles.shape
-    levels = blocks * SUB
+    _, _, tiles, _, _ = a_tiles.shape
     entries = weights.shape[0]
-    chunks = 2
+    chunks = 4
     chunk_rows = FLUXES * CAP + devices * 2 * CAP // LANES
-    return pl.pallas_call(
-        functools.partial(atm_kernel, chunks),
-        out_shape=(
-            jax.ShapeDtypeStruct((FIELDS, levels, tiles, LANES), F32),
-            jax.ShapeDtypeStruct((levels, tiles, LANES), F32),
-            jax.ShapeDtypeStruct((devices * chunk_rows, LANES), F32),
-            jax.ShapeDtypeStruct((entries,), jnp.int32),
-        ),
-        in_specs=[
-            spec_any(),
-            spec_any(),
-            spec_any(),
-            spec_smem(),
-            spec_smem(),
-            spec_smem(),
-            spec_smem(),
-            spec_any(),
-        ],
-        out_specs=(spec_any(), spec_any(), spec_vmem(), spec_smem()),
+    out_shape = (devices * chunk_rows, LANES)
+    return pl.pallas_call(
+        functools.partial(atm_kernel, chunks, chunk_rows),
+        out_shape=jax.ShapeDtypeStruct(out_shape, F32),
+        in_specs=[spec_any()] * 8,
+        out_specs=spec_any(),
         scratch_shapes=[
             pltpu.VMEM(a_tiles.shape, F32),
             pltpu.VMEM(d_tiles.shape, F32),
             pltpu.VMEM(s_rows.shape, F32),
             pltpu.VMEM(weights.shape, BF16),
-            pltpu.VMEM((FIELDS, levels, tiles, LANES), F32),
-            pltpu.VMEM((levels, tiles, LANES), F32),
+            pltpu.VMEM((FIELDS, tiles, LANES), F32),
+            pltpu.VMEM((tiles, LANES), F32),
             pltpu.VMEM((tiles * 16, LANES), F32),
+            pltpu.VMEM(out_shape, F32),
+            pltpu.SMEM(mix.shape, F32),
+            pltpu.SMEM((entries,), jnp.int32),
+            pltpu.SMEM((entries,), jnp.int32),
+            pltpu.SMEM((entries,), jnp.int32),
             pltpu.SMEM((devices,), jnp.int32),
             pltpu.SemaphoreType.DMA((chunks, 2)),
-            pltpu.SemaphoreType.DMA((chunks, 2)),
-            pltpu.SemaphoreType.DMA,
-            pltpu.SemaphoreType.DMA,
+            pltpu.SemaphoreType.DMA((7,)),
         ],
         compiler_params=params(60),
         name="atm_forward",
     )(a_tiles, d_tiles, s_rows, mix, dest, tile_ids, row_ids, weights)
 
 
-def back_kernel(y_ref, e_ref, out_ref):
+def solve_kernel(a_ref, d_ref, s_ref, out_ref, y_buf, e_buf):
     blocks, tiles = out_ref.shape[1], out_ref.shape[2]
+    a_rows = a_ref.reshape(FIELDS * blocks * tiles * SUB, LANES)
+    d_rows = d_ref.reshape(blocks * tiles * SUB, LANES)
     rows = out_ref.reshape(FIELDS * blocks * tiles * SUB, LANES)
     groups = tiles // SUB
+
+    def surface(v, tile):
+        return s_ref[pl.ds(tile * FIELDS + v, SUB, stride=FIELDS), :]
+
+    def keep(lb, r, tile, coef, solved):
+        level = lb * SUB + r
+        e_buf[level, pl.ds(tile, SUB), :] = coef
+        for v in range(FIELDS):
+            y_buf[v, level, pl.ds(tile, SUB), :] = solved[v]
+
+    eliminate(a_rows, d_rows, surface, tiles, blocks, 0, groups, keep)
 
     def block(lb, carry):
         carry = list(carry)
         for r in range(SUB):
             for g in range(groups):
-                coef = e_ref[lb * SUB + r, pl.ds(g * SUB, SUB), :]
+                coef = e_buf[lb * SUB + r, pl.ds(g * SUB, SUB), :]
                 if r == 0:
                     coef = coef * jnp.where(lb == 0, 0.0, 1.0).astype(F32)
                 for v in range(FIELDS):
-                    x = y_ref[v, lb * SUB + r, pl.ds(g * SUB, SUB), :]
+                    x = y_buf[v, lb * SUB + r, pl.ds(g * SUB, SUB), :]
                     x = x + coef * carry[g * FIELDS + v]
                     row = ((v * blocks + lb) * tiles + g * SUB) * SUB + r
                     rows[pl.ds(row, SUB, stride=SUB), :] = x
@@ -263,25 +275,30 @@
     lax.fori_loop(0, blocks, block, (zero,) * (groups * FIELDS))
 
 
-def atm_back(y, e):
-    _, levels, tiles, _ = y.shape
-    blocks = levels // SUB
+def atm_solve(a_tiles, d_tiles, s_rows):
+    _, blocks, tiles, _, _ = a_tiles.shape
+    levels = blocks * SUB
     per = 16
     return pl.pallas_call(
-        back_kernel,
+        solve_kernel,
         grid=(tiles // per,),
-        out_shape=jax.ShapeDtypeStruct((FIELDS, blocks, tiles, SUB, LANES), F32),
+        out_shape=jax.ShapeDtypeStruct(a_tiles.shape, F32),
         in_specs=[
-            pl.BlockSpec((FIELDS, levels, per, LANES), lambda i: (0, 0, i, 0)),
-            pl.BlockSpec((levels, per, LANES), lambda i: (0, i, 0)),
+            pl.BlockSpec((FIELDS, blocks, per, SUB, LANES), lambda i: (0, 0, i, 0, 0)),
+            pl.BlockSpec((blocks, per, SUB, LANES), lambda i: (0, i, 0, 0)),
+            pl.BlockSpec((per * FIELDS, LANES), lambda i: (i, 0)),
         ],
         out_specs=pl.BlockSpec((FIELDS, blocks, per, SUB, LANES), lambda i: (0, 0, i, 0, 0)),
-        compiler_params=params(16),
+        scratch_shapes=[
+            pltpu.VMEM((FIELDS, levels, per, LANES), F32),
+            pltpu.VMEM((levels, per, LANES), F32),
+        ],
+        compiler_params=params(60),
         cost_estimate=pl.CostEstimate(
-            flops=2 * y.size, bytes_accessed=9 * y.size, transcendentals=0
-        ),
-        name="atm_back",
-    )(y, e)
+            flops=8 * a_tiles.size, bytes_accessed=9 * a_tiles.size, transcendentals=0
+        ),
+        name="atm_solve",
+    )(a_tiles, d_tiles, s_rows)
 
 
 def edge_kernel(q_ref, m_ref, low_row, high_row, low_col, high_col):
@@ -327,8 +344,12 @@
     return [(i + 1, i) for i in range(count - 1)]
 
 
-def bulk_kernel(q_ref, resp_ref, bulk_ref):
+def bulk_kernel(q_ref, resp_ref, dest_ref, bulk_ref, rows_ref, slot_ref, count):
     depth = q_ref.shape[0] // FIELDS
+    for g in range(FIELDS):
+        for f in range(FLUXES):
+            i = g * FLUXES + f
+            rows_ref[i : i + 1, :] = jnp.full((1, LANES), resp_ref[g, f], F32)
     tops = [q_ref[v * depth] for v in range(FIELDS)]
     for f in range(FLUXES):
         total = resp_ref[0, f] * tops[0]
@@ -336,19 +357,36 @@
             total = total + resp_ref[v, f] * tops[v]
         bulk_ref[f] = 1.0 + 0.5 * jnp.tanh(total)
 
-
-def ocean_bulk(q, response):
+    for d in range(count.shape[0]):
+        count[d] = 0
+
+    def entry(e, _):
+        d = dest_ref[e]
+        k = count[d]
+        count[d] = k + 1
+        slot_ref[e] = d * (FIELDS * CAP) + k
+        return 0
+
+    lax.fori_loop(0, dest_ref.shape[0], entry, 0)
+
+
+def ocean_bulk(q, response, dest, devices):
     return pl.pallas_call(
         bulk_kernel,
-        out_shape=jax.ShapeDtypeStruct((FLUXES,) + q.shape[1:], F32),
-        in_specs=[spec_vmem(), spec_smem()],
-        out_specs=spec_vmem(),
+        out_shape=(
+            jax.ShapeDtypeStruct((FLUXES,) + q.shape[1:], F32),
+            jax.ShapeDtypeStruct((FIELDS * FLUXES, LANES), F32),
+            jax.ShapeDtypeStruct(dest.shape, jnp.int32),
+        ),
+        in_specs=[spec_vmem(), spec_smem(), spec_smem()],
+        out_specs=(spec_vmem(), spec_vmem(), spec_smem()),
+        scratch_shapes=[pltpu.SMEM((devices,), jnp.int32)],
         compiler_params=params(8),
         cost_estimate=pl.CostEstimate(
             flops=3 * q.size, bytes_accessed=2 * q.size, transcendentals=q.size // 3
         ),
         name="ocean_bulk",
-    )(q, response)
+    )(q, response, dest)
 
 
 def stencil(levels, q_ref, m_ref, east_ref, west_ref, north_ref, south_ref, save):
@@ -461,7 +499,7 @@
             f = 2 * j + p
             drive = both[p * rows : (p + 1) * rows] * bulk_ref[f]
             for g in range(FIELDS):
-                term = resp_ref[g, f] * drive
+                term = resp_ref[g * FLUXES + f, :][None, :] * drive
                 force[g] = term if f == 0 else force[g] + term
     mask = m_ref[...].astype(F32)
     for g in range(FIELDS):
@@ -481,7 +519,7 @@
             jax.ShapeDtypeStruct(surf.shape, F32),
             jax.ShapeDtypeStruct((sources, FIELDS * CAP, LANES), F32),
         ),
-        in_specs=[spec_vmem()] * 4 + [spec_smem()],
+        in_specs=[spec_vmem()] * 5,
         out_specs=(spec_vmem(), spec_vmem()),
         compiler_params=params(16),
         cost_estimate=pl.CostEstimate(
@@ -491,9 +529,17 @@
     )(got, bulk, surf, mask, response)
 
 
-def regrid_kernel(got_ref, w_ref, slot_ref, tile_ref, out_ref):
+def regrid_kernel(got_ref, w_ref, slot_hbm, tile_hbm, out_ref, slot_ref, tile_ref, sems):
     entries = w_ref.shape[0]
+    copies = (
+        pltpu.make_async_copy(slot_hbm, slot_ref, sems.at[0]),
+        pltpu.make_async_copy(tile_hbm, tile_ref, sems.at[1]),
+    )
+    for copy in copies:
+        copy.start()
     out_ref[...] = jnp.zeros_like(out_ref)
+    for copy in copies:
+        copy.wait()
 
     def group(i, _):
         results = []
@@ -513,15 +559,20 @@
             out_ref[tile] = out_ref[tile] + value
         return 0
 
-    lax.fori_loop(0, entries // SUB, group, 0)
+    lax.fori_loop(0, entries // SUB, group, 0, unroll=min(entries // SUB, 8))
 
 
 def regrid_back(got, weights, slots, tile_ids, tiles):
     return pl.pallas_call(
         regrid_kernel,
         out_shape=jax.ShapeDtypeStruct((tiles, FIELDS, LANES), F32),
-        in_specs=[spec_vmem(), spec_vmem(), spec_smem(), spec_smem()],
+        in_specs=[spec_vmem(), spec_vmem(), spec_any(), spec_any()],
         out_specs=spec_vmem(),
+        scratch_shapes=[
+            pltpu.SMEM(slots.shape, jnp.int32),
+            pltpu.SMEM(slots.shape, jnp.int32),
+            pltpu.SemaphoreType.DMA((2,)),
+        ],
         compiler_params=params(16),
         name="regrid_back",
     )(got, weights, slots, tile_ids)
@@ -553,16 +604,9 @@
     d_tiles = diffusivity.reshape(blocks, SUB, tiles, LANES).transpose(0, 2, 1, 3)
     s_rows = surface_prev.reshape(FIELDS, tiles, LANES).transpose(1, 0, 2)
     s_rows = s_rows.reshape(tiles * FIELDS, LANES)
-    y, e, outgoing, slots = atm_forward(
-        a_tiles,
-        d_tiles,
-        s_rows,
-        flux_mix,
-        entry_dest[:, 0],
-        entry_tile,
-        entry_row,
-        regrid_blocks,
-        devices,
+    dest = entry_dest[:, 0]
+    outgoing = atm_forward(
+        a_tiles, d_tiles, s_rows, flux_mix, dest, entry_tile, entry_row, regrid_blocks, devices
     )
 
     q = ocean_state.reshape(FIELDS * depth, rows, LANES)
@@ -578,13 +622,15 @@
         lax.ppermute(low_col, "tile", shift("tile", -1)),
         lax.ppermute(high_col, "tile", shift("tile", 1)),
     )
-    bulk = ocean_bulk(q, flux_response)
+    bulk, resp_rows, slots = ocean_bulk(q, flux_response, dest, devices)
     surf = ocean_top(q, land_mask, edges)
-    atm_next = atm_back(y, e).transpose(0, 1, 3, 2, 4).reshape(FIELDS, levels, columns)
-
-    top, returning = ocean_combine(incoming, bulk, surf, land_mask, flux_response, devices)
+    top, returning = ocean_combine(incoming, bulk, surf, land_mask, resp_rows, devices)
     arrived = exchange(returning)
     q_next = ocean_deep(q, land_mask, edges, top)
+    q_next, a_tiles, d_tiles, s_rows = lax.optimization_barrier(
+        (q_next, a_tiles, d_tiles, s_rows)
+    )
+    atm_next = atm_solve(a_tiles, d_tiles, s_rows).transpose(0, 1, 3, 2, 4).reshape(FIELDS, levels, columns)
     back = regrid_back(
         arrived.reshape(devices * FIELDS * CAP, LANES), regrid_blocks, slots, entry_tile, tiles
     )

time: 53.7 us -> 49.9 us (0.929)
  local copies, waits for them, and re-layouts: 3.44 us -> 0.02 us
  waiting for transfers between devices: 9.77 us -> 8.97 us
    unnamed x20 -> x12, local copies, waits for them, and re-layouts: 3.44 us -> 0.02 us
    pallas_call x3, Pallas kernels: 11.1 us -> 13 us  [the longest x1 6.22 us: atm_solve(): pl.pallas_call(solve_kernel, grid=(tiles // per,), out_shape=jax.ShapeDty...]
    pallas_call x1, Pallas kernels: 3.26 us -> 2.44 us  [regrid_back(): pl.pallas_call(regrid_kernel, out_shape=jax.ShapeDtypeStruct((tiles, FIEL...]
    ppermute x1, waiting for transfers between devices: 0.75 us -> 0.01 us  [per_device(): lax.ppermute(high_row, 'sec', shift('sec', 1))]
    pallas_call x1, Pallas kernels: 1.82 us -> 1.25 us  [ocean_combine(): pl.pallas_call(combine_kernel, out_shape=(jax.ShapeDtypeStruct(surf.shape...]
  transfers between devices with their start and end apart: 6 -> 6, of which waited for: 3 -> 2; matrix products, arithmetic and copies ran while one was open for 0% -> 0% of each run, Pallas kernels for 13% -> 22%
where the time goes in v4:
time: 49.9 us; the launch traced here: 49.6 us
  starting transfers between devices  20 us (40%)
  Pallas kernels  19.7 us (39%)
  waiting for transfers between devices  8.97 us (18%)
  between operations  0.81 us (2%)
    all_to_all x2, starting transfers between devices, exchange(): return lax.all_to_all(x, BOTH, split_axis=0, concat_axis=0, tiled=True)  9.89 us
    all_to_all x2, waiting for transfers between devices, exchange(): return lax.all_to_all(x, BOTH, split_axis=0, concat_axis=0, tiled=True)  8.96 us
    pallas_call x1, Pallas kernels, atm_solve(): pl.pallas_call(solve_kernel, grid=(tiles // per,), out_shape=jax.ShapeDty...  6.22 us
    pallas_call x1, Pallas kernels, atm_forward(): pl.pallas_call(functools.partial(atm_kernel, chunks, chunk_rows), out_sha...  5.04 us
    ppermute x1, starting transfers between devices, per_device(): lax.ppermute(high_row, 'sec', shift('sec', 1))  4.55 us
    ppermute x1, starting transfers between devices, per_device(): lax.ppermute(high_col, 'tile', shift('tile', 1))  3.03 us
    pallas_call x1, Pallas kernels, regrid_back(): pl.pallas_call(regrid_kernel, out_shape=jax.ShapeDtypeStruct((tiles, FIEL...  2.44 us
    pallas_call x1, Pallas kernels, ocean_deep(): pl.pallas_call(deep_kernel, out_shape=jax.ShapeDtypeStruct(q.shape, F32),...  2.34 us
  transfers between devices with their start and end apart: 6, of which 2 were waited for; matrix products, arithmetic and copies ran while one was open for 0% of the time, Pallas kernels for 22%

profile of v4, /device:TPU:0, one launch (start us, length us, event | category | flops | bytes accessed | tf_op | source)
XLA Modules:
  0.0 49.6 jit_solution(6993036392742597111)
XLA Ops:
  0.6 0.0 copy-start
  0.6 0.0 copy-start.2
  0.7 0.0 copy-start.3
  0.7 5.0 %atm_forward.1 = f32[1344,128]{1,0:T(8,128)} custom-call(f32[4,4,64,8,128]{4,3,2,1,0:T(8,128)} %bitcast.31, f32[4,64,8,128]{3,2,1,0:T(8,128)} %bitcast.33, f32[256,128]{1,0:T(8,128)} %bitcast.38, f32[10,12]{1,0:T(8,128)} %mix_hbm.1, s32[64]{0:T(128)} %bitcast.29, s32[64]{0:T(128)} %tile_hbm.3, s32[64]{0:T(128)} %row_hbm.1, bf16[64,128,128]{2,1,0:T(8,128)(2,1)} %w_ref.3), custom_call_target="tpu_custom_call" | custom-call | tf_op jit(solution)/shard_map/atm_forward/pallas_call | solution.py:214
  5.7 7.3 %all-to-all-start = ((f32[32,21,2,128]{3,2,1,0:T(2,128)}), f32[32,21,2,128]{3,2,1,0:T(2,128)S(1)}, u32[]{:S(2)}, u32[]{:S(2)}) async-start(f32[32,21,2,128]{3,2,1,0:T(2,128)} %bitcast.36), calls=%async_computation | async-start | bytes 1376256 | tf_op jit(solution)/shard_map/all_to_all | solution.py:582
  13.0 0.4 ocean_edges.1
  13.4 1.3 %collective-permute-start.2 = (f32[64,128]{1,0:T(8,128)S(1)}, f32[64,128]{1,0:T(8,128)S(1)}, u32[]{:S(2)}, u32[]{:S(2)}) collective-permute-start(f32[64,128]{1,0:T(8,128)S(1)} %get-tuple-element.21), channel_id=1, source_target_pairs={{1,0},{2,1},{3,2},{4,3},{5,4},{6,5},{7,6},{9,8},{10,9},{11,10},{12... | collective-permute-start | bytes 98312 | tf_op jit(solution)/shard_map/ppermute | solution.py:622
  14.7 3.0 %collective-permute-start.3 = (f32[64,128]{1,0:T(8,128)S(1)}, f32[64,128]{1,0:T(8,128)S(1)}, u32[]{:S(2)}, u32[]{:S(2)}) collective-permute-start(f32[64,128]{1,0:T(8,128)S(1)} %get-tuple-element.22), channel_id=1, source_target_pairs={{0,1},{1,2},{2,3},{3,4},{4,5},{5,6},{6,7},{8,9},{9,10},{10,11},{11... | collective-permute-start | bytes 98312 | tf_op jit(solution)/shard_map/ppermute | solution.py:623
  17.7 1.3 %collective-permute-start = (f32[40,128]{1,0:T(8,128)S(1)}, f32[40,128]{1,0:T(8,128)S(1)}, u32[]{:S(2)}, u32[]{:S(2)}) collective-permute-start(f32[40,128]{1,0:T(8,128)S(1)} %get-tuple-element.19), channel_id=1, source_target_pairs={{8,0},{16,8},{24,16},{9,1},{17,9},{25,17},{10,2},{18,10},{26,18},{... | collective-permute-start | bytes 61448 | tf_op jit(solution)/shard_map/ppermute | solution.py:620
  19.0 4.5 %collective-permute-start.1 = (f32[40,128]{1,0:T(8,128)S(1)}, f32[40,128]{1,0:T(8,128)S(1)}, u32[]{:S(2)}, u32[]{:S(2)}) collective-permute-start(f32[40,128]{1,0:T(8,128)S(1)} %get-tuple-element.20), channel_id=1, source_target_pairs={{0,8},{8,16},{16,24},{1,9},{9,17},{17,25},{2,10},{10,18},{18,26},{... | collective-permute-start | bytes 61448 | tf_op jit(solution)/shard_map/ppermute | solution.py:621
  23.6 1.8 %ocean_bulk.1 = (f32[10,64,128]{2,1,0:T(8,128)S(1)}, f32[40,128]{1,0:T(8,128)S(1)}, s32[64]{0:T(128)S(1)}) custom-call(f32[32,64,128]{2,1,0:T(8,128)S(1)} %bitcast.24, f32[4,10]{1,0:T(4,128)S(1)} %copy-done.3, s32[64]{0:T(128)S(1)} %bitcast.30), custom_call_target="tpu_custom_call" | custom-call | flops 786432 | bytes 524288 | tf_op jit(solution)/shard_map/ocean_bulk/pallas_call | solution.py:374
  25.4 0.0 collective-permute-done.east_ref
  25.4 0.0 collective-permute-done.1.west_ref
  25.4 0.0 collective-permute-done.2.north_ref
  25.5 0.0 collective-permute-done.3.south_ref
  25.5 0.3 ocean_top.1.surf_ref
  25.7 7.1 %all-to-all-done = f32[32,21,2,128]{3,2,1,0:T(2,128)S(1)} async-done(((f32[32,21,2,128]{3,2,1,0:T(2,128)}), f32[32,21,2,128]{3,2,1,0:T(2,128)S(1)}, u32[]{:S(2)}, u32[]{:S(2)}) %all-to-all-start) | async-done | bytes 688160 | tf_op jit(solution)/shard_map/all_to_all | solution.py:582
  32.9 1.3 %ocean_combine.1 = (f32[4,64,128]{2,1,0:T(8,128)S(1)}, f32[32,16,128]{2,1,0:T(8,128)}) custom-call(f32[1344,128]{1,0:T(8,128)S(1)} %bitcast.27, f32[10,64,128]{2,1,0:T(8,128)S(1)} %get-tuple-element.24.bulk_ref, f32[4,64,128]{2,1,0:T(8,128)S(1)} %ocean_top.1.surf_ref, s32[64,128]{1,0:T(8,128)S(1)} %copy-done.2, f32[40,128]{1,0:T(8,128)S(1)} %get-tuple-element.25.resp_ref), custom_call_target="tpu_custom_call" | custom-call | flops 688128 | bytes 688128 | tf_op jit(solution)/shard_map/ocean_combine/pallas_call | solution.py:516
  34.1 2.6 %all-to-all-start.1 = ((f32[32,16,128]{2,1,0:T(8,128)}), f32[32,16,128]{2,1,0:T(8,128)S(1)}, u32[]{:S(2)}, u32[]{:S(2)}) async-start(f32[32,16,128]{2,1,0:T(8,128)} %get-tuple-element.31), calls=%async_computation.1 | async-start | bytes 524288 | tf_op jit(solution)/shard_map/all_to_all | solution.py:582
  36.7 2.3 %ocean_deep.1 = f32[32,64,128]{2,1,0:T(8,128)} custom-call(f32[32,64,128]{2,1,0:T(8,128)S(1)} %bitcast.26, s32[64,128]{1,0:T(8,128)S(1)} %copy-done.2, f32[40,128]{1,0:T(8,128)S(1)} %collective-permute-done.east_ref, f32[40,128]{1,0:T(8,128)S(1)} %collective-permute-done.1.west_ref, f32[64,128]{1,0:T(8,128)S(1)} %collective-permute-done.2.north_ref, ...), custom_call_target="tpu_custom_call" | custom-call | flops 7864320 | bytes 2097152 | tf_op jit(solution)/shard_map/ocean_deep/pallas_call | solution.py:459
  39.1 6.2 %atm_solve.1 = f32[4,4,64,8,128]{4,3,2,1,0:T(8,128)} custom-call(f32[4,4,64,8,128]{4,3,2,1,0:T(8,128)} %bitcast.32, f32[4,64,8,128]{3,2,1,0:T(8,128)} %bitcast.34, f32[256,128]{1,0:T(8,128)} %bitcast.39), custom_call_target="tpu_custom_call" | custom-call | flops 8388608 | bytes 9437184 | tf_op jit(solution)/shard_map/atm_solve/pallas_call | solution.py:282
  45.3 1.8 %all-to-all-done.1 = f32[32,16,128]{2,1,0:T(8,128)S(1)} async-done(((f32[32,16,128]{2,1,0:T(8,128)}), f32[32,16,128]{2,1,0:T(8,128)S(1)}, u32[]{:S(2)}, u32[]{:S(2)}) %all-to-all-start.1) | async-done | bytes 262176 | tf_op jit(solution)/shard_map/all_to_all | solution.py:582
  47.1 0.0 copy-done.5
  47.1 2.4 %regrid_back.1 = f32[64,4,128]{2,1,0:T(4,128)} custom-call(f32[512,128]{1,0:T(8,128)S(1)} %bitcast.28, bf16[64,128,128]{2,1,0:T(8,128)(2,1)S(1)} %copy-done.1, s32[64]{0:T(128)S(1)} %get-tuple-element.32.slot_hbm, s32[64]{0:T(128)S(1)} %copy-done.5), custom_call_target="tpu_custom_call" | custom-call | tf_op jit(solution)/shard_map/regrid_back/pallas_call | solution.py:566
  (8 shorter events, 0.0 us)
Async XLA Ops:
  0.6 12.4 %copy-start = (f32[4,8,64,128]{3,2,1,0:T(8,128)S(1)}, f32[4,8,64,128]{3,2,1,0:T(8,128)}, u32[]{:S(2)}) copy-start(f32[4,8,64,128]{3,2,1,0:T(8,128)} %param.19) | copy-start | bytes 3145732
  0.6 12.4 %copy-start.2 = (s32[64,128]{1,0:T(8,128)S(1)}, s32[64,128]{1,0:T(8,128)}, u32[]{:S(2)}) copy-start(s32[64,128]{1,0:T(8,128)} %m_ref.7) | copy-start | bytes 98308
  0.7 23.0 %copy-start.3 = (f32[4,10]{1,0:T(4,128)S(1)}, f32[4,10]{1,0:T(4,128)}, u32[]{:S(2)}) copy-start(f32[4,10]{1,0:T(4,128)} %resp_ref.1) | copy-start | bytes 484
  0.7 23.0 %copy-start.4 = (s32[64,1]{0,1:T(1,128)S(1)}, s32[64,1]{0,1:T(1,128)}, u32[]{:S(2)}) copy-start(s32[64,1]{0,1:T(1,128)} %param.15) | copy-start | bytes 772
  5.7 27.2 %all-to-all-start = ((f32[32,21,2,128]{3,2,1,0:T(2,128)}), f32[32,21,2,128]{3,2,1,0:T(2,128)S(1)}, u32[]{:S(2)}, u32[]{:S(2)}) async-start(f32[32,21,2,128]{3,2,1,0:T(2,128)} %bitcast.36), calls=%async_computation | async-start | bytes 1376256 | tf_op jit(solution)/shard_map/all_to_all | solution.py:582
  13.4 12.0 %collective-permute-start.2 = (f32[64,128]{1,0:T(8,128)S(1)}, f32[64,128]{1,0:T(8,128)S(1)}, u32[]{:S(2)}, u32[]{:S(2)}) collective-permute-start(f32[64,128]{1,0:T(8,128)S(1)} %get-tuple-element.21), channel_id=1, source_target_pairs={{1,0},{2,1},{3,2},{4,3},{5,4},{6,5},{7,6},{9,8},{10,9},{11,10},{12... | collective-permute-start | bytes 98312 | tf_op jit(solution)/shard_map/ppermute | solution.py:622
  14.7 10.7 %collective-permute-start.3 = (f32[64,128]{1,0:T(8,128)S(1)}, f32[64,128]{1,0:T(8,128)S(1)}, u32[]{:S(2)}, u32[]{:S(2)}) collective-permute-start(f32[64,128]{1,0:T(8,128)S(1)} %get-tuple-element.22), channel_id=1, source_target_pairs={{0,1},{1,2},{2,3},{3,4},{4,5},{5,6},{6,7},{8,9},{9,10},{10,11},{11... | collective-permute-start | bytes 98312 | tf_op jit(solution)/shard_map/ppermute | solution.py:623
  17.7 7.7 %collective-permute-start = (f32[40,128]{1,0:T(8,128)S(1)}, f32[40,128]{1,0:T(8,128)S(1)}, u32[]{:S(2)}, u32[]{:S(2)}) collective-permute-start(f32[40,128]{1,0:T(8,128)S(1)} %get-tuple-element.19), channel_id=1, source_target_pairs={{8,0},{16,8},{24,16},{9,1},{17,9},{25,17},{10,2},{18,10},{26,18},{... | collective-permute-start | bytes 61448 | tf_op jit(solution)/shard_map/ppermute | solution.py:620
  19.0 6.4 %collective-permute-start.1 = (f32[40,128]{1,0:T(8,128)S(1)}, f32[40,128]{1,0:T(8,128)S(1)}, u32[]{:S(2)}, u32[]{:S(2)}) collective-permute-start(f32[40,128]{1,0:T(8,128)S(1)} %get-tuple-element.20), channel_id=1, source_target_pairs={{0,8},{8,16},{16,24},{1,9},{9,17},{17,25},{2,10},{10,18},{18,26},{... | collective-permute-start | bytes 61448 | tf_op jit(solution)/shard_map/ppermute | solution.py:621
  34.1 13.0 %all-to-all-start.1 = ((f32[32,16,128]{2,1,0:T(8,128)}), f32[32,16,128]{2,1,0:T(8,128)S(1)}, u32[]{:S(2)}, u32[]{:S(2)}) async-start(f32[32,16,128]{2,1,0:T(8,128)} %get-tuple-element.31), calls=%async_computation.1 | async-start | bytes 524288 | tf_op jit(solution)/shard_map/all_to_all | solution.py:582
  39.1 8.0 %copy-start.1 = (bf16[64,128,128]{2,1,0:T(8,128)(2,1)S(1)}, bf16[64,128,128]{2,1,0:T(8,128)(2,1)}, u32[]{:S(2)}) copy-start(bf16[64,128,128]{2,1,0:T(8,128)(2,1)} %w_ref.3) | copy-start | bytes 6291460
  39.1 8.0 %copy-start.5 = (s32[64]{0:T(128)S(1)}, s32[64]{0:T(128)}, u32[]{:S(2)}) copy-start(s32[64]{0:T(128)} %tile_hbm.3) | copy-start | bytes 772

commit v5 on v4

--- a/solution.py
+++ b/solution.py
@@ -344,7 +344,7 @@
     return [(i + 1, i) for i in range(count - 1)]
 
 
-def bulk_kernel(q_ref, resp_ref, dest_ref, bulk_ref, rows_ref, slot_ref, count):
+def bulk_kernel(q_ref, resp_ref, dest_ref, bulk_ref, rows_ref, pick_ref, wide, count):
     depth = q_ref.shape[0] // FIELDS
     for g in range(FIELDS):
         for f in range(FLUXES):
@@ -357,6 +357,8 @@
             total = total + resp_ref[v, f] * tops[v]
         bulk_ref[f] = 1.0 + 0.5 * jnp.tanh(total)
 
+    entries = dest_ref.shape[0]
+    lane = lax.broadcasted_iota(jnp.int32, (1, wide.shape[1]), 1)
     for d in range(count.shape[0]):
         count[d] = 0
 
@@ -364,23 +366,27 @@
         d = dest_ref[e]
         k = count[d]
         count[d] = k + 1
-        slot_ref[e] = d * (FIELDS * CAP) + k
+        for p in range(2):
+            here = d * (2 * CAP) + p * CAP + k
+            wide[pl.ds(p * entries + e, 1), :] = (lane == here).astype(F32)
         return 0
 
-    lax.fori_loop(0, dest_ref.shape[0], entry, 0)
+    lax.fori_loop(0, entries, entry, 0, unroll=4)
+    pick_ref[...] = wide[...].astype(BF16)
 
 
 def ocean_bulk(q, response, dest, devices):
+    picks = (2 * dest.shape[0], devices * 2 * CAP)
     return pl.pallas_call(
         bulk_kernel,
         out_shape=(
             jax.ShapeDtypeStruct((FLUXES,) + q.shape[1:], F32),
             jax.ShapeDtypeStruct((FIELDS * FLUXES, LANES), F32),
-            jax.ShapeDtypeStruct(dest.shape, jnp.int32),
+            jax.ShapeDtypeStruct(picks, BF16),
         ),
         in_specs=[spec_vmem(), spec_smem(), spec_smem()],
-        out_specs=(spec_vmem(), spec_vmem(), spec_smem()),
-        scratch_shapes=[pltpu.SMEM((devices,), jnp.int32)],
+        out_specs=(spec_vmem(),) * 3,
+        scratch_shapes=[pltpu.VMEM(picks, F32), pltpu.SMEM((devices,), jnp.int32)],
         compiler_params=params(8),
         cost_estimate=pl.CostEstimate(
             flops=3 * q.size, bytes_accessed=2 * q.size, transcendentals=q.size // 3
@@ -529,31 +535,49 @@
     )(got, bulk, surf, mask, response)
 
 
-def regrid_kernel(got_ref, w_ref, slot_hbm, tile_hbm, out_ref, slot_ref, tile_ref, sems):
+def turn_kernel(w_ref, out_ref):
+    for e in range(w_ref.shape[0]):
+        out_ref[e] = jnp.transpose(w_ref[e])
+
+
+def turn_blocks(weights):
+    entries = weights.shape[0]
+    per = 32
+    spec = pl.BlockSpec((per,) + weights.shape[1:], lambda i: (i, 0, 0))
+    return pl.pallas_call(
+        turn_kernel,
+        grid=(entries // per,),
+        out_shape=jax.ShapeDtypeStruct(weights.shape, BF16),
+        in_specs=[spec],
+        out_specs=spec,
+        compiler_params=params(58),
+        cost_estimate=pl.CostEstimate(
+            flops=weights.size, bytes_accessed=4 * weights.size, transcendentals=0
+        ),
+        name="turn_blocks",
+    )(weights)
+
+
+def regrid_kernel(got_ref, pick_ref, w_ref, tile_hbm, out_ref, parts, tile_ref, sem):
     entries = w_ref.shape[0]
-    copies = (
-        pltpu.make_async_copy(slot_hbm, slot_ref, sems.at[0]),
-        pltpu.make_async_copy(tile_hbm, tile_ref, sems.at[1]),
-    )
-    for copy in copies:
-        copy.start()
+    rows = got_ref.shape[0] * SUB
+    copy = pltpu.make_async_copy(tile_hbm, tile_ref, sem)
+    copy.start()
     out_ref[...] = jnp.zeros_like(out_ref)
-    for copy in copies:
-        copy.wait()
+    pick = pick_ref[...]
+    for j in range(FIELDS // 2):
+        data = got_ref[:, j * SUB : (j + 1) * SUB, :].reshape(rows, LANES)
+        for h, half in enumerate(halves(data)):
+            at = (h * FIELDS + 2 * j) * entries
+            parts[at : at + 2 * entries, :] = dot32(pick, half)
+    copy.wait()
 
     def group(i, _):
         results = []
         for u in range(SUB):
             e = i * SUB + u
-            slot = slot_ref[e]
-            rows = got_ref[pl.ds(slot, FIELDS, stride=CAP), :]
-            high, low = halves(rows)
-            both = lax.dot_general(
-                jnp.concatenate([high, low], axis=0),
-                w_ref[e],
-                (((1,), (1,)), ((), ())),
-                preferred_element_type=F32,
-            )
+            rows = parts[pl.ds(e, 2 * FIELDS, stride=entries), :]
+            both = dot32(rows.astype(BF16), w_ref[e])
             results.append((tile_ref[e], both[:FIELDS] + both[FIELDS:]))
         for tile, value in results:
             out_ref[tile] = out_ref[tile] + value
@@ -562,20 +586,21 @@
     lax.fori_loop(0, entries // SUB, group, 0, unroll=min(entries // SUB, 8))
 
 
-def regrid_back(got, weights, slots, tile_ids, tiles):
+def regrid_back(got, picks, turned, tile_ids, tiles):
+    entries = turned.shape[0]
     return pl.pallas_call(
         regrid_kernel,
         out_shape=jax.ShapeDtypeStruct((tiles, FIELDS, LANES), F32),
-        in_specs=[spec_vmem(), spec_vmem(), spec_any(), spec_any()],
+        in_specs=[spec_vmem(), spec_vmem(), spec_vmem(), spec_any()],
         out_specs=spec_vmem(),
         scratch_shapes=[
-            pltpu.SMEM(slots.shape, jnp.int32),
-            pltpu.SMEM(slots.shape, jnp.int32),
-            pltpu.SemaphoreType.DMA((2,)),
+            pltpu.VMEM((2 * FIELDS * entries, LANES), F32),
+            pltpu.SMEM(tile_ids.shape, jnp.int32),
+            pltpu.SemaphoreType.DMA,
         ],
         compiler_params=params(16),
         name="regrid_back",
-    )(got, weights, slots, tile_ids)
+    )(got, picks, turned, tile_ids)
 
 
 def exchange(x):
@@ -610,7 +635,8 @@
     )
 
     q = ocean_state.reshape(FIELDS * depth, rows, LANES)
-    outgoing, q = lax.optimization_barrier((outgoing, q))
+    outgoing, q, blocks_in = lax.optimization_barrier((outgoing, q, regrid_blocks))
+    turned = turn_blocks(blocks_in)
     chunk_rows = outgoing.shape[0] // devices
     incoming = exchange(outgoing.reshape(devices, chunk_rows // 2, 2, LANES))
     incoming = incoming.reshape(outgoing.shape)
@@ -622,7 +648,8 @@
         lax.ppermute(low_col, "tile", shift("tile", -1)),
         lax.ppermute(high_col, "tile", shift("tile", 1)),
     )
-    bulk, resp_rows, slots = ocean_bulk(q, flux_response, dest, devices)
+    bulk, resp_rows, picks = ocean_bulk(q, flux_response, dest, devices)
+    turned, edges = lax.optimization_barrier((turned, edges))
     surf = ocean_top(q, land_mask, edges)
     top, returning = ocean_combine(incoming, bulk, surf, land_mask, resp_rows, devices)
     arrived = exchange(returning)
@@ -631,9 +658,7 @@
         (q_next, a_tiles, d_tiles, s_rows)
     )
     atm_next = atm_solve(a_tiles, d_tiles, s_rows).transpose(0, 1, 3, 2, 4).reshape(FIELDS, levels, columns)
-    back = regrid_back(
-        arrived.reshape(devices * FIELDS * CAP, LANES), regrid_blocks, slots, entry_tile, tiles
-    )
+    back = regrid_back(arrived, picks, turned, entry_tile, tiles)
     surface_next = back.transpose(1, 0, 2).reshape(FIELDS, columns)
     return atm_next, q_next.reshape(ocean_state.shape), surface_next
 

time: 49.9 us -> 49.4 us (0.990)
  waiting for transfers between devices: 8.97 us -> 6.75 us
  Pallas kernels: 19.7 us -> 21.4 us
    pallas_call x0 -> x1, Pallas kernels: none -> 2.89 us  [turn_blocks(): pl.pallas_call(turn_kernel, grid=(entries // per,), out_shape=jax.ShapeDt...]
    all_to_all x2, waiting for transfers between devices: 8.96 us -> 6.74 us  [exchange(): return lax.all_to_all(x, BOTH, split_axis=0, concat_axis=0, tiled=True)]
    pallas_call x1, Pallas kernels: 1.79 us -> 1.14 us  [ocean_bulk(): pl.pallas_call(bulk_kernel, out_shape=(jax.ShapeDtypeStruct((FLUXES,) + q...]
    pallas_call x1, Pallas kernels: 2.44 us -> 1.89 us  [regrid_back(): pl.pallas_call(regrid_kernel, out_shape=jax.ShapeDtypeStruct((tiles, FIEL...]
  transfers between devices with their start and end apart: 6 -> 6, of which waited for: 2 -> 2; matrix products, arithmetic and copies ran while one was open for 0% -> 0% of each run, Pallas kernels for 22% -> 27%
where the time goes in v5:
time: 49.4 us; the launch traced here: 49 us
  Pallas kernels  21.4 us (43%)
  starting transfers between devices  20 us (40%)
  waiting for transfers between devices  6.75 us (14%)
  between operations  0.79 us (2%)
    all_to_all x2, starting transfers between devices, exchange(): return lax.all_to_all(x, BOTH, split_axis=0, concat_axis=0, tiled=True)  9.88 us
    all_to_all x2, waiting for transfers between devices, exchange(): return lax.all_to_all(x, BOTH, split_axis=0, concat_axis=0, tiled=True)  6.74 us
    pallas_call x1, Pallas kernels, atm_solve(): pl.pallas_call(solve_kernel, grid=(tiles // per,), out_shape=jax.ShapeDty...  6.22 us
    pallas_call x1, Pallas kernels, atm_forward(): pl.pallas_call(functools.partial(atm_kernel, chunks, chunk_rows), out_sha...  5.04 us
    ppermute x1, starting transfers between devices, per_device(): lax.ppermute(high_row, 'sec', shift('sec', 1))  4.55 us
    ppermute x1, starting transfers between devices, per_device(): lax.ppermute(high_col, 'tile', shift('tile', 1))  3.03 us
    pallas_call x1, Pallas kernels, turn_blocks(): pl.pallas_call(turn_kernel, grid=(entries // per,), out_shape=jax.ShapeDt...  2.89 us
    pallas_call x1, Pallas kernels, ocean_deep(): pl.pallas_call(deep_kernel, out_shape=jax.ShapeDtypeStruct(q.shape, F32),...  2.34 us
  transfers between devices with their start and end apart: 6, of which 2 were waited for; matrix products, arithmetic and copies ran while one was open for 0% of the time, Pallas kernels for 27%

profile of v5, /device:TPU:0, one launch (start us, length us, event | category | flops | bytes accessed | tf_op | source)
XLA Modules:
  0.0 49.0 jit_solution(1212534282459931549)
XLA Ops:
  0.6 0.0 copy-start
  0.6 0.0 copy-start.2
  0.7 0.0 copy-start.3
  0.7 5.0 %atm_forward.1 = f32[1344,128]{1,0:T(8,128)} custom-call(f32[4,4,64,8,128]{4,3,2,1,0:T(8,128)} %bitcast.29, f32[4,64,8,128]{3,2,1,0:T(8,128)} %bitcast.31, f32[256,128]{1,0:T(8,128)} %bitcast.36, f32[10,12]{1,0:T(8,128)} %mix_hbm.1, s32[64]{0:T(128)} %bitcast.27, s32[64]{0:T(128)} %tile_hbm.3, s32[64]{0:T(128)} %row_hbm.1, bf16[64,128,128]{2,1,0:T(8,128)(2,1)} %w_ref.2), custom_call_target="tpu_custom_call" | custom-call | tf_op jit(solution)/shard_map/atm_forward/pallas_call | solution.py:214
  5.7 7.3 %all-to-all-start = ((f32[32,21,2,128]{3,2,1,0:T(2,128)}), f32[32,21,2,128]{3,2,1,0:T(2,128)S(1)}, u32[]{:S(2)}, u32[]{:S(2)}) async-start(f32[32,21,2,128]{3,2,1,0:T(2,128)} %bitcast.34), calls=%async_computation | async-start | bytes 1376256 | tf_op jit(solution)/shard_map/all_to_all | solution.py:607
  13.1 0.4 ocean_edges.1
  13.4 1.3 %collective-permute-start.2 = (f32[64,128]{1,0:T(8,128)S(1)}, f32[64,128]{1,0:T(8,128)S(1)}, u32[]{:S(2)}, u32[]{:S(2)}) collective-permute-start(f32[64,128]{1,0:T(8,128)S(1)} %get-tuple-element.28), channel_id=1, source_target_pairs={{1,0},{2,1},{3,2},{4,3},{5,4},{6,5},{7,6},{9,8},{10,9},{11,10},{12... | collective-permute-start | bytes 98312 | tf_op jit(solution)/shard_map/ppermute | solution.py:648
  14.7 3.0 %collective-permute-start.3 = (f32[64,128]{1,0:T(8,128)S(1)}, f32[64,128]{1,0:T(8,128)S(1)}, u32[]{:S(2)}, u32[]{:S(2)}) collective-permute-start(f32[64,128]{1,0:T(8,128)S(1)} %get-tuple-element.29), channel_id=1, source_target_pairs={{0,1},{1,2},{2,3},{3,4},{4,5},{5,6},{6,7},{8,9},{9,10},{10,11},{11... | collective-permute-start | bytes 98312 | tf_op jit(solution)/shard_map/ppermute | solution.py:649
  17.8 1.3 %collective-permute-start = (f32[40,128]{1,0:T(8,128)S(1)}, f32[40,128]{1,0:T(8,128)S(1)}, u32[]{:S(2)}, u32[]{:S(2)}) collective-permute-start(f32[40,128]{1,0:T(8,128)S(1)} %get-tuple-element.26), channel_id=1, source_target_pairs={{8,0},{16,8},{24,16},{9,1},{17,9},{25,17},{10,2},{18,10},{26,18},{... | collective-permute-start | bytes 61448 | tf_op jit(solution)/shard_map/ppermute | solution.py:646
  19.1 4.5 %collective-permute-start.1 = (f32[40,128]{1,0:T(8,128)S(1)}, f32[40,128]{1,0:T(8,128)S(1)}, u32[]{:S(2)}, u32[]{:S(2)}) collective-permute-start(f32[40,128]{1,0:T(8,128)S(1)} %get-tuple-element.27), channel_id=1, source_target_pairs={{0,8},{8,16},{16,24},{1,9},{9,17},{17,25},{2,10},{10,18},{18,26},{... | collective-permute-start | bytes 61448 | tf_op jit(solution)/shard_map/ppermute | solution.py:647
  23.6 1.1 %ocean_bulk.1 = (f32[10,64,128]{2,1,0:T(8,128)S(1)}, f32[40,128]{1,0:T(8,128)S(1)}, bf16[128,256]{1,0:T(8,128)(2,1)S(1)}) custom-call(f32[32,64,128]{2,1,0:T(8,128)S(1)} %bitcast.23, f32[4,10]{1,0:T(4,128)S(1)} %copy-done.3, s32[64]{0:T(128)S(1)} %bitcast.28), custom_call_target="tpu_custom_call" | custom-call | flops 786432 | bytes 524288 | tf_op jit(solution)/shard_map/ocean_bulk/pallas_call | solution.py:380
  24.8 2.9 %turn_blocks.1.w_ref = bf16[64,128,128]{2,1,0:T(8,128)(2,1)} custom-call(bf16[64,128,128]{2,1,0:T(8,128)(2,1)} %w_ref.2), custom_call_target="tpu_custom_call" | custom-call | flops 1048576 | bytes 4194304 | tf_op jit(solution)/shard_map/turn_blocks/pallas_call | solution.py:547
  27.7 0.0 collective-permute-done.east_ref
  27.7 0.0 collective-permute-done.1.west_ref
  27.7 0.0 collective-permute-done.2.north_ref
  27.7 0.0 collective-permute-done.3.south_ref
  27.7 0.3 ocean_top.1.surf_ref
  28.0 4.9 %all-to-all-done = f32[32,21,2,128]{3,2,1,0:T(2,128)S(1)} async-done(((f32[32,21,2,128]{3,2,1,0:T(2,128)}), f32[32,21,2,128]{3,2,1,0:T(2,128)S(1)}, u32[]{:S(2)}, u32[]{:S(2)}) %all-to-all-start) | async-done | bytes 688160 | tf_op jit(solution)/shard_map/all_to_all | solution.py:607
  32.9 1.3 %ocean_combine.1 = (f32[4,64,128]{2,1,0:T(8,128)S(1)}, f32[32,16,128]{2,1,0:T(8,128)}) custom-call(f32[1344,128]{1,0:T(8,128)S(1)} %bitcast.26, f32[10,64,128]{2,1,0:T(8,128)S(1)} %get-tuple-element.35.bulk_ref, f32[4,64,128]{2,1,0:T(8,128)S(1)} %ocean_top.1.surf_ref, s32[64,128]{1,0:T(8,128)S(1)} %copy-done.2, f32[40,128]{1,0:T(8,128)S(1)} %get-tuple-element.36.resp_ref), custom_call_target="tpu_custom_call" | custom-call | flops 688128 | bytes 688128 | tf_op jit(solution)/shard_map/ocean_combine/pallas_call | solution.py:522
  34.2 2.6 %all-to-all-start.1 = ((f32[32,16,128]{2,1,0:T(8,128)}), f32[32,16,128]{2,1,0:T(8,128)S(1)}, u32[]{:S(2)}, u32[]{:S(2)}) async-start(f32[32,16,128]{2,1,0:T(8,128)} %get-tuple-element.42), calls=%async_computation.1 | async-start | bytes 524288 | tf_op jit(solution)/shard_map/all_to_all | solution.py:607
  36.8 2.3 %ocean_deep.1 = f32[32,64,128]{2,1,0:T(8,128)} custom-call(f32[32,64,128]{2,1,0:T(8,128)S(1)} %bitcast.25, s32[64,128]{1,0:T(8,128)S(1)} %copy-done.2, f32[40,128]{1,0:T(8,128)S(1)} %collective-permute-done.east_ref, f32[40,128]{1,0:T(8,128)S(1)} %collective-permute-done.1.west_ref, f32[64,128]{1,0:T(8,128)S(1)} %collective-permute-done.2.north_ref, ...), custom_call_target="tpu_custom_call" | custom-call | flops 7864320 | bytes 2097152 | tf_op jit(solution)/shard_map/ocean_deep/pallas_call | solution.py:465
  39.1 6.2 %atm_solve.1 = f32[4,4,64,8,128]{4,3,2,1,0:T(8,128)} custom-call(f32[4,4,64,8,128]{4,3,2,1,0:T(8,128)} %bitcast.30, f32[4,64,8,128]{3,2,1,0:T(8,128)} %bitcast.32, f32[256,128]{1,0:T(8,128)} %bitcast.37), custom_call_target="tpu_custom_call" | custom-call | flops 8388608 | bytes 9437184 | tf_op jit(solution)/shard_map/atm_solve/pallas_call | solution.py:282
  45.3 1.8 %all-to-all-done.1.got_ref = f32[32,16,128]{2,1,0:T(8,128)S(1)} async-done(((f32[32,16,128]{2,1,0:T(8,128)}), f32[32,16,128]{2,1,0:T(8,128)S(1)}, u32[]{:S(2)}, u32[]{:S(2)}) %all-to-all-start.1) | async-done | bytes 262176 | tf_op jit(solution)/shard_map/all_to_all | solution.py:607
  47.1 1.9 %regrid_back.1 = f32[64,4,128]{2,1,0:T(4,128)} custom-call(f32[32,16,128]{2,1,0:T(8,128)S(1)} %all-to-all-done.1.got_ref, bf16[128,256]{1,0:T(8,128)(2,1)S(1)} %get-tuple-element.43.pick_ref, bf16[64,128,128]{2,1,0:T(8,128)(2,1)S(1)} %copy-done.1, s32[64]{0:T(128)S(1)} %copy-done.5), custom_call_target="tpu_custom_call" | custom-call | tf_op jit(solution)/shard_map/regrid_back/pallas_call | solution.py:591
  (9 shorter events, 0.0 us)
Async XLA Ops:
  0.6 12.4 %copy-start = (f32[4,8,64,128]{3,2,1,0:T(8,128)S(1)}, f32[4,8,64,128]{3,2,1,0:T(8,128)}, u32[]{:S(2)}) copy-start(f32[4,8,64,128]{3,2,1,0:T(8,128)} %param.19) | copy-start | bytes 3145732
  0.6 12.4 %copy-start.2 = (s32[64,128]{1,0:T(8,128)S(1)}, s32[64,128]{1,0:T(8,128)}, u32[]{:S(2)}) copy-start(s32[64,128]{1,0:T(8,128)} %m_ref.7) | copy-start | bytes 98308
  0.7 23.0 %copy-start.3 = (f32[4,10]{1,0:T(4,128)S(1)}, f32[4,10]{1,0:T(4,128)}, u32[]{:S(2)}) copy-start(f32[4,10]{1,0:T(4,128)} %resp_ref.1) | copy-start | bytes 484
  0.7 23.0 %copy-start.4 = (s32[64,1]{0,1:T(1,128)S(1)}, s32[64,1]{0,1:T(1,128)}, u32[]{:S(2)}) copy-start(s32[64,1]{0,1:T(1,128)} %param.15) | copy-start | bytes 772
  5.7 27.2 %all-to-all-start = ((f32[32,21,2,128]{3,2,1,0:T(2,128)}), f32[32,21,2,128]{3,2,1,0:T(2,128)S(1)}, u32[]{:S(2)}, u32[]{:S(2)}) async-start(f32[32,21,2,128]{3,2,1,0:T(2,128)} %bitcast.34), calls=%async_computation | async-start | bytes 1376256 | tf_op jit(solution)/shard_map/all_to_all | solution.py:607
  13.4 14.3 %collective-permute-start.2 = (f32[64,128]{1,0:T(8,128)S(1)}, f32[64,128]{1,0:T(8,128)S(1)}, u32[]{:S(2)}, u32[]{:S(2)}) collective-permute-start(f32[64,128]{1,0:T(8,128)S(1)} %get-tuple-element.28), channel_id=1, source_target_pairs={{1,0},{2,1},{3,2},{4,3},{5,4},{6,5},{7,6},{9,8},{10,9},{11,10},{12... | collective-permute-start | bytes 98312 | tf_op jit(solution)/shard_map/ppermute | solution.py:648
  14.7 13.0 %collective-permute-start.3 = (f32[64,128]{1,0:T(8,128)S(1)}, f32[64,128]{1,0:T(8,128)S(1)}, u32[]{:S(2)}, u32[]{:S(2)}) collective-permute-start(f32[64,128]{1,0:T(8,128)S(1)} %get-tuple-element.29), channel_id=1, source_target_pairs={{0,1},{1,2},{2,3},{3,4},{4,5},{5,6},{6,7},{8,9},{9,10},{10,11},{11... | collective-permute-start | bytes 98312 | tf_op jit(solution)/shard_map/ppermute | solution.py:649
  17.8 9.9 %collective-permute-start = (f32[40,128]{1,0:T(8,128)S(1)}, f32[40,128]{1,0:T(8,128)S(1)}, u32[]{:S(2)}, u32[]{:S(2)}) collective-permute-start(f32[40,128]{1,0:T(8,128)S(1)} %get-tuple-element.26), channel_id=1, source_target_pairs={{8,0},{16,8},{24,16},{9,1},{17,9},{25,17},{10,2},{18,10},{26,18},{... | collective-permute-start | bytes 61448 | tf_op jit(solution)/shard_map/ppermute | solution.py:646
  19.1 8.6 %collective-permute-start.1 = (f32[40,128]{1,0:T(8,128)S(1)}, f32[40,128]{1,0:T(8,128)S(1)}, u32[]{:S(2)}, u32[]{:S(2)}) collective-permute-start(f32[40,128]{1,0:T(8,128)S(1)} %get-tuple-element.27), channel_id=1, source_target_pairs={{0,8},{8,16},{16,24},{1,9},{9,17},{17,25},{2,10},{10,18},{18,26},{... | collective-permute-start | bytes 61448 | tf_op jit(solution)/shard_map/ppermute | solution.py:647
  34.2 13.0 %all-to-all-start.1 = ((f32[32,16,128]{2,1,0:T(8,128)}), f32[32,16,128]{2,1,0:T(8,128)S(1)}, u32[]{:S(2)}, u32[]{:S(2)}) async-start(f32[32,16,128]{2,1,0:T(8,128)} %get-tuple-element.42), calls=%async_computation.1 | async-start | bytes 524288 | tf_op jit(solution)/shard_map/all_to_all | solution.py:607
  39.1 8.0 %copy-start.1 = (bf16[64,128,128]{2,1,0:T(8,128)(2,1)S(1)}, bf16[64,128,128]{2,1,0:T(8,128)(2,1)}, u32[]{:S(2)}) copy-start(bf16[64,128,128]{2,1,0:T(8,128)(2,1)} %turn_blocks.1.w_ref) | copy-start | bytes 6291460
  39.1 8.0 %copy-start.5 = (s32[64]{0:T(128)S(1)}, s32[64]{0:T(128)}, u32[]{:S(2)}) copy-start(s32[64]{0:T(128)} %tile_hbm.3) | copy-start | bytes 772

commit v6 on v5

--- a/solution.py
+++ b/solution.py
@@ -186,8 +186,7 @@
         d = dest_ref[e]
         k = count[d]
         count[d] = k + 1
-        here = me * (2 * CAP) + k
-        hit = (spot == here) | (spot == here + CAP)
+        hit = spot == me * CAP + k
         table = pl.ds(d * chunk_rows + FLUXES * CAP, table_rows)
         out_ref[table, :] += jnp.where(hit, row_ref[e] + 1, 0).astype(F32)
         picked = flux[pl.ds(pl.multiple_of(tile_ref[e] * 16, 16), 16), :]
@@ -209,7 +208,7 @@
     _, _, tiles, _, _ = a_tiles.shape
     entries = weights.shape[0]
     chunks = 4
-    chunk_rows = FLUXES * CAP + devices * 2 * CAP // LANES
+    chunk_rows = FLUXES * CAP + devices * CAP // LANES
     out_shape = (devices * chunk_rows, LANES)
     return pl.pallas_call(
         functools.partial(atm_kernel, chunks, chunk_rows),
@@ -487,11 +486,17 @@
     spot = lax.broadcasted_iota(jnp.int32, (2 * rows, LANES), 1)
     pair = (spot // CAP) % 2 == x // rows
     wanted = jnp.where(pair, (x % rows + 1).astype(F32), -1.0)
+    lane_in = lax.broadcasted_iota(jnp.int32, (LANES, LANES), 0)
+    lane_out = lax.broadcasted_iota(jnp.int32, (LANES, LANES), 1)
+    twice = lane_out // (2 * CAP) * CAP + lane_out % CAP
     hots = []
     for j in range(table_rows):
         seen = got_ref[pl.ds(FLUXES * CAP + j, sources, stride=chunk_rows), :]
         seen = jnp.sum(seen, axis=0, keepdims=True)
-        hots.append((seen == wanted).astype(F32))
+        seen = jnp.broadcast_to(seen, (SUB, LANES)).astype(BF16)
+        for p in range(2):
+            spread = (lane_in == twice + p * (LANES // 2)).astype(F32).astype(BF16)
+            hots.append((dot32(seen, spread)[0:1] == wanted).astype(F32))
     hot = jnp.concatenate([h.astype(BF16) for h in hots], axis=1)
 
     force = [None] * FIELDS
@@ -638,7 +643,7 @@
     outgoing, q, blocks_in = lax.optimization_barrier((outgoing, q, regrid_blocks))
     turned = turn_blocks(blocks_in)
     chunk_rows = outgoing.shape[0] // devices
-    incoming = exchange(outgoing.reshape(devices, chunk_rows // 2, 2, LANES))
+    incoming = exchange(outgoing.reshape(devices, chunk_rows, 1, LANES))
     incoming = incoming.reshape(outgoing.shape)
 
     low_row, high_row, low_col, high_col = ocean_edges(q, land_mask)

time: 49.4 us -> 49.2 us (level)
  no operation moved by 1% of the time
where the time goes in v6:
time: 49.2 us; the launch traced here: 48.8 us
  Pallas kernels  21.5 us (44%)
  starting transfers between devices  20.1 us (41%)
  waiting for transfers between devices  6.4 us (13%)
  between operations  0.79 us (2%)
    all_to_all x2, starting transfers between devices, exchange(): return lax.all_to_all(x, BOTH, split_axis=0, concat_axis=0, tiled=True)  9.89 us
    all_to_all x2, waiting for transfers between devices, exchange(): return lax.all_to_all(x, BOTH, split_axis=0, concat_axis=0, tiled=True)  6.39 us
    pallas_call x1, Pallas kernels, atm_solve(): pl.pallas_call(solve_kernel, grid=(tiles // per,), out_shape=jax.ShapeDty...  6.22 us
    pallas_call x1, Pallas kernels, atm_forward(): pl.pallas_call(functools.partial(atm_kernel, chunks, chunk_rows), out_sha...  5.03 us
    ppermute x1, starting transfers between devices, per_device(): lax.ppermute(high_row, 'sec', shift('sec', 1))  4.55 us
    ppermute x1, starting transfers between devices, per_device(): lax.ppermute(high_col, 'tile', shift('tile', 1))  3.03 us
    pallas_call x1, Pallas kernels, turn_blocks(): pl.pallas_call(turn_kernel, grid=(entries // per,), out_shape=jax.ShapeDt...  2.89 us
    pallas_call x1, Pallas kernels, ocean_deep(): pl.pallas_call(deep_kernel, out_shape=jax.ShapeDtypeStruct(q.shape, F32),...  2.34 us
  transfers between devices with their start and end apart: 6, of which 2 were waited for; matrix products, arithmetic and copies ran while one was open for 0% of the time, Pallas kernels for 27%

profile of v6, /device:TPU:0, one launch (start us, length us, event | category | flops | bytes accessed | tf_op | source)
XLA Modules:
  0.0 48.8 jit_solution(9692289344276982216)
XLA Ops:
  0.7 5.0 %atm_forward.1 = f32[1312,128]{1,0:T(8,128)} custom-call(f32[4,4,64,8,128]{4,3,2,1,0:T(8,128)} %bitcast.29, f32[4,64,8,128]{3,2,1,0:T(8,128)} %bitcast.31, f32[256,128]{1,0:T(8,128)} %bitcast.36, f32[10,12]{1,0:T(8,128)} %mix_hbm.1, s32[64]{0:T(128)} %bitcast.27, s32[64]{0:T(128)} %tile_hbm.3, s32[64]{0:T(128)} %row_hbm.1, bf16[64,128,128]{2,1,0:T(8,128)(2,1)} %w_ref.2), custom_call_target="tpu_custom_call" | custom-call | tf_op jit(solution)/shard_map/atm_forward/pallas_call | solution.py:213
  5.7 7.3 %all-to-all-start = ((f32[32,41,1,128]{3,2,1,0:T(1,128)}), f32[32,41,1,128]{3,2,1,0:T(1,128)S(1)}, u32[]{:S(2)}, u32[]{:S(2)}) async-start(f32[32,41,1,128]{3,2,1,0:T(1,128)} %bitcast.34), calls=%async_computation | async-start | bytes 1343488 | tf_op jit(solution)/shard_map/all_to_all | solution.py:612
  13.0 0.4 ocean_edges.1
  13.4 1.3 %collective-permute-start.2 = (f32[64,128]{1,0:T(8,128)S(1)}, f32[64,128]{1,0:T(8,128)S(1)}, u32[]{:S(2)}, u32[]{:S(2)}) collective-permute-start(f32[64,128]{1,0:T(8,128)S(1)} %get-tuple-element.28), channel_id=1, source_target_pairs={{1,0},{2,1},{3,2},{4,3},{5,4},{6,5},{7,6},{9,8},{10,9},{11,10},{12... | collective-permute-start | bytes 98312 | tf_op jit(solution)/shard_map/ppermute | solution.py:653
  14.7 3.0 %collective-permute-start.3 = (f32[64,128]{1,0:T(8,128)S(1)}, f32[64,128]{1,0:T(8,128)S(1)}, u32[]{:S(2)}, u32[]{:S(2)}) collective-permute-start(f32[64,128]{1,0:T(8,128)S(1)} %get-tuple-element.29), channel_id=1, source_target_pairs={{0,1},{1,2},{2,3},{3,4},{4,5},{5,6},{6,7},{8,9},{9,10},{10,11},{11... | collective-permute-start | bytes 98312 | tf_op jit(solution)/shard_map/ppermute | solution.py:654
  17.7 1.3 %collective-permute-start = (f32[40,128]{1,0:T(8,128)S(1)}, f32[40,128]{1,0:T(8,128)S(1)}, u32[]{:S(2)}, u32[]{:S(2)}) collective-permute-start(f32[40,128]{1,0:T(8,128)S(1)} %get-tuple-element.26), channel_id=1, source_target_pairs={{8,0},{16,8},{24,16},{9,1},{17,9},{25,17},{10,2},{18,10},{26,18},{... | collective-permute-start | bytes 61448 | tf_op jit(solution)/shard_map/ppermute | solution.py:651
  19.0 4.5 %collective-permute-start.1 = (f32[40,128]{1,0:T(8,128)S(1)}, f32[40,128]{1,0:T(8,128)S(1)}, u32[]{:S(2)}, u32[]{:S(2)}) collective-permute-start(f32[40,128]{1,0:T(8,128)S(1)} %get-tuple-element.27), channel_id=1, source_target_pairs={{0,8},{8,16},{16,24},{1,9},{9,17},{17,25},{2,10},{10,18},{18,26},{... | collective-permute-start | bytes 61448 | tf_op jit(solution)/shard_map/ppermute | solution.py:652
  23.6 0.0 copy-done.3
  23.6 0.0 copy-done.4
  23.6 1.1 %ocean_bulk.1 = (f32[10,64,128]{2,1,0:T(8,128)S(1)}, f32[40,128]{1,0:T(8,128)S(1)}, bf16[128,256]{1,0:T(8,128)(2,1)S(1)}) custom-call(f32[32,64,128]{2,1,0:T(8,128)S(1)} %bitcast.23, f32[4,10]{1,0:T(4,128)S(1)} %copy-done.3, s32[64]{0:T(128)S(1)} %bitcast.28), custom_call_target="tpu_custom_call" | custom-call | flops 786432 | bytes 524288 | tf_op jit(solution)/shard_map/ocean_bulk/pallas_call | solution.py:379
  24.8 2.9 %turn_blocks.1.w_ref = bf16[64,128,128]{2,1,0:T(8,128)(2,1)} custom-call(bf16[64,128,128]{2,1,0:T(8,128)(2,1)} %w_ref.2), custom_call_target="tpu_custom_call" | custom-call | flops 1048576 | bytes 4194304 | tf_op jit(solution)/shard_map/turn_blocks/pallas_call | solution.py:552
  27.7 0.0 collective-permute-done.east_ref
  27.7 0.0 collective-permute-done.1.west_ref
  27.7 0.0 collective-permute-done.2.north_ref
  27.7 0.0 collective-permute-done.3.south_ref
  27.7 0.3 ocean_top.1.surf_ref
  28.0 4.6 %all-to-all-done = f32[32,41,1,128]{3,2,1,0:T(1,128)S(1)} async-done(((f32[32,41,1,128]{3,2,1,0:T(1,128)}), f32[32,41,1,128]{3,2,1,0:T(1,128)S(1)}, u32[]{:S(2)}, u32[]{:S(2)}) %all-to-all-start) | async-done | bytes 671776 | tf_op jit(solution)/shard_map/all_to_all | solution.py:612
  32.5 1.4 %ocean_combine.1 = (f32[4,64,128]{2,1,0:T(8,128)S(1)}, f32[32,16,128]{2,1,0:T(8,128)}) custom-call(f32[1312,128]{1,0:T(8,128)S(1)} %bitcast.26, f32[10,64,128]{2,1,0:T(8,128)S(1)} %get-tuple-element.35.bulk_ref, f32[4,64,128]{2,1,0:T(8,128)S(1)} %ocean_top.1.surf_ref, s32[64,128]{1,0:T(8,128)S(1)} %copy-done.2, f32[40,128]{1,0:T(8,128)S(1)} %get-tuple-element.36.resp_ref), custom_call_target="tpu_custom_call" | custom-call | flops 671744 | bytes 671744 | tf_op jit(solution)/shard_map/ocean_combine/pallas_call | solution.py:527
  33.9 2.6 %all-to-all-start.1 = ((f32[32,16,128]{2,1,0:T(8,128)}), f32[32,16,128]{2,1,0:T(8,128)S(1)}, u32[]{:S(2)}, u32[]{:S(2)}) async-start(f32[32,16,128]{2,1,0:T(8,128)} %get-tuple-element.42), calls=%async_computation.1 | async-start | bytes 524288 | tf_op jit(solution)/shard_map/all_to_all | solution.py:612
  36.5 2.3 %ocean_deep.1 = f32[32,64,128]{2,1,0:T(8,128)} custom-call(f32[32,64,128]{2,1,0:T(8,128)S(1)} %bitcast.25, s32[64,128]{1,0:T(8,128)S(1)} %copy-done.2, f32[40,128]{1,0:T(8,128)S(1)} %collective-permute-done.east_ref, f32[40,128]{1,0:T(8,128)S(1)} %collective-permute-done.1.west_ref, f32[64,128]{1,0:T(8,128)S(1)} %collective-permute-done.2.north_ref, ...), custom_call_target="tpu_custom_call" | custom-call | flops 7864320 | bytes 2097152 | tf_op jit(solution)/shard_map/ocean_deep/pallas_call | solution.py:464
  38.9 6.2 %atm_solve.1 = f32[4,4,64,8,128]{4,3,2,1,0:T(8,128)} custom-call(f32[4,4,64,8,128]{4,3,2,1,0:T(8,128)} %bitcast.30, f32[4,64,8,128]{3,2,1,0:T(8,128)} %bitcast.32, f32[256,128]{1,0:T(8,128)} %bitcast.37), custom_call_target="tpu_custom_call" | custom-call | flops 8388608 | bytes 9437184 | tf_op jit(solution)/shard_map/atm_solve/pallas_call | solution.py:281
  45.1 1.8 %all-to-all-done.1.got_ref = f32[32,16,128]{2,1,0:T(8,128)S(1)} async-done(((f32[32,16,128]{2,1,0:T(8,128)}), f32[32,16,128]{2,1,0:T(8,128)S(1)}, u32[]{:S(2)}, u32[]{:S(2)}) %all-to-all-start.1) | async-done | bytes 262176 | tf_op jit(solution)/shard_map/all_to_all | solution.py:612
  46.9 0.0 copy-done.1
  46.9 1.9 %regrid_back.1 = f32[64,4,128]{2,1,0:T(4,128)} custom-call(f32[32,16,128]{2,1,0:T(8,128)S(1)} %all-to-all-done.1.got_ref, bf16[128,256]{1,0:T(8,128)(2,1)S(1)} %get-tuple-element.43.pick_ref, bf16[64,128,128]{2,1,0:T(8,128)(2,1)S(1)} %copy-done.1, s32[64]{0:T(128)S(1)} %copy-done.5), custom_call_target="tpu_custom_call" | custom-call | tf_op jit(solution)/shard_map/regrid_back/pallas_call | solution.py:596
  (9 shorter events, 0.0 us)
Async XLA Ops:
  0.6 12.4 %copy-start = (f32[4,8,64,128]{3,2,1,0:T(8,128)S(1)}, f32[4,8,64,128]{3,2,1,0:T(8,128)}, u32[]{:S(2)}) copy-start(f32[4,8,64,128]{3,2,1,0:T(8,128)} %param.19) | copy-start | bytes 3145732
  0.6 12.4 %copy-start.2 = (s32[64,128]{1,0:T(8,128)S(1)}, s32[64,128]{1,0:T(8,128)}, u32[]{:S(2)}) copy-start(s32[64,128]{1,0:T(8,128)} %m_ref.7) | copy-start | bytes 98308
  0.7 22.9 %copy-start.3 = (f32[4,10]{1,0:T(4,128)S(1)}, f32[4,10]{1,0:T(4,128)}, u32[]{:S(2)}) copy-start(f32[4,10]{1,0:T(4,128)} %resp_ref.1) | copy-start | bytes 484
  0.7 22.9 %copy-start.4 = (s32[64,1]{0,1:T(1,128)S(1)}, s32[64,1]{0,1:T(1,128)}, u32[]{:S(2)}) copy-start(s32[64,1]{0,1:T(1,128)} %param.15) | copy-start | bytes 772
  5.7 26.8 %all-to-all-start = ((f32[32,41,1,128]{3,2,1,0:T(1,128)}), f32[32,41,1,128]{3,2,1,0:T(1,128)S(1)}, u32[]{:S(2)}, u32[]{:S(2)}) async-start(f32[32,41,1,128]{3,2,1,0:T(1,128)} %bitcast.34), calls=%async_computation | async-start | bytes 1343488 | tf_op jit(solution)/shard_map/all_to_all | solution.py:612
  13.4 14.3 %collective-permute-start.2 = (f32[64,128]{1,0:T(8,128)S(1)}, f32[64,128]{1,0:T(8,128)S(1)}, u32[]{:S(2)}, u32[]{:S(2)}) collective-permute-start(f32[64,128]{1,0:T(8,128)S(1)} %get-tuple-element.28), channel_id=1, source_target_pairs={{1,0},{2,1},{3,2},{4,3},{5,4},{6,5},{7,6},{9,8},{10,9},{11,10},{12... | collective-permute-start | bytes 98312 | tf_op jit(solution)/shard_map/ppermute | solution.py:653
  14.7 13.0 %collective-permute-start.3 = (f32[64,128]{1,0:T(8,128)S(1)}, f32[64,128]{1,0:T(8,128)S(1)}, u32[]{:S(2)}, u32[]{:S(2)}) collective-permute-start(f32[64,128]{1,0:T(8,128)S(1)} %get-tuple-element.29), channel_id=1, source_target_pairs={{0,1},{1,2},{2,3},{3,4},{4,5},{5,6},{6,7},{8,9},{9,10},{10,11},{11... | collective-permute-start | bytes 98312 | tf_op jit(solution)/shard_map/ppermute | solution.py:654
  17.7 9.9 %collective-permute-start = (f32[40,128]{1,0:T(8,128)S(1)}, f32[40,128]{1,0:T(8,128)S(1)}, u32[]{:S(2)}, u32[]{:S(2)}) collective-permute-start(f32[40,128]{1,0:T(8,128)S(1)} %get-tuple-element.26), channel_id=1, source_target_pairs={{8,0},{16,8},{24,16},{9,1},{17,9},{25,17},{10,2},{18,10},{26,18},{... | collective-permute-start | bytes 61448 | tf_op jit(solution)/shard_map/ppermute | solution.py:651
  19.0 8.6 %collective-permute-start.1 = (f32[40,128]{1,0:T(8,128)S(1)}, f32[40,128]{1,0:T(8,128)S(1)}, u32[]{:S(2)}, u32[]{:S(2)}) collective-permute-start(f32[40,128]{1,0:T(8,128)S(1)} %get-tuple-element.27), channel_id=1, source_target_pairs={{0,8},{8,16},{16,24},{1,9},{9,17},{17,25},{2,10},{10,18},{18,26},{... | collective-permute-start | bytes 61448 | tf_op jit(solution)/shard_map/ppermute | solution.py:652
  33.9 13.0 %all-to-all-start.1 = ((f32[32,16,128]{2,1,0:T(8,128)}), f32[32,16,128]{2,1,0:T(8,128)S(1)}, u32[]{:S(2)}, u32[]{:S(2)}) async-start(f32[32,16,128]{2,1,0:T(8,128)} %get-tuple-element.42), calls=%async_computation.1 | async-start | bytes 524288 | tf_op jit(solution)/shard_map/all_to_all | solution.py:612
  38.9 8.0 %copy-start.1 = (bf16[64,128,128]{2,1,0:T(8,128)(2,1)S(1)}, bf16[64,128,128]{2,1,0:T(8,128)(2,1)}, u32[]{:S(2)}) copy-start(bf16[64,128,128]{2,1,0:T(8,128)(2,1)} %turn_blocks.1.w_ref) | copy-start | bytes 6291460
  38.9 8.0 %copy-start.5 = (s32[64]{0:T(128)S(1)}, s32[64]{0:T(128)}, u32[]{:S(2)}) copy-start(s32[64]{0:T(128)} %tile_hbm.3) | copy-start | bytes 772
